TPU v7x, 32 devices: a whole 2x2x4 slice. The times are simulated.
32 devices in a mesh: ctx: 4 (over z), dom: 2 (over y), rep: 4 (over x, core).
Axes of the slice: x: 2, y: 2, z: 4, core: 2. Of those that a mesh axis runs over, the one named last changes fastest.
Arguments:
- hidden: bfloat16 [4, 2, 512, 2048], P('rep', 'dom', 'ctx'), may hold values from -6 to 6
- bmat: bfloat16 [4, 2, 512, 128], P('rep', 'dom', 'ctx'), may hold values from -0.5 to 0.5
- cmat: bfloat16 [4, 2, 512, 128], P('rep', 'dom', 'ctx'), may hold values from -6 to 6
- tokens: int32 [4, 2, 512], P('rep', 'dom', 'ctx'), may hold values from 0 to 3
- table: float32 [4, 128], replicated, may hold values from -0.5 to 0.5
- step_size: float32 [4, 2, 512, 16], P('rep', 'dom', 'ctx'), may hold values from 0.005 to 0.05
- log_decay: float32 [4, 2, 512, 16], P('rep', 'dom', 'ctx'), may hold values from 0 to 1.5
- skip_gain: float32 [16], replicated, may hold values from 0.5 to 1.5
- prev_state: float32 [4, 2, 16, 128, 128], P('rep', 'dom', 'ctx'), may hold values from -0.5 to 0.5
- ancestors: int32 [4, 2], P('rep', 'dom'), may hold values from 0 to 1
- suffix_start: int32 [4], P('rep'), may hold values from 128 to 511
- cotangent: bfloat16 [4, 2, 512, 2048], P('rep', 'dom', 'ctx'), may hold values from -6 to 6
Outputs:
- mixed: bfloat16 [4, 2, 512, 2048], P('rep', 'dom', 'ctx')
- grad_hidden: bfloat16 [4, 2, 512, 2048], P('rep', 'dom', 'ctx')
- grad_bmat: bfloat16 [4, 2, 512, 128], P('rep', 'dom', 'ctx')
- grad_cmat: bfloat16 [4, 2, 512, 128], P('rep', 'dom', 'ctx')
- grad_table: float32 [4, 128], replicated
- grad_skip: float32 [16], replicated
All inputs are finite; a program needn't handle non-finite values.
Results may differ from a plain program's by a relative error of at most 0.008.
Values sent between devices are 32-bit elements; how exact they have to be, the bound alone decides.
No kernel may reach another device: no remote copies, remote signals or barrier semaphores. Data moves between devices by JAX's collectives and lax.ppermute only.
A program may use at most 192 MiB of HBM per device.

v0:
```python
import math

import jax
import jax.numpy as jnp
from jax import lax
from jax.sharding import PartitionSpec as P


def carried_in(value, axis, join, neutral, backward):
    count, mine = (lax.axis_size(axis), lax.axis_index(axis))
    pieces = jax.tree.map(lambda part: lax.all_gather(part, axis), value)
    if backward:
        pieces = jax.tree.map(lambda part: part[::-1], pieces)
        mine = count - 1 - mine
    running = jax.tree.map(
        lambda part, zero: jnp.full_like(part, 0) + jnp.asarray(zero, part.dtype), value, neutral
    )

    def turn(position, running):
        longer = join(running, jax.tree.map(lambda part: part[position], pieces))
        return jax.tree.map(lambda new, old: jnp.where(position < mine, new, old), longer, running)

    return lax.fori_loop(0, count - 1, turn, running)


def weigh(factor, values):
    return (factor[:, :, None] * values.astype(jnp.float32)).astype(jnp.bfloat16)


def block_terms(hidden_rows, writer, reader, step_rows, rate_rows, grad_rows):
    cumulative = jnp.cumsum(rate_rows, axis=0)
    totals = cumulative[-1]
    scaled = (step_rows[:, :, None] * hidden_rows.astype(jnp.float32)).astype(jnp.bfloat16)
    inner_dot = jnp.einsum("tn,sn->ts", reader, writer, preferred_element_type=jnp.float32)
    across = cumulative.T
    kernel = jnp.exp(-jnp.abs(across[:, :, None] - across[:, None, :]))
    weights = (kernel * inner_dot[None]).astype(jnp.bfloat16)
    mixed_in = jnp.einsum("hts,shp->thp", weights, scaled, preferred_element_type=jnp.float32)
    back_in = jnp.einsum("hts,thp->shp", weights, grad_rows, preferred_element_type=jnp.float32)
    paired = jnp.einsum("thp,shp->hts", grad_rows, scaled, preferred_element_type=jnp.float32)
    crossed = jnp.sum(kernel * paired, axis=0).astype(jnp.bfloat16)
    reader_in = jnp.einsum("ts,sn->tn", crossed, writer, preferred_element_type=jnp.float32)
    writer_in = jnp.einsum("ts,tn->sn", crossed, reader, preferred_element_type=jnp.float32)
    rising = jnp.exp(-cumulative)
    falling = jnp.exp(-(totals[None] - cumulative))
    state_end = jnp.einsum(
        "shp,sn->hpn", weigh(falling, scaled), writer, preferred_element_type=jnp.float32
    )
    state_begin = jnp.einsum(
        "shp,sn->hpn", weigh(rising, scaled), writer, preferred_element_type=jnp.float32
    )
    grad_end = jnp.einsum(
        "thp,tn->hpn", weigh(falling, grad_rows), reader, preferred_element_type=jnp.float32
    )
    grad_begin = jnp.einsum(
        "thp,tn->hpn", weigh(rising, grad_rows), reader, preferred_element_type=jnp.float32
    )
    decays = jnp.exp(-totals)
    return (
        mixed_in,
        back_in,
        reader_in,
        writer_in,
        rising,
        falling,
        scaled,
        decays,
        state_end,
        state_begin,
        grad_end,
        grad_begin,
    )


def finish(
    hidden_rows,
    writer,
    reader,
    step_rows,
    grad_rows,
    skip_gain,
    block_out,
    state_in,
    state_back,
    grad_in,
    grad_back,
):
    mixed_in, back_in, reader_in, writer_in, rising, falling, scaled = block_out
    state_in = state_in.astype(jnp.bfloat16)
    state_back = state_back.astype(jnp.bfloat16)
    grad_in = grad_in.astype(jnp.bfloat16)
    grad_back = grad_back.astype(jnp.bfloat16)
    rise = rising[:, :, None]
    fall = falling[:, :, None]
    mixed = (
        mixed_in
        + rise * jnp.einsum("hpn,tn->thp", state_in, reader, preferred_element_type=jnp.float32)
        + fall * jnp.einsum("hpn,tn->thp", state_back, reader, preferred_element_type=jnp.float32)
        + skip_gain[None, :, None] * hidden_rows.astype(jnp.float32)
    )
    back = (
        back_in
        + rise * jnp.einsum("hpn,sn->shp", grad_in, writer, preferred_element_type=jnp.float32)
        + fall * jnp.einsum("hpn,sn->shp", grad_back, writer, preferred_element_type=jnp.float32)
    )
    grad_hidden = step_rows[:, :, None] * back + skip_gain[None, :, None] * grad_rows.astype(
        jnp.float32
    )
    grad_reader = reader_in + jnp.sum(
        rise * jnp.einsum("thp,hpn->thn", grad_rows, state_in, preferred_element_type=jnp.float32)
        + fall
        * jnp.einsum("thp,hpn->thn", grad_rows, state_back, preferred_element_type=jnp.float32),
        axis=1,
    )
    grad_writer = writer_in + jnp.sum(
        rise * jnp.einsum("shp,hpn->shn", scaled, grad_in, preferred_element_type=jnp.float32)
        + fall * jnp.einsum("shp,hpn->shn", scaled, grad_back, preferred_element_type=jnp.float32),
        axis=1,
    )
    return (
        mixed.astype(jnp.bfloat16),
        grad_hidden.astype(jnp.bfloat16),
        grad_reader.astype(jnp.bfloat16),
        grad_writer,
    )


def chain_pair(earlier, latter):
    return (earlier[0] * latter[0], earlier[1] * latter[0][:, :, None, None] + latter[1])


def per_device(
    hidden,
    bmat,
    cmat,
    tokens,
    table,
    step_size,
    log_decay,
    skip_gain,
    prev_state,
    ancestors,
    suffix_start,
    cotangent,
):
    prompt_count, part_count, length, feature_dim = hidden.shape
    pair_count = prompt_count * part_count
    head_count = skip_gain.shape[0]
    head_dim = feature_dim // head_count
    state_dim = bmat.shape[3]
    vocab_size = table.shape[0]
    onehot = (tokens[..., None] == jnp.arange(vocab_size)[None, None, None, :]).astype(jnp.float32)
    looked = jnp.einsum("rplv,vn->rpln", onehot, table, precision=lax.Precision.HIGHEST)
    writer_all = (bmat.astype(jnp.float32) + looked).astype(jnp.bfloat16)
    symbol_site_indices = lax.axis_index("ctx") * length + jnp.arange(length)
    live_rows = symbol_site_indices[None, :] < suffix_start[:, None]
    grad_all = jnp.where(live_rows[:, None, :, None], cotangent, jnp.zeros_like(cotangent))
    shard_part = lax.all_gather(prev_state, "dom", axis=1, tiled=True)
    owners = jnp.arange(shard_part.shape[1])
    chosen = (ancestors[:, :, None] == owners[None, None, :]).astype(jnp.float32)
    chosen_heads = jnp.einsum(
        "rpk,rkhdn->rphdn", chosen, shard_part, precision=lax.Precision.HIGHEST
    )
    begin_state = lax.all_gather(chosen_heads, "ctx", axis=2, tiled=True).reshape(
        pair_count, head_count, head_dim, state_dim
    )
    hidden_rows = hidden.reshape(pair_count, length, head_count, head_dim)
    grad_rows = grad_all.reshape(pair_count, length, head_count, head_dim)
    writer = writer_all.reshape(pair_count, length, state_dim)
    reader = cmat.reshape(pair_count, length, state_dim)
    step_rows = step_size.reshape(pair_count, length, head_count)
    rate_rows = log_decay.reshape(pair_count, length, head_count)
    block_out = jax.vmap(block_terms)(hidden_rows, writer, reader, step_rows, rate_rows, grad_rows)
    decays, state_end, state_begin, grad_end, grad_begin = block_out[7:]
    at_first = jnp.where(lax.axis_index("ctx") == 0, 1.0, 0.0)
    seeded = state_end + at_first * decays[:, :, None, None] * begin_state
    unit_decay = jnp.ones_like(decays)
    zero_state = jnp.zeros_like(state_end)
    state_in = carried_in((decays, seeded), "ctx", chain_pair, (unit_decay, zero_state), False)[1]
    state_back = carried_in(
        (decays, state_begin), "ctx", chain_pair, (unit_decay, zero_state), True
    )[1]
    grad_in = carried_in((decays, grad_end), "ctx", chain_pair, (unit_decay, zero_state), False)[1]
    grad_back = carried_in((decays, grad_begin), "ctx", chain_pair, (unit_decay, zero_state), True)[
        1
    ]
    state_in = state_in + at_first * begin_state
    results = jax.vmap(finish, in_axes=(0, 0, 0, 0, 0, None, 0, 0, 0, 0, 0))(
        hidden_rows,
        writer,
        reader,
        step_rows,
        grad_rows,
        skip_gain,
        block_out[:7],
        state_in,
        state_back,
        grad_in,
        grad_back,
    )
    mixed = results[0].reshape(hidden.shape)
    grad_hidden = results[1].reshape(hidden.shape)
    grad_cmat = results[2].reshape(cmat.shape)
    grad_writer = results[3]
    total_rows = (
        pair_count * length * lax.axis_size("ctx") * lax.axis_size("dom") * lax.axis_size("rep")
    )
    writer_scale = 1.0 / math.sqrt(head_count * head_dim)
    total_scale = 1.0 / math.sqrt(total_rows)
    grad_bmat = (grad_writer * writer_scale).astype(jnp.bfloat16).reshape(bmat.shape)
    table_part = jnp.einsum(
        "clv,cln->vn",
        onehot.reshape(pair_count, length, vocab_size),
        grad_writer,
        precision=lax.Precision.HIGHEST,
    ) * (writer_scale * total_scale)
    skip_part = jnp.einsum(
        "clhp,clhp->h", hidden_rows, grad_rows, preferred_element_type=jnp.float32
    ) * (total_scale / math.sqrt(head_dim))
    grad_table, grad_skip = lax.psum((table_part, skip_part), ("ctx", "dom", "rep"))
    return (mixed, grad_hidden, grad_bmat, grad_cmat, grad_table, grad_skip)


def solution(mesh):
    return jax.shard_map(
        per_device,
        mesh=mesh,
        in_specs=(
            P("rep", "dom", "ctx", None),
            P("rep", "dom", "ctx", None),
            P("rep", "dom", "ctx", None),
            P("rep", "dom", "ctx"),
            P(),
            P("rep", "dom", "ctx", None),
            P("rep", "dom", "ctx", None),
            P(),
            P("rep", "dom", "ctx", None, None),
            P("rep", "dom"),
            P("rep"),
            P("rep", "dom", "ctx", None),
        ),
        out_specs=(
            P("rep", "dom", "ctx", None),
            P("rep", "dom", "ctx", None),
            P("rep", "dom", "ctx", None),
            P("rep", "dom", "ctx", None),
            P(),
            P(),
        ),
        check_vma=False,
    )
```

profile of v0, /device:TPU:0, one launch (start us, length us, event | category | flops | bytes accessed | tf_op | source)
XLA Modules:
  0.0 392.6 jit_solution(15929040369824743849)
XLA Ops:
  7.2 10.2 %all_gather.41 = f32[1,2,4,128,128]{4,3,2,0,1:T(8,128)S(1)} all-gather(f32[1,1,4,128,128]{4,3,2,0,1:T(8,128)} %bitcast.289), channel_id=1, replica_groups=mesh['ctx'=4,'dom'=2,'rep'=4] {'dom'}, dimensions={1}, use_global_device_ids=true | all-gather | bytes 786432 | tf_op jit(solution)/shard_map/all_gather | solution.py:158
  18.1 2.0 fusion.43
  25.8 2.4 mul.344
  28.9 3.0 fusion.32
  41.1 8.6 %all-gather.11.cloned.1.call-done = f32[16,128,128]{2,1,0:T(8,128)} async-done(((f32[4,128,128]{2,1,0:T(8,128)}), f32[16,128,128]{2,1,0:T(8,128)}) %all-gather.11.cloned.1.call-update) | async-done | bytes 1048592 | tf_op jit(solution)/shard_map/all_gather | solution.py:164
  49.6 2.5 convolution_add_fusion
  52.5 2.2 copy.106
  54.8 9.5 %all_gather.40 = f32[4,1,16]{2,1,0:T(1,128)S(1)} all-gather(f32[1,1,16]{2,1,0:T(1,128)S(1)} %get-tuple-element.554), channel_id=1, replica_groups=mesh['ctx'=4,'dom'=2,'rep'=4] {'ctx'}, dimensions={0}, use_global_device_ids=true | all-gather | bytes 320 | tf_op jit(solution)/shard_map/all_gather | solution.py:11
  64.5 2.5 copy.114
  67.0 1.9 fusion.27
  68.9 62.6 %all-gather.15.cloned.1.call-done = f32[64,128,128]{2,1,0:T(8,128)} async-done(((f32[16,128,128]{2,1,0:T(8,128)}), f32[64,128,128]{2,1,0:T(8,128)}) %all-gather.15.cloned.1.call-update) | async-done | bytes 4194320 | tf_op jit(solution)/shard_map/all_gather | solution.py:11
  131.5 4.6 %rev.11 = f32[4,1,16,128,128]{4,3,2,1,0:T(8,128)} reverse(f32[4,1,16,128,128]{4,3,2,1,0:T(8,128)} %bitcast.277), dimensions={0} | reverse | bytes 8388608 | tf_op jit(solution)/shard_map/rev | solution.py:13
  136.1 76.3 %all-gather.19.cloned.1.call-done = f32[64,128,128]{2,1,0:T(8,128)} async-done(((f32[16,128,128]{2,1,0:T(8,128)}), f32[64,128,128]{2,1,0:T(8,128)}) %all-gather.19.cloned.1.call-update) | async-done | bytes 4194320 | tf_op jit(solution)/shard_map/all_gather | solution.py:11
  212.4 4.7 %rev.12 = f32[4,1,16,128,128]{4,3,2,1,0:T(8,128)} reverse(f32[4,1,16,128,128]{4,3,2,1,0:T(8,128)} %bitcast.278), dimensions={0} | reverse | bytes 8388608 | tf_op jit(solution)/shard_map/rev | solution.py:13
  217.0 4.6 %while.59 = (s32[]{:T(128)}, f32[1,16,128,128]{3,2,1,0:T(8,128)S(1)}, s32[]{:T(128)}, f32[4,1,16]{2,1,0:T(1,128)S(1)}, f32[4,1,16,128,128]{4,3,2,1,0:T(8,128)}, /*index=5*/s32[]{:T(128)}, s32[]{:T(128)}) while((s32[]{:T(128)}, f32[1,16,128,128]{3,2,1,0:T(8,128)S(1)}, s32[]{:T(128)}, f32[4,1,16]{2,1,0:T(1,128)S(1)}, ...), condition=%wide.region_8.9_spmd.clone, body=%wide.region_7.8_spmd.clone.sunk | while | flops 1048580 | bytes 3146025 | solution.py:23
  223.0 70.2 %all-gather.17.cloned.1.call-done = f32[64,128,128]{2,1,0:T(8,128)} async-done(((f32[16,128,128]{2,1,0:T(8,128)}), f32[64,128,128]{2,1,0:T(8,128)}) %all-gather.17.cloned.1.call-update) | async-done | bytes 4194320 | tf_op jit(solution)/shard_map/all_gather | solution.py:11
  293.1 4.5 %while.58 = (s32[]{:T(128)}, f32[1,16,128,128]{3,2,1,0:T(8,128)S(1)}, s32[]{:T(128)}, f32[4,1,16]{2,1,0:T(1,128)S(1)}, f32[4,1,16,128,128]{4,3,2,1,0:T(8,128)}, /*index=5*/s32[]{:T(128)}, s32[]{:T(128)}) while((s32[]{:T(128)}, f32[1,16,128,128]{3,2,1,0:T(8,128)S(1)}, s32[]{:T(128)}, f32[4,1,16]{2,1,0:T(1,128)S(1)}, ...), condition=%wide.region_6.7_spmd.clone, body=%wide.region_5.6_spmd.clone.sunk | while | flops 1048580 | bytes 3146025 | solution.py:23
  297.9 3.4 fusion.23
  301.3 2.1 copy.125
  307.5 43.5 %all-reduce = (f32[4,128]{1,0:T(4,128)}, f32[16]{0:T(128)}) all-reduce(f32[4,128]{1,0:T(4,128)S(1)} %convolution_multiply_fusion.3, f32[16]{0:T(128)S(1)} %broadcast_multiply_fusion), channel_id=1, replica_groups=mesh['ctx'=4,'dom'=2,'rep'=4] {'ctx','dom','rep'}, use_global_device_ids=true, to_apply=%region_12.13 | all-reduce | flops 528 | bytes 4224 | tf_op jit(solution)/shard_map/psum | solution.py:220
  351.0 4.5 %while.57 = (s32[]{:T(128)}, f32[1,16,128,128]{3,2,1,0:T(8,128)S(1)}, s32[]{:T(128)}, f32[4,1,16]{2,1,0:T(1,128)S(1)}, f32[4,1,16,128,128]{4,3,2,1,0:T(8,128)}, /*index=5*/s32[]{:T(128)}, s32[]{:T(128)}) while((s32[]{:T(128)}, f32[1,16,128,128]{3,2,1,0:T(8,128)S(1)}, s32[]{:T(128)}, f32[4,1,16]{2,1,0:T(1,128)S(1)}, ...), condition=%wide.region_4.5_spmd.clone, body=%wide.region_3.4_spmd.clone.sunk | while | flops 1048580 | bytes 3146025 | solution.py:23
  359.0 15.9 %all-gather.13.cloned.1.call-done = f32[64,128,128]{2,1,0:T(8,128)} async-done(((f32[16,128,128]{2,1,0:T(8,128)}), f32[64,128,128]{2,1,0:T(8,128)}) %all-gather.13.cloned.1.call-update) | async-done | bytes 4194320 | tf_op jit(solution)/shard_map/all_gather | solution.py:11
  374.9 4.5 %while.56 = (s32[]{:T(128)}, f32[1,16,128,128]{3,2,1,0:T(8,128)S(1)}, s32[]{:T(128)}, f32[4,1,16]{2,1,0:T(1,128)S(1)}, f32[4,1,16,128,128]{4,3,2,1,0:T(8,128)}, /*index=5*/s32[]{:T(128)}, s32[]{:T(128)}) while((s32[]{:T(128)}, f32[1,16,128,128]{3,2,1,0:T(8,128)S(1)}, s32[]{:T(128)}, f32[4,1,16]{2,1,0:T(1,128)S(1)}, ...), condition=%wide.region_2.3_spmd.clone, body=%wide.region_1.2_spmd.clone.sunk | while | flops 1048580 | bytes 3146025 | solution.py:23
  382.5 2.6 fusion.24
  (116 shorter events, 46.3 us)
Async XLA Ops:
  7.2 29.0 %copy-start = (bf16[1,1,128,128]{3,2,1,0:T(8,128)(2,1)S(1)}, bf16[1,1,128,128]{3,2,1,0:T(8,128)(2,1)}, u32[]{:S(2)}) copy-start(bf16[1,1,128,128]{3,2,1,0:T(8,128)(2,1)} %param.22) | copy-start | bytes 98308
  7.2 42.4 %all-gather.11.cloned.1.call-start = ((), (), s32[]{:S(2)}) async-start(), calls=%async_computation | async-start | bytes 1310720 | tf_op jit(solution)/shard_map/all_gather | solution.py:164
  7.2 17.1 %copy-start.11 = (f32[1,1,128,16]{2,3,1,0:T(8,128)S(1)}, f32[1,1,128,16]{2,3,1,0:T(8,128)}, u32[]{:S(2)}) copy-start(f32[1,1,128,16]{2,3,1,0:T(8,128)} %param.25) | copy-start | bytes 24580
  20.1 111.4 %all-gather.15.cloned.1.call-start = ((), (), s32[]{:S(2)}) async-start(), calls=%async_computation.2 | async-start | bytes 5242880 | tf_op jit(solution)/shard_map/all_gather | solution.py:11
  21.4 7.5 %copy-start.6 = (bf16[1,1,128,2048]{3,2,1,0:T(8,128)(2,1)S(1)}, bf16[1,1,128,2048]{3,2,1,0:T(8,128)(2,1)}, u32[]{:S(2)}) copy-start(bf16[1,1,128,2048]{3,2,1,0:T(8,128)(2,1)} %param.20) | copy-start | bytes 1572868
  21.4 7.5 %copy-start.8 = (bf16[1,1,128,2048]{3,2,1,0:T(8,128)(2,1)S(1)}, bf16[1,1,128,2048]{3,2,1,0:T(8,128)(2,1)}, u32[]{:S(2)}) copy-start(bf16[1,1,128,2048]{3,2,1,0:T(8,128)(2,1)} %param.31) | copy-start | bytes 1572868
  28.2 5.1 %copy-start.13 = (s32[1,1,128]{2,1,0:T(1,128)S(1)}, s32[1,1,128]{2,1,0:T(1,128)}, u32[]{:S(2)}) copy-start(s32[1,1,128]{2,1,0:T(1,128)} %param.23) | copy-start | bytes 1540
  28.2 5.1 %copy-start.14 = (bf16[1,1,128,128]{3,2,1,0:T(8,128)(2,1)S(1)}, bf16[1,1,128,128]{3,2,1,0:T(8,128)(2,1)}, u32[]{:S(2)}) copy-start(bf16[1,1,128,128]{3,2,1,0:T(8,128)(2,1)} %param.21) | copy-start | bytes 98308
  28.2 5.1 %copy-start.15 = (f32[4,128]{1,0:T(4,128)S(1)}, f32[4,128]{1,0:T(4,128)}, u32[]{:S(2)}) copy-start(f32[4,128]{1,0:T(4,128)} %param.24) | copy-start | bytes 6148
  31.9 5.7 %copy-start.10 = (bf16[1,1,128,2048]{3,2,1,0:T(8,128)(2,1)S(1)}, bf16[1,1,128,2048]{3,2,1,0:T(8,128)(2,1)}, u32[]{:S(2)}) copy-start(bf16[1,1,128,2048]{3,2,1,0:T(8,128)(2,1)} %get-tuple-element.551) | copy-start | bytes 1572868
  34.8 177.6 %all-gather.19.cloned.1.call-start = ((), (), s32[]{:S(2)}) async-start(), calls=%async_computation.4 | async-start | bytes 5242880 | tf_op jit(solution)/shard_map/all_gather | solution.py:11
  37.5 3.0 copy-start.9
  37.5 255.7 %all-gather.17.cloned.1.call-start = ((), (), s32[]{:S(2)}) async-start(), calls=%async_computation.3 | async-start | bytes 5242880 | tf_op jit(solution)/shard_map/all_gather | solution.py:11
  39.2 335.7 %all-gather.13.cloned.1.call-start = ((), (), s32[]{:S(2)}) async-start(), calls=%async_computation.1 | async-start | bytes 5242880 | tf_op jit(solution)/shard_map/all_gather | solution.py:11
  40.5 11.6 %copy-start.4 = (bf16[16,8,16,128]{3,2,1,0:T(8,128)(2,1)}, bf16[16,8,16,128]{3,2,1,0:T(8,128)(2,1)S(1)}, u32[]{:S(2)}) copy-start(bf16[16,8,16,128]{3,2,1,0:T(8,128)(2,1)S(1)} %copy.147) | copy-start | bytes 1572868
  40.9 11.2 %copy-start.2 = (bf16[16,8,16,128]{3,2,1,0:T(8,128)(2,1)}, bf16[16,8,16,128]{3,2,1,0:T(8,128)(2,1)S(1)}, u32[]{:S(2)}) copy-start(bf16[16,8,16,128]{3,2,1,0:T(8,128)(2,1)S(1)} %copy.146) | copy-start | bytes 1572868
  293.1 4.8 %copy-start.12 = (f32[16]{0:T(128)S(1)}, f32[16]{0:T(128)}, u32[]{:S(2)}) copy-start(f32[16]{0:T(128)} %param.27) | copy-start | bytes 196
  351.0 6.5 %copy-start.5 = (bf16[16,8,16,128]{3,2,1,0:T(8,128)(2,1)S(1)}, bf16[16,8,16,128]{3,2,1,0:T(8,128)(2,1)}, u32[]{:S(2)}) copy-start(bf16[16,8,16,128]{3,2,1,0:T(8,128)(2,1)} %copy-done.4) | copy-start | bytes 1572868
  355.5 19.4 %copy-start.1 = (f32[1,16,128,128]{3,2,1,0:T(8,128)S(1)}, f32[1,16,128,128]{3,2,1,0:T(8,128)}, u32[]{:S(2)}) copy-start(f32[1,16,128,128]{3,2,1,0:T(8,128)} %custom-call) | copy-start | bytes 3145732
  379.4 1.8 copy-start.7
  379.4 3.2 copy-start.3
Sparse Core Ops, SparseCore 0:
  20.2 29.3 all-gather.10
  51.2 80.2 all-gather.14
  133.1 79.2 all-gather.18
  213.8 79.2 all-gather.16
  294.6 80.2 all-gather.12
where the time goes:
time: 394 us; the launch traced here: 393 us
  waiting for transfers between devices  234 us (59%)
  blocking collectives  63.2 us (16%)
  local copies, waits for them, and re-layouts  28.8 us (7%)
  matrix products  26.5 us (7%)
  other arithmetic  24.6 us (6%)
  between operations  15.5 us (4%)
    all_gather x4, waiting for transfers between devices, carried_in(): pieces = jax.tree.map(lambda part: lax.all_gather(part, axis), value)  225 us
    psum x1, blocking collectives, per_device(): lax.psum((table_part, skip_part), ('ctx', 'dom', 'rep'))  43.5 us
    select_n x12, other arithmetic, turn(): jnp.where(position < mine, new, old)  17.7 us
    all_gather x1, blocking collectives, per_device(): shard_part = lax.all_gather(prev_state, 'dom', axis=1, tiled=True)  10.2 us
    all_gather x1, blocking collectives, carried_in(): pieces = jax.tree.map(lambda part: lax.all_gather(part, axis), value)  9.49 us
    rev x3, local copies, waits for them, and re-layouts, carried_in(): pieces = jax.tree.map(lambda part: part[::-1], pieces)  9.28 us
    all_gather x1, waiting for transfers between devices, per_device(): lax.all_gather(chosen_heads, 'ctx', axis=2, tiled=True)  8.56 us
  transfers between devices with their start and end apart: 5, of which 5 were waited for; matrix products, arithmetic and copies ran while one was open for 17% of the time, Pallas kernels for 0%

commit v1 on v0

v1 whole, which is shorter than its diff:
```python
import functools
import math

import jax
import jax.numpy as jnp
from jax import lax
from jax.experimental import pallas as pl
from jax.experimental.pallas import tpu as pltpu
from jax.sharding import PartitionSpec as P

F32 = jnp.float32
BF16 = jnp.bfloat16
EXACT = lax.Precision.HIGHEST
NN = (((1,), (0,)), ((), ()))
NT = (((1,), (1,)), ((), ()))
TN = (((0,), (0,)), ((), ()))
CHUNKS = 4
HBM, CHIP = pltpu.HBM, pltpu.VMEM


def dot(left, right, dims=NN, precision=None):
    return lax.dot_general(
        left, right, dims, precision=precision, preferred_element_type=F32
    )


def one_hot_rows(tokens_row, rows):
    kinds = lax.broadcasted_iota(jnp.int32, (rows, tokens_row.shape[1]), 0)
    return kinds == tokens_row


def live_rows(meta, shape):
    return meta[0] + lax.broadcasted_iota(jnp.int32, shape, 0) < meta[1]


def column(cols, kind, per_chunk, head):
    at = kind * per_chunk + head
    return cols[:, at : at + 1]


STEP, RISE, FALL, CUM = range(4)


def start_kernel(
    per_chunk, head_dim, vocab, chunks,
    meta, bmat, cmat, tokens, table, step_t, rate_t, hid_far, cot_far,
    up_first, down_first, up_small, down_small, cols, writer,
    hid, cot, sems,
):
    length = bmat.shape[0]
    state = bmat.shape[1]
    part = per_chunk * head_dim
    lines = up_small.shape[1]
    copies = []
    for chunk in range(chunks):
        span = slice(chunk * part, (chunk + 1) * part)
        pair = [
            pltpu.make_async_copy(far.at[:, span], near.at[:, span], sems.at[chunk, at])
            for at, (far, near) in enumerate(((hid_far, hid), (cot_far, cot)))
        ]
        for copy in pair:
            copy.start()
        copies.append(pair)

    row = lax.broadcasted_iota(jnp.int32, (length, length), 0)
    col = lax.broadcasted_iota(jnp.int32, (length, length), 1)
    lower = jnp.where(col <= row, 1.0, 0.0).astype(F32)
    cumulative = dot(lower, rate_t[...], NT, EXACT)
    totals = cumulative[length - 1 : length, :]
    rising = jnp.exp(-cumulative)
    falling = jnp.exp(-(totals - cumulative))
    step = step_t[...].T
    for at in range(chunks):
        lo = at * per_chunk
        for kind, values in enumerate((step, rising, falling, cumulative)):
            cols[at, :, kind * per_chunk : (kind + 1) * per_chunk] = values[:, lo : lo + per_chunk]
    hot = one_hot_rows(tokens[...], vocab)
    looked = dot(jnp.where(hot, 1.0, 0.0).astype(F32), table[...], TN, EXACT)
    rows = (bmat[...].astype(F32) + looked).astype(BF16)
    writer[...] = rows
    chosen = jnp.where(one_hot_rows(tokens[...], lines), 1.0, 0.0).astype(BF16)
    kinds = lax.broadcasted_iota(jnp.int32, (lines, part), 0)
    live = live_rows(meta, (length, head_dim))
    for chunk in range(chunks):
        for copy in copies[chunk]:
            copy.wait()
        fallen, risen, grad_fallen, grad_risen, gone, skips = [], [], [], [], [], []
        for head in range(per_chunk):
            number = chunk * per_chunk + head
            at = slice(number * head_dim, (number + 1) * head_dim)
            rise = rising[:, number : number + 1]
            fall = falling[:, number : number + 1]
            values = hid[:, at].astype(F32)
            scaled = (step[:, number : number + 1] * values).astype(BF16).astype(F32)
            grads = jnp.where(live, cot[:, at].astype(F32), 0.0)
            fallen.append((fall * scaled).astype(BF16))
            risen.append((rise * scaled).astype(BF16))
            if chunk == 0:
                grad_fallen.append((fall * grads).astype(BF16))
                grad_risen.append((rise * grads).astype(BF16))
            gone.append(jnp.broadcast_to(rise[length - 1 : length, :], (1, head_dim)))
            skips.append(jnp.sum(values * grads, axis=0, keepdims=True))
        fallen, risen, gone, skips = (
            jnp.concatenate(parts, axis=1) for parts in (fallen, risen, gone, skips)
        )
        up_lines = jnp.where(
            kinds == vocab, jnp.where(meta[2] == 0, gone, 0.0), dot(chosen, fallen)
        )
        down_lines = jnp.where(
            kinds == vocab, gone, jnp.where(kinds == vocab + 1, skips, dot(chosen, risen))
        )
        up_small[chunk] = up_lines
        down_small[chunk] = down_lines
        small_rows = slice(2 * state + chunk * lines, 2 * state + (chunk + 1) * lines)
        up_first[small_rows, :] = up_lines
        down_first[small_rows, :] = down_lines
        if chunk == 0:
            writer_t, reader_t = rows.T, cmat[...].T
            up_first[0:state, :] = dot(writer_t, fallen)
            down_first[0:state, :] = dot(writer_t, risen)
            up_first[state : 2 * state, :] = dot(reader_t, jnp.concatenate(grad_fallen, axis=1))
            down_first[state : 2 * state, :] = dot(reader_t, jnp.concatenate(grad_risen, axis=1))


def combine_kernel(vocab, has_small, land, source, waits, *refs):
    meta, received, own, small, decays = refs[:5]
    send, held, near, rounded, sems = refs[-5:]
    del waits
    state = own.shape[2]
    fetch = [
        pltpu.make_async_copy(own.at[meta[source], at], near.at[at], sems.at[at])
        for at in range(2)
    ]
    for copy in fetch:
        copy.start()
    rounded[...] = received[0 : 2 * state, :].astype(BF16)
    store = pltpu.make_async_copy(rounded, held.at[meta[land]], sems.at[2])
    store.start()
    decay = decays[meta[source], vocab : vocab + 1, :]
    if has_small:
        lines = small.shape[1]
        for at in range(small.shape[0]):
            rows = slice(2 * state + at * lines, 2 * state + (at + 1) * lines)
            send[rows, :] = decays[at, vocab : vocab + 1, :] * received[rows, :] + small[at]
    for at in range(2):
        fetch[at].wait()
        rows = slice(at * state, (at + 1) * state)
        send[rows, :] = decay * received[rows, :] + near[at]
    store.wait()


def inner_kernel(
    per_chunk, head_dim, vocab,
    meta, hid, cot, writer, cmat, tokens, cols,
    up, down, mixed_in, back_in, reader_in, writer_in, tab,
    inner, inner_t, cross, writer_t, reader_t,
):
    chunk = pl.program_id(0)
    length = hid.shape[0]

    @pl.when(chunk == 0)
    def _():
        inner[...] = dot(cmat[...], writer[...], NT)
        inner_t[...] = dot(writer[...], cmat[...], NT)
        cross[...] = jnp.zeros_like(cross)
        writer_t[...] = writer[...].T
        reader_t[...] = cmat[...].T

    mine = cols[0]
    across = mine.T
    live = live_rows(meta, (length, head_dim))
    fallen, risen, grad_fallen, grad_risen = [], [], [], []
    for head in range(per_chunk):
        at = slice(head * head_dim, (head + 1) * head_dim)
        row = CUM * per_chunk + head
        decay = jnp.exp(
            -jnp.abs(column(mine, CUM, per_chunk, head) - across[row : row + 1, :])
        )
        rise = column(mine, RISE, per_chunk, head)
        fall = column(mine, FALL, per_chunk, head)
        scaled = (column(mine, STEP, per_chunk, head) * hid[:, at].astype(F32)).astype(BF16)
        grads_wide = jnp.where(live, cot[:, at].astype(F32), 0.0)
        grads = grads_wide.astype(BF16)
        scaled_wide = scaled.astype(F32)
        fallen.append((fall * scaled_wide).astype(BF16))
        risen.append((rise * scaled_wide).astype(BF16))
        grad_fallen.append((fall * grads_wide).astype(BF16))
        grad_risen.append((rise * grads_wide).astype(BF16))
        mixed_in[:, at] = dot((decay * inner[...]).astype(BF16), scaled)
        back_in[:, at] = dot((decay * inner_t[...]).astype(BF16), grads)
        cross[...] += decay * dot(grads, scaled, NT)
    up[0, 0] = dot(writer_t[...], jnp.concatenate(fallen, axis=1))
    up[0, 1] = dot(reader_t[...], jnp.concatenate(grad_fallen, axis=1))
    down[0, 0] = dot(writer_t[...], jnp.concatenate(risen, axis=1))
    down[0, 1] = dot(reader_t[...], jnp.concatenate(grad_risen, axis=1))

    @pl.when(chunk == pl.num_programs(0) - 1)
    def _():
        crossed = cross[...].astype(BF16)
        reader_in[...] = dot(crossed, writer[...])
        into = dot(crossed.astype(F32).T.astype(BF16), cmat[...])
        writer_in[...] = into
        chosen = jnp.where(one_hot_rows(tokens[...], tab.shape[0]), 1.0, 0.0).astype(F32)
        tab[...] = dot(chosen, into, precision=EXACT)


def sums_kernel(
    per_chunk, head_dim, vocab, table_scale, skip_scale,
    meta, earlier, later, small, grad_up, grad_down, tab, total, acc,
):
    chunk = pl.program_id(0)
    lines, width = earlier.shape

    @pl.when(chunk == 0)
    def _():
        acc[...] = jnp.zeros_like(acc)

    def split(lhs, rhs):
        high = lhs.astype(BF16)
        low = (lhs - high.astype(F32)).astype(BF16)
        both = dot(jnp.concatenate([high, low], axis=0), rhs.astype(BF16), NT)
        return both[0:lines] + both[lines:]

    head_of = chunk * per_chunk + lax.broadcasted_iota(jnp.int32, (128, width), 1) // head_dim
    picks = jnp.where(
        head_of == lax.broadcasted_iota(jnp.int32, (128, width), 0), 1.0, 0.0
    ).astype(F32)
    kinds = lax.broadcasted_iota(jnp.int32, (lines, 128), 0)
    tables = split(later[...], grad_up[0, 0]) + split(earlier[...], grad_down[0, 0])
    skips = jnp.broadcast_to(small[0, vocab + 1 : vocab + 2, :], (lines, width))
    acc[...] += jnp.where(kinds < vocab, tables, split(skips, picks))

    @pl.when(chunk == pl.num_programs(0) - 1)
    def _():
        total[...] = jnp.where(
            kinds < vocab,
            (acc[...] + tab[...]) * table_scale,
            jnp.where(kinds == vocab, acc[...] * skip_scale, 0.0),
        )


def finish_chunk(
    per_chunk, head_dim, vocab, meta, chunk, gains, hid, cot, writer, cmat, mine,
    mixed_in, back_in, chain_in, chain_back, begin_here, begin_there, earlier,
    mixed, grad_hidden, acc_c, acc_w,
):
    length = hid.shape[0]
    state = chain_in.shape[0] // 2
    live = live_rows(meta, (length, head_dim))
    begins = jnp.concatenate(
        [
            jnp.where(meta[3] != 0, begin_here[at], begin_there[at]).T
            for at in range(per_chunk)
        ],
        axis=1,
    )
    passed = jnp.where(meta[2] == 0, 1.0, earlier[vocab : vocab + 1, :])
    state_in = (chain_in[0:state].astype(F32) + passed * begins).astype(BF16)
    grad_in = chain_in[state:]
    state_back = chain_back[0:state]
    grad_back = chain_back[state:]
    from_in = dot(cmat, state_in)
    from_back = dot(cmat, state_back)
    grad_from_in = dot(writer, grad_in)
    grad_from_back = dot(writer, grad_back)
    fallen, risen, grad_fallen, grad_risen = [], [], [], []
    for head in range(per_chunk):
        at = slice(head * head_dim, (head + 1) * head_dim)
        rise = column(mine, RISE, per_chunk, head)
        fall = column(mine, FALL, per_chunk, head)
        step = column(mine, STEP, per_chunk, head)
        gain = gains[chunk * per_chunk + head]
        values = hid[:, at].astype(F32)
        scaled = (step * values).astype(BF16).astype(F32)
        grads = jnp.where(live, cot[:, at].astype(F32), 0.0)
        mixed[:, at] = (
            mixed_in[:, at] + rise * from_in[:, at] + fall * from_back[:, at] + gain * values
        ).astype(BF16)
        back = back_in[:, at] + rise * grad_from_in[:, at] + fall * grad_from_back[:, at]
        grad_hidden[:, at] = (step * back + gain * grads).astype(BF16)
        fallen.append((fall * scaled).astype(BF16))
        risen.append((rise * scaled).astype(BF16))
        grad_fallen.append((fall * grads).astype(BF16))
        grad_risen.append((rise * grads).astype(BF16))
    fallen, risen, grad_fallen, grad_risen = (
        jnp.concatenate(parts, axis=1) for parts in (fallen, risen, grad_fallen, grad_risen)
    )
    acc_c[...] += dot(grad_risen, state_in, NT) + dot(grad_fallen, state_back, NT)
    acc_w[...] += dot(risen, grad_in, NT) + dot(fallen, grad_back, NT)


def early_kernel(
    per_chunk, head_dim, vocab,
    meta, gains, hid, cot, writer, cmat, cols, mixed_in, back_in, reader_in, writer_in,
    held_up, held_down, begin_here, begin_there, earlier, *refs,
):
    mixed, grad_hidden, acc_c, acc_w = refs[-4:]
    chunk = pl.program_id(0)

    @pl.when(chunk == 0)
    def _():
        acc_c[...] = reader_in[...]
        acc_w[...] = writer_in[...]

    finish_chunk(
        per_chunk, head_dim, vocab, meta, chunk, gains, hid, cot, writer[...], cmat[...],
        cols[0], mixed_in, back_in, held_up[0], held_down[0], begin_here, begin_there, earlier,
        mixed, grad_hidden, acc_c, acc_w,
    )


def last_kernel(
    per_chunk, head_dim, vocab, bmat_scale, up_land, down_land, chunk,
    meta, gains, hid, cot, writer, cmat, cols, mixed_in, back_in, sum_c, sum_w,
    held_up, held_down, begin_here, begin_there, earlier, got_up, got_down, mixed_old, hidden_old,
    mixed, grad_hidden, grad_cmat, grad_bmat, acc_c, acc_w,
):
    del mixed_old, hidden_old
    acc_c[...] = sum_c[...]
    acc_w[...] = sum_w[...]
    chain_in = jnp.where(meta[up_land] == chunk, got_up[...].astype(BF16), held_up[0])
    chain_back = jnp.where(meta[down_land] == chunk, got_down[...].astype(BF16), held_down[0])
    finish_chunk(
        per_chunk, head_dim, vocab, meta, chunk, gains, hid, cot, writer[...], cmat[...],
        cols[0], mixed_in, back_in, chain_in, chain_back, begin_here, begin_there, earlier,
        mixed, grad_hidden, acc_c, acc_w,
    )
    grad_cmat[...] = acc_c[...].astype(BF16)
    grad_bmat[...] = (acc_w[...] * bmat_scale).astype(BF16)


def whole(shape):
    return pl.BlockSpec(shape, lambda *_: (0,) * len(shape))


def call(body, scalars, grid, ins, outs, scratch=(), aliases=None, limit=16 << 20):
    results = pl.pallas_call(
        body,
        out_shape=[
            jax.ShapeDtypeStruct(shape, kind) if place is None else place(shape, kind)
            for shape, kind, _, place in outs
        ],
        grid_spec=pltpu.PrefetchScalarGridSpec(
            num_scalar_prefetch=len(scalars),
            grid=grid,
            in_specs=[spec for _, spec, _ in ins],
            out_specs=[spec for _, _, spec, _ in outs],
            scratch_shapes=list(scratch),
        ),
        input_output_aliases=aliases or {},
        compiler_params=pltpu.CompilerParams(vmem_limit_bytes=limit),
    )(
        *scalars,
        *[
            array if place is None else pltpu.with_memory_space_constraint(array, place)
            for array, _, place in ins
        ],
    )
    return results


def sum_steps(axes):
    steps = []
    for axis in axes:
        count = lax.axis_size(axis)
        if count & (count - 1):
            steps.append(lambda value, axis=axis: lax.psum(value, axis))
            continue
        hop = 1
        while hop < count:
            swap = [(at, at ^ hop) for at in range(count)]
            steps.append(
                lambda value, axis=axis, swap=swap: value + lax.ppermute(value, axis, swap)
            )
            hop *= 2
    return steps


def per_device(
    hidden, bmat, cmat, tokens, table, step_size, log_decay, skip_gain,
    prev_state, ancestors, suffix_start, cotangent,
):
    prompts, parts, length, width = hidden.shape
    assert prompts * parts == 1
    heads = skip_gain.shape[0]
    head_dim = width // heads
    state_dim = bmat.shape[3]
    vocab = table.shape[0]
    count = lax.axis_size("ctx")
    doms = lax.axis_size("dom")
    place = lax.axis_index("ctx")
    chunks = CHUNKS
    per_chunk = heads // chunks
    part = width // chunks
    total_rows = length * count * doms * lax.axis_size("rep")
    bmat_scale = 1.0 / math.sqrt(width)
    total_scale = 1.0 / math.sqrt(total_rows)
    lines = -(-(vocab + 2) // 8) * 8
    slots = chunks + count - 2

    hid = hidden.reshape(length, width)
    cot = cotangent.reshape(length, width)
    writes = bmat.reshape(length, state_dim)
    reads = cmat.reshape(length, state_dim)
    toks = tokens.reshape(1, length)
    steps_t = jnp.swapaxes(step_size, 2, 3).reshape(heads, length)
    rates_t = jnp.swapaxes(log_decay, 2, 3).reshape(heads, length)
    ancestor = ancestors[0, 0]
    here = ancestor == lax.axis_index("dom")

    times = jnp.arange(slots, dtype=jnp.int32)
    from_last = count - 1 - place
    table_of = []
    for far in (place, from_last):
        lands = times - jnp.maximum(far, 1) + 1
        table_of.append(jnp.where((lands >= 0) & (lands < chunks), lands, chunks))
        table_of.append(jnp.clip(times + 1 - far, 0, chunks - 1))
    base = jnp.stack([place * length, suffix_start[0], place, here]).astype(jnp.int32)
    meta = jnp.concatenate([base] + table_of)
    up_land, up_source, down_land, down_source = (4 + at * slots for at in range(4))

    own_state = prev_state[0, 0]
    if doms == 2:
        begin_here = lax.all_gather(own_state, "ctx", tiled=True)
    else:
        own_state = lax.dynamic_index_in_dim(
            lax.all_gather(own_state, "dom"), ancestor, 0, keepdims=False
        )
        begin_here = lax.all_gather(own_state, "ctx", tiled=True)

    anywhere = pl.BlockSpec(memory_space=pl.ANY)
    near = pl.BlockSpec(memory_space=pltpu.VMEM)
    by_chunk = pl.BlockSpec((length, part), lambda k, *_: (0, k))
    one_cols = pl.BlockSpec((1, length, 128), lambda k, *_: (k, 0, 0))
    pair = pl.BlockSpec((1, 2, state_dim, part), lambda k, *_: (k, 0, 0, 0))
    one_small = pl.BlockSpec((1, lines, part), lambda k, *_: (k, 0, 0))
    square = whole((length, state_dim))
    tok_spec = whole((1, length))
    full_rows = 2 * state_dim + chunks * lines
    small_shape = (chunks, lines, part)
    first = ((full_rows, part), F32, whole((full_rows, part)), CHIP)

    up_first, down_first, up_small, down_small, cols, writer = call(
        functools.partial(start_kernel, per_chunk, head_dim, vocab, chunks),
        (meta,), (1,),
        [
            (writes, square, HBM), (reads, square, HBM), (toks, tok_spec, HBM),
            (table, whole(table.shape), HBM), (steps_t, whole(steps_t.shape), HBM),
            (rates_t, whole(rates_t.shape), HBM), (hid, anywhere, HBM), (cot, anywhere, HBM),
        ],
        [
            first, first,
            (small_shape, F32, whole(small_shape), CHIP),
            (small_shape, F32, whole(small_shape), CHIP),
            ((chunks, length, 128), F32, whole((chunks, length, 128)), HBM),
            ((length, state_dim), BF16, square, HBM),
        ],
        [
            pltpu.VMEM((length, width), BF16), pltpu.VMEM((length, width), BF16),
            pltpu.SemaphoreType.DMA((chunks, 2)),
        ],
    )

    up, down, mixed_in, back_in, reader_in, writer_in, tab = call(
        functools.partial(inner_kernel, per_chunk, head_dim, vocab),
        (meta,), (chunks,),
        [
            (hid, by_chunk, HBM), (cot, by_chunk, HBM), (writer, square, HBM),
            (reads, square, HBM), (toks, tok_spec, HBM), (cols, one_cols, HBM),
        ],
        [
            ((chunks, 2, state_dim, part), F32, pair, HBM),
            ((chunks, 2, state_dim, part), F32, pair, HBM),
            ((length, width), F32, by_chunk, HBM),
            ((length, width), F32, by_chunk, HBM),
            ((length, state_dim), F32, square, HBM),
            ((length, state_dim), F32, square, HBM),
            ((lines, state_dim), F32, whole((lines, state_dim)), HBM),
        ],
        [pltpu.VMEM((length, length), F32)] * 3 + [pltpu.VMEM((state_dim, length), BF16)] * 2,
    )

    def step_chain(slot, received, own, small, land, source, held, waits):
        has_small = slot < count - 2
        rows = full_rows if has_small else 2 * state_dim
        held_shape = (chunks + 1, 2 * state_dim, part)
        ins = [
            (received, near, CHIP), (own, anywhere, HBM), (small, near, CHIP),
            (down_small, near, CHIP),
        ]
        aliases = {}
        if held is not None:
            aliases = {1 + len(ins): 1}
            ins.append((held, anywhere, HBM))
        ins += [(value, anywhere, None) for value in waits]
        return call(
            functools.partial(
                combine_kernel, vocab, has_small, land + slot, source + slot, len(waits)
            ),
            (meta,), (), ins,
            [((rows, part), F32, near, CHIP), (held_shape, BF16, anywhere, HBM)],
            [
                pltpu.VMEM((2, state_dim, part), F32), pltpu.VMEM((2 * state_dim, part), BF16),
                pltpu.SemaphoreType.DMA((3,)),
            ],
            aliases=aliases,
        )

    upward = [(at, at + 1) for at in range(count - 1)]
    downward = [(at + 1, at) for at in range(count - 1)]
    lines_at = 2 * state_dim // lines
    from_slot = pl.BlockSpec((lines, part), lambda k, *_: (lines_at + k, 0))
    grad_part = pl.BlockSpec((1, 1, state_dim, part), lambda k, *_: (k, 1, 0, 0))
    sums = sum_steps(("rep", "dom", "ctx"))
    send_up, send_down, held_up, held_down = up_first, down_first, None, None
    begin_there = begin_here
    total = None
    for slot in range(slots):
        got_up = lax.ppermute(send_up, "ctx", upward)
        got_down = lax.ppermute(send_down, "ctx", downward)
        waits = []
        if slot == count - 2:
            earlier, later = got_up, got_down
            waits.append(begin_here)
        if slot == count - 1:
            if doms == 2:
                begin_there = lax.ppermute(begin_here, "dom", [(0, 1), (1, 0)])
            (total,) = call(
                functools.partial(
                    sums_kernel, per_chunk, head_dim, vocab,
                    bmat_scale * total_scale, total_scale / math.sqrt(head_dim),
                ),
                (meta,), (chunks,),
                [
                    (earlier, from_slot, None), (later, from_slot, None),
                    (down_small, one_small, None), (up, grad_part, HBM),
                    (down, grad_part, HBM), (tab, whole(tab.shape), HBM),
                ],
                [((lines, state_dim), F32, whole((lines, state_dim)), None)],
                [pltpu.VMEM((lines, state_dim), F32)],
            )
            waits.append(total)
        if slot >= count:
            for step in sums[:2]:
                total = step(total)
            sums = sums[2:]
            waits.append(total)
            waits.append(begin_there)
        if slot == slots - 1:
            break
        send_up, held_up = step_chain(
            slot, got_up, up, up_small, up_land, up_source, held_up, waits
        )
        send_down, held_down = step_chain(
            slot, got_down, down, down_small, down_land, down_source, held_down, []
        )

    def chunk_specs(at):
        return (
            pl.BlockSpec((length, part), lambda k, *_: (0, k + at)),
            pl.BlockSpec((1, length, 128), lambda k, *_: (k + at, 0, 0)),
            pl.BlockSpec((1, 2 * state_dim, part), lambda k, *_: (k + at, 0, 0)),
            pl.BlockSpec((per_chunk, head_dim, state_dim), lambda k, *_: (k + at, 0, 0)),
            pl.BlockSpec((lines, part), lambda k, *_: (lines_at + k + at, 0)),
        )

    def finish_ins(at, sum_c, sum_w):
        slab, col, chain, states, small = chunk_specs(at)
        return [
            (hid, slab, HBM), (cot, slab, HBM), (writer, square, HBM), (reads, square, HBM),
            (cols, col, HBM), (mixed_in, slab, HBM), (back_in, slab, HBM),
            (sum_c, square, HBM), (sum_w, square, HBM),
            (held_up, chain, HBM), (held_down, chain, HBM),
            (begin_here, states, HBM), (begin_there, states, HBM), (earlier, small, None),
        ]

    slab = chunk_specs(0)[0]
    mixed, grad_hidden, sum_c, sum_w = call(
        functools.partial(early_kernel, per_chunk, head_dim, vocab),
        (meta, skip_gain), (chunks - 1,),
        finish_ins(0, reader_in, writer_in) + [(value, anywhere, None) for value in waits[:1]],
        [
            ((length, width), BF16, slab, HBM), ((length, width), BF16, slab, HBM),
            ((length, state_dim), F32, square, HBM), ((length, state_dim), F32, square, HBM),
        ],
    )
    for step in sums:
        total = step(total)
    ins = finish_ins(chunks - 1, sum_c, sum_w) + [
        (got_up, whole(got_up.shape), None), (got_down, whole(got_down.shape), None),
        (mixed, anywhere, HBM), (grad_hidden, anywhere, HBM),
    ]
    slab = chunk_specs(chunks - 1)[0]
    mixed, grad_hidden, grad_cmat, grad_bmat = call(
        functools.partial(
            last_kernel, per_chunk, head_dim, vocab, bmat_scale,
            up_land + slots - 1, down_land + slots - 1, chunks - 1,
        ),
        (meta, skip_gain), (1,), ins,
        [
            ((length, width), BF16, slab, HBM), ((length, width), BF16, slab, HBM),
            ((length, state_dim), BF16, square, HBM), ((length, state_dim), BF16, square, HBM),
        ],
        [pltpu.VMEM((length, state_dim), F32)] * 2,
        aliases={len(ins): 0, len(ins) + 1: 1},
    )
    return (
        mixed.reshape(hidden.shape),
        grad_hidden.reshape(hidden.shape),
        grad_bmat.reshape(bmat.shape),
        grad_cmat.reshape(cmat.shape),
        total[:vocab, :],
        total[vocab, :heads],
    )


def solution(mesh):
    rows = P("rep", "dom", "ctx", None)
    return jax.shard_map(
        per_device,
        mesh=mesh,
        in_specs=(
            rows, rows, rows, P("rep", "dom", "ctx"), P(), rows, rows, P(),
            P("rep", "dom", "ctx", None, None), P("rep", "dom"), P("rep"), rows,
        ),
        out_specs=(rows, rows, rows, rows, P(), P()),
        check_vma=False,
    )
```

time: 394 us -> 156 us (0.40)
  waiting for transfers between devices: 234 us -> 50 us
  blocking collectives: 63.2 us -> 0 us
  starting transfers between devices: 0.21 us -> 46.5 us
  Pallas kernels: 0 us -> 41.7 us
  local copies, waits for them, and re-layouts: 28.8 us -> 1.18 us
  matrix products: 26.5 us -> 0 us
  other arithmetic: 24.6 us -> 0.03 us
    all_gather x5 -> x1, waiting for transfers between devices: 234 us -> 0.02 us  [per_device(): begin_here = lax.all_gather(own_state, 'ctx', tiled=True)]
    ppermute x0 -> x18, waiting for transfers between devices: none -> 50 us  [the longest x6 33.2 us: per_device(): got_down = lax.ppermute(send_down, 'ctx', downward)]
    ppermute x0 -> x18, starting transfers between devices: none -> 46.5 us  [the longest x6 31.6 us: per_device(): got_up = lax.ppermute(send_up, 'ctx', upward)]
    psum x1 -> x0, blocking collectives: 43.5 us -> none  [per_device(): lax.psum((table_part, skip_part), ('ctx', 'dom', 'rep'))]
    pallas_call x0 -> x15, Pallas kernels: none -> 41.7 us  [call(): pl.pallas_call(body, out_shape=[jax.ShapeDtypeStruct(shape, kind) if plac...]
    dot_general x21 -> x0, matrix products: 26.5 us -> none  [the longest x1 3.39 us: block_terms(): jnp.einsum('hts,thp->shp', weights, grad_rows, preferred_element_type=jnp...]
    all_gather x2 -> x0, blocking collectives: 19.7 us -> none  [the longest x1 10.2 us: per_device(): shard_part = lax.all_gather(prev_state, 'dom', axis=1, tiled=True)]
    select_n x12 -> x1, other arithmetic: 17.7 us -> 0.01 us  [per_device(): table_of.append(jnp.where((lands >= 0) & (lands < chunks), lands, chunks))]
  transfers between devices with their start and end apart: 5 -> 19, of which waited for: 5 -> 11; matrix products, arithmetic and copies ran while one was open for 17% -> 1% of each run, Pallas kernels for 0% -> 22%
where the time goes in v1:
time: 156 us; the launch traced here: 155 us
  waiting for transfers between devices  50 us (32%)
  starting transfers between devices  46.5 us (30%)
  Pallas kernels  41.7 us (27%)
  between operations  15.6 us (10%)
    pallas_call x15, Pallas kernels, call(): pl.pallas_call(body, out_shape=[jax.ShapeDtypeStruct(shape, kind) if plac...  41.7 us
    ppermute x6, waiting for transfers between devices, per_device(): got_down = lax.ppermute(send_down, 'ctx', downward)  33.2 us
    ppermute x6, starting transfers between devices, per_device(): got_up = lax.ppermute(send_up, 'ctx', upward)  31.6 us
    ppermute x5, waiting for transfers between devices, sum_steps(): lax.ppermute(value, axis, swap)  13.4 us
    ppermute x6, starting transfers between devices, per_device(): got_down = lax.ppermute(send_down, 'ctx', downward)  7.75 us
    ppermute x5, starting transfers between devices, sum_steps(): lax.ppermute(value, axis, swap)  5.55 us
    ppermute x6, waiting for transfers between devices, per_device(): got_up = lax.ppermute(send_up, 'ctx', upward)  3.38 us
  transfers between devices with their start and end apart: 19, of which 11 were waited for; matrix products, arithmetic and copies ran while one was open for 1% of the time, Pallas kernels for 22%

profile of v1, /device:TPU:0, one launch (start us, length us, event | category | flops | bytes accessed | tf_op | source)
XLA Modules:
  0.0 155.0 jit_solution(10490341944247926350)
XLA Ops:
  8.6 4.6 %shard_map.163 = (f32[288,512]{1,0:T(8,128)S(1)}, f32[288,512]{1,0:T(8,128)S(1)}, f32[4,8,512]{2,1,0:T(8,128)S(1)}, f32[4,8,512]{2,1,0:T(8,128)S(1)}, f32[4,128,128]{2,1,0:T(8,128)}, /*index=5*/bf16[128,128]{1,0:T(8,128)(2,1)}) custom-call(s32[28]{0:T(128)S(1)} %concatenate.3.meta.refs_0_, bf16[128,128]{1,0:T(8,128)(2,1)} %bitcast.39, ...), custom_call_target="tpu_custom_call" | custom-call | tf_op jit(solution)/shard_map/pallas_call | solution.py:337
  14.6 5.6 %collective-permute-start = (f32[288,512]{1,0:T(8,128)S(1)}, f32[288,512]{1,0:T(8,128)S(1)}, u32[]{:S(2)}, u32[]{:S(2)}) collective-permute-start(f32[288,512]{1,0:T(8,128)S(1)} %get-tuple-element.53), channel_id=1, source_target_pairs={{0,8},{8,16},{16,24},{1,9},{9,17},{17,25},{2,10},{10,18},{18,26},{... | collective-permute-start | bytes 1769480 | tf_op jit(solution)/shard_map/ppermute | solution.py:519
  20.2 7.2 %shard_map.164 = (f32[4,2,128,512]{3,2,1,0:T(8,128)}, f32[4,2,128,512]{3,2,1,0:T(8,128)}, f32[128,2048]{1,0:T(8,128)}, f32[128,2048]{1,0:T(8,128)}, f32[128,128]...) custom-call(s32[28]{0:T(128)S(1)} %concatenate.3.meta.refs_0_, bf16[128,2048]{1,0:T(8,128)(2,1)} %bitcast.25, ...), custom_call_target="tpu_custom_call" | custom-call | tf_op jit(solution)/shard_map/pallas_call | solution.py:337
  27.3 4.6 %collective-permute-done.4.refs_1_ = f32[288,512]{1,0:T(8,128)S(1)} collective-permute-done((f32[288,512]{1,0:T(8,128)S(1)}, f32[288,512]{1,0:T(8,128)S(1)}, u32[]{:S(2)}, u32[]{:S(2)}) %collective-permute-start.4) | collective-permute-done | bytes 589856 | tf_op jit(solution)/shard_map/ppermute | solution.py:520
  32.0 1.7 %shard_map.168 = (f32[288,512]{1,0:T(8,128)S(1)}, bf16[5,256,512]{2,1,0:T(8,128)(2,1)}) custom-call(s32[28]{0:T(128)S(1)} %concatenate.3.meta.refs_0_, f32[288,512]{1,0:T(8,128)S(1)} %collective-permute-done.4.refs_1_, f32[4,2,128,512]{3,2,1,0:T(8,128)} %get-tuple-element.64.refs_2_.grad_down, f32[4,8,512]{2,1,0:T(8,128)S(1)} %get-tuple-element.56.refs_4_.refs_3_.small, ...), custom_call_target="tpu_custom_call" | custom-call | tf_op jit(solution)/shard_map/pallas_call | solution.py:337
  35.0 2.4 %collective-permute-done.refs_1_ = f32[288,512]{1,0:T(8,128)S(1)} collective-permute-done((f32[288,512]{1,0:T(8,128)S(1)}, f32[288,512]{1,0:T(8,128)S(1)}, u32[]{:S(2)}, u32[]{:S(2)}) %collective-permute-start) | collective-permute-done | bytes 589856 | tf_op jit(solution)/shard_map/ppermute | solution.py:519
  39.1 7.9 %collective-permute-start.1 = (f32[288,512]{1,0:T(8,128)S(1)}, f32[288,512]{1,0:T(8,128)S(1)}, u32[]{:S(2)}, u32[]{:S(2)}) collective-permute-start(f32[288,512]{1,0:T(8,128)S(1)} %get-tuple-element.57), channel_id=1, source_target_pairs={{0,8},{8,16},{16,24},{1,9},{9,17},{17,25},{2,10},{10,18},{18,26},{... | collective-permute-start | bytes 1769480 | tf_op jit(solution)/shard_map/ppermute | solution.py:519
  47.0 14.0 %collective-permute-done.5.refs_1_ = f32[288,512]{1,0:T(8,128)S(1)} collective-permute-done((f32[288,512]{1,0:T(8,128)S(1)}, f32[288,512]{1,0:T(8,128)S(1)}, u32[]{:S(2)}, u32[]{:S(2)}) %collective-permute-start.5) | collective-permute-done | bytes 589856 | tf_op jit(solution)/shard_map/ppermute | solution.py:520
  64.0 1.7 %shard_map.166 = (f32[288,512]{1,0:T(8,128)S(1)}, bf16[5,256,512]{2,1,0:T(8,128)(2,1)}) custom-call(s32[28]{0:T(128)S(1)} %concatenate.3.meta.refs_0_, f32[288,512]{1,0:T(8,128)S(1)} %collective-permute-done.1.refs_1_, f32[4,2,128,512]{3,2,1,0:T(8,128)} %get-tuple-element.54.refs_2_.grad_up, ...), custom_call_target="tpu_custom_call", output_to_operand_aliasing={{1}: (5, {})} | custom-call | tf_op jit(solution)/shard_map/pallas_call | solution.py:337
  65.8 4.6 %collective-permute-start.2 = (f32[288,512]{1,0:T(8,128)S(1)}, f32[288,512]{1,0:T(8,128)S(1)}, u32[]{:S(2)}, u32[]{:S(2)}) collective-permute-start(f32[288,512]{1,0:T(8,128)S(1)} %get-tuple-element.59), channel_id=1, source_target_pairs={{0,8},{8,16},{16,24},{1,9},{9,17},{17,25},{2,10},{10,18},{18,26},{... | collective-permute-start | bytes 1769480 | tf_op jit(solution)/shard_map/ppermute | solution.py:519
  70.4 9.2 %collective-permute-done.6.later.refs_1_ = f32[288,512]{1,0:T(8,128)S(1)} collective-permute-done((f32[288,512]{1,0:T(8,128)S(1)}, f32[288,512]{1,0:T(8,128)S(1)}, u32[]{:S(2)}, u32[]{:S(2)}) %collective-permute-start.6) | collective-permute-done | bytes 589856 | tf_op jit(solution)/shard_map/ppermute | solution.py:520
  82.6 1.7 %shard_map.167 = (f32[256,512]{1,0:T(8,128)S(1)}, bf16[5,256,512]{2,1,0:T(8,128)(2,1)}) custom-call(s32[28]{0:T(128)S(1)} %concatenate.3.meta.refs_0_, f32[288,512]{1,0:T(8,128)S(1)} %collective-permute-done.2.refs_1_.earlier, f32[4,2,128,512]{3,2,1,0:T(8,128)} %get-tuple-element.54.refs_2_.grad_up, ...), custom_call_target="tpu_custom_call", output_to_operand_aliasing={{1}: (5, {})} | custom-call | tf_op jit(solution)/shard_map/pallas_call | solution.py:337
  84.4 4.6 %collective-permute-start.3 = (f32[256,512]{1,0:T(8,128)S(1)}, f32[256,512]{1,0:T(8,128)S(1)}, u32[]{:S(2)}, u32[]{:S(2)}) collective-permute-start(f32[256,512]{1,0:T(8,128)S(1)} %get-tuple-element.61), channel_id=1, source_target_pairs={{0,8},{8,16},{16,24},{1,9},{9,17},{17,25},{2,10},{10,18},{18,26},{... | collective-permute-start | bytes 1572872 | tf_op jit(solution)/shard_map/ppermute | solution.py:519
  90.5 5.3 %collective-permute-done.11.refs_1_ = f32[256,512]{1,0:T(8,128)S(1)} collective-permute-done((f32[256,512]{1,0:T(8,128)S(1)}, f32[256,512]{1,0:T(8,128)S(1)}, u32[]{:S(2)}, u32[]{:S(2)}) %collective-permute-start.11) | collective-permute-done | bytes 524320 | tf_op jit(solution)/shard_map/ppermute | solution.py:520
  98.8 3.3 %shard_map.170.refs_6_ = f32[8,128]{1,0:T(8,128)S(1)} custom-call(s32[28]{0:T(128)S(1)} %concatenate.3.meta.refs_0_, f32[288,512]{1,0:T(8,128)S(1)} %collective-permute-done.2.refs_1_.earlier, f32[288,512]{1,0:T(8,128)S(1)} %collective-permute-done.6.later.refs_1_, f32[4,8,512]{2,1,0:T(8,128)S(1)} %get-tuple-element.56.refs_4_.refs_3_.small, ...), custom_call_target="tpu_custom_call" | custom-call | tf_op jit(solution)/shard_map/pallas_call | solution.py:337
  102.2 1.7 %shard_map.171 = (f32[256,512]{1,0:T(8,128)S(1)}, bf16[5,256,512]{2,1,0:T(8,128)(2,1)}) custom-call(s32[28]{0:T(128)S(1)} %concatenate.3.meta.refs_0_, f32[256,512]{1,0:T(8,128)S(1)} %collective-permute-done.3.refs_1_, f32[4,2,128,512]{3,2,1,0:T(8,128)} %get-tuple-element.54.refs_2_.grad_up, ...), custom_call_target="tpu_custom_call", output_to_operand_aliasing={{1}: (5, {})} | custom-call | tf_op jit(solution)/shard_map/pallas_call | solution.py:337
  103.9 4.6 %collective-permute-start.7 = (f32[256,512]{1,0:T(8,128)S(1)}, f32[256,512]{1,0:T(8,128)S(1)}, u32[]{:S(2)}, u32[]{:S(2)}) collective-permute-start(f32[256,512]{1,0:T(8,128)S(1)} %get-tuple-element.69), channel_id=1, source_target_pairs={{0,8},{8,16},{16,24},{1,9},{9,17},{17,25},{2,10},{10,18},{18,26},{... | collective-permute-start | bytes 1572872 | tf_op jit(solution)/shard_map/ppermute | solution.py:519
  111.0 2.3 %collective-permute-done.9 = f32[8,128]{1,0:T(8,128)S(1)} collective-permute-done((f32[8,128]{1,0:T(8,128)S(1)}, f32[8,128]{1,0:T(8,128)S(1)}, u32[]{:S(2)}, u32[]{:S(2)}) %collective-permute-start.9) | collective-permute-done | bytes 4128 | tf_op jit(solution)/shard_map/ppermute | solution.py:373
  119.1 4.4 %collective-permute-start.15 = (f32[256,512]{1,0:T(8,128)S(1)}, f32[256,512]{1,0:T(8,128)S(1)}, u32[]{:S(2)}, u32[]{:S(2)}) collective-permute-start(f32[256,512]{1,0:T(8,128)S(1)} %get-tuple-element.80), channel_id=1, source_target_pairs={{0,8},{8,16},{16,24},{1,9},{9,17},{17,25},{2,10},{10,18},{18,26},{... | collective-permute-start | bytes 1572872 | tf_op jit(solution)/shard_map/ppermute | solution.py:519
  124.7 2.5 %collective-permute-done.13 = f32[8,128]{1,0:T(8,128)S(1)} collective-permute-done((f32[8,128]{1,0:T(8,128)S(1)}, f32[8,128]{1,0:T(8,128)S(1)}, u32[]{:S(2)}, u32[]{:S(2)}) %collective-permute-start.13) | collective-permute-done | bytes 4128 | tf_op jit(solution)/shard_map/ppermute | solution.py:373
  128.7 4.5 %collective-permute-done.14 = f32[8,128]{1,0:T(8,128)S(1)} collective-permute-done((f32[8,128]{1,0:T(8,128)S(1)}, f32[8,128]{1,0:T(8,128)S(1)}, u32[]{:S(2)}, u32[]{:S(2)}) %collective-permute-start.14) | collective-permute-done | bytes 4128 | tf_op jit(solution)/shard_map/ppermute | solution.py:373
  134.7 3.0 %collective-permute-done.17 = f32[8,128]{1,0:T(8,128)S(1)} collective-permute-done((f32[8,128]{1,0:T(8,128)S(1)}, f32[8,128]{1,0:T(8,128)S(1)}, u32[]{:S(2)}, u32[]{:S(2)}) %collective-permute-start.17) | collective-permute-done | bytes 4128 | tf_op jit(solution)/shard_map/ppermute | solution.py:373
  138.8 5.9 %shard_map.176 = (bf16[128,2048]{1,0:T(8,128)(2,1)}, bf16[128,2048]{1,0:T(8,128)(2,1)}, f32[128,128]{1,0:T(8,128)}, f32[128,128]{1,0:T(8,128)}) custom-call(s32[28]{0:T(128)S(1)} %concatenate.3.meta.refs_0_, f32[16]{0:T(128)S(1)} %copy-done.1, bf16[128,2048]{1,0:T(8,128)(2,1)} %bitcast.26, bf16[128,2048]{1,0:T(8,128)(2,1)} %bitcast.30, ...), custom_call_target="tpu_custom_call" | custom-call | tf_op jit(solution)/shard_map/pallas_call | solution.py:337
  144.7 3.5 %shard_map.177 = (bf16[128,2048]{1,0:T(8,128)(2,1)}, bf16[128,2048]{1,0:T(8,128)(2,1)}, bf16[128,128]{1,0:T(8,128)(2,1)}, bf16[128,128]{1,0:T(8,128)(2,1)}) custom-call(s32[28]{0:T(128)S(1)} %concatenate.3.meta.refs_0_, f32[16]{0:T(128)S(1)} %copy-done.1, bf16[128,2048]{1,0:T(8,128)(2,1)} %bitcast.27, ...), custom_call_target="tpu_custom_call", output_to_operand_aliasing={{0}: (18, {}), {1}: (19, {})} | custom-call | tf_op jit(solution)/shard_map/pallas_call | solution.py:337
  (44 shorter events, 28.6 us)
Async XLA Ops:
  7.2 75.4 %all-gather.3.cloned.1.call-start = ((), (), s32[]{:S(2)}) async-start(), calls=%async_computation | async-start | bytes 1310720 | tf_op jit(solution)/shard_map/all_gather | solution.py:424
  13.3 18.7 %collective-permute-start.4 = (f32[288,512]{1,0:T(8,128)S(1)}, f32[288,512]{1,0:T(8,128)S(1)}, u32[]{:S(2)}, u32[]{:S(2)}) collective-permute-start(f32[288,512]{1,0:T(8,128)S(1)} %get-tuple-element.63), channel_id=1, source_target_pairs={{8,0},{16,8},{24,16},{9,1},{17,9},{25,17},{10,2},{18,10},{26,18},{... | collective-permute-start | bytes 1769480 | tf_op jit(solution)/shard_map/ppermute | solution.py:520
  14.6 22.8 %collective-permute-start = (f32[288,512]{1,0:T(8,128)S(1)}, f32[288,512]{1,0:T(8,128)S(1)}, u32[]{:S(2)}, u32[]{:S(2)}) collective-permute-start(f32[288,512]{1,0:T(8,128)S(1)} %get-tuple-element.53), channel_id=1, source_target_pairs={{0,8},{8,16},{16,24},{1,9},{9,17},{17,25},{2,10},{10,18},{18,26},{... | collective-permute-start | bytes 1769480 | tf_op jit(solution)/shard_map/ppermute | solution.py:519
  33.7 27.3 %collective-permute-start.5 = (f32[288,512]{1,0:T(8,128)S(1)}, f32[288,512]{1,0:T(8,128)S(1)}, u32[]{:S(2)}, u32[]{:S(2)}) collective-permute-start(f32[288,512]{1,0:T(8,128)S(1)} %get-tuple-element.65), channel_id=1, source_target_pairs={{8,0},{16,8},{24,16},{9,1},{17,9},{25,17},{10,2},{18,10},{26,18},{... | collective-permute-start | bytes 1769480 | tf_op jit(solution)/shard_map/ppermute | solution.py:520
  39.1 24.9 %collective-permute-start.1 = (f32[288,512]{1,0:T(8,128)S(1)}, f32[288,512]{1,0:T(8,128)S(1)}, u32[]{:S(2)}, u32[]{:S(2)}) collective-permute-start(f32[288,512]{1,0:T(8,128)S(1)} %get-tuple-element.57), channel_id=1, source_target_pairs={{0,8},{8,16},{16,24},{1,9},{9,17},{17,25},{2,10},{10,18},{18,26},{... | collective-permute-start | bytes 1769480 | tf_op jit(solution)/shard_map/ppermute | solution.py:519
  62.7 16.8 %collective-permute-start.6 = (f32[288,512]{1,0:T(8,128)S(1)}, f32[288,512]{1,0:T(8,128)S(1)}, u32[]{:S(2)}, u32[]{:S(2)}) collective-permute-start(f32[288,512]{1,0:T(8,128)S(1)} %get-tuple-element.67), channel_id=1, source_target_pairs={{8,0},{16,8},{24,16},{9,1},{17,9},{25,17},{10,2},{18,10},{26,18},{... | collective-permute-start | bytes 1769480 | tf_op jit(solution)/shard_map/ppermute | solution.py:520
  65.8 16.8 %collective-permute-start.2 = (f32[288,512]{1,0:T(8,128)S(1)}, f32[288,512]{1,0:T(8,128)S(1)}, u32[]{:S(2)}, u32[]{:S(2)}) collective-permute-start(f32[288,512]{1,0:T(8,128)S(1)} %get-tuple-element.59), channel_id=1, source_target_pairs={{0,8},{8,16},{16,24},{1,9},{9,17},{17,25},{2,10},{10,18},{18,26},{... | collective-permute-start | bytes 1769480 | tf_op jit(solution)/shard_map/ppermute | solution.py:519
  81.3 14.5 %collective-permute-start.11 = (f32[256,512]{1,0:T(8,128)S(1)}, f32[256,512]{1,0:T(8,128)S(1)}, u32[]{:S(2)}, u32[]{:S(2)}) collective-permute-start(f32[256,512]{1,0:T(8,128)S(1)} %get-tuple-element.73), channel_id=1, source_target_pairs={{8,0},{16,8},{24,16},{9,1},{17,9},{25,17},{10,2},{18,10},{26,18},{... | collective-permute-start | bytes 1572872 | tf_op jit(solution)/shard_map/ppermute | solution.py:520
  84.4 17.8 %collective-permute-start.3 = (f32[256,512]{1,0:T(8,128)S(1)}, f32[256,512]{1,0:T(8,128)S(1)}, u32[]{:S(2)}, u32[]{:S(2)}) collective-permute-start(f32[256,512]{1,0:T(8,128)S(1)} %get-tuple-element.61), channel_id=1, source_target_pairs={{0,8},{8,16},{16,24},{1,9},{9,17},{17,25},{2,10},{10,18},{18,26},{... | collective-permute-start | bytes 1572872 | tf_op jit(solution)/shard_map/ppermute | solution.py:519
  88.9 27.4 %collective-permute-start.10 = (f32[16,128,128]{2,1,0:T(8,128)}, f32[16,128,128]{2,1,0:T(8,128)S(1)}, u32[]{:S(2)}, u32[]{:S(2)}) collective-permute-start(f32[16,128,128]{2,1,0:T(8,128)} %bitcast.14.refs_6_.begin_here), channel_id=1, source_target_pairs={{0,4},{4,0},{1,5},{5,1},{2,6},{6,2},{3,7},{7,3},{8,12},{12,8},{9,1... | collective-permute-start | bytes 3145736 | tf_op jit(solution)/shard_map/ppermute | solution.py:527
  97.5 15.8 %collective-permute-start.12 = (f32[256,512]{1,0:T(8,128)S(1)}, f32[256,512]{1,0:T(8,128)S(1)}, u32[]{:S(2)}, u32[]{:S(2)}) collective-permute-start(f32[256,512]{1,0:T(8,128)S(1)} %get-tuple-element.75), channel_id=1, source_target_pairs={{8,0},{16,8},{24,16},{9,1},{17,9},{25,17},{10,2},{18,10},{26,18},{... | collective-permute-start | bytes 1572872 | tf_op jit(solution)/shard_map/ppermute | solution.py:520
  103.9 13.5 %collective-permute-start.7 = (f32[256,512]{1,0:T(8,128)S(1)}, f32[256,512]{1,0:T(8,128)S(1)}, u32[]{:S(2)}, u32[]{:S(2)}) collective-permute-start(f32[256,512]{1,0:T(8,128)S(1)} %get-tuple-element.69), channel_id=1, source_target_pairs={{0,8},{8,16},{16,24},{1,9},{9,17},{17,25},{2,10},{10,18},{18,26},{... | collective-permute-start | bytes 1572872 | tf_op jit(solution)/shard_map/ppermute | solution.py:519
  108.5 1.2 collective-permute-start.8
  109.7 3.6 %collective-permute-start.9 = (f32[8,128]{1,0:T(8,128)S(1)}, f32[8,128]{1,0:T(8,128)S(1)}, u32[]{:S(2)}, u32[]{:S(2)}) collective-permute-start(f32[8,128]{1,0:T(8,128)S(1)} %add.30), channel_id=1, source_target_pairs={{0,2},{1,3},{2,0},{3,1},{4,6},{5,7},{6,4},{7,5},{8,10},{9,11},{10,... | collective-permute-start | bytes 12296 | tf_op jit(solution)/shard_map/ppermute | solution.py:373
  115.1 29.6 %collective-permute-start.16 = (f32[256,512]{1,0:T(8,128)S(1)}, f32[256,512]{1,0:T(8,128)S(1)}, u32[]{:S(2)}, u32[]{:S(2)}) collective-permute-start(f32[256,512]{1,0:T(8,128)S(1)} %get-tuple-element.81), channel_id=1, source_target_pairs={{8,0},{16,8},{24,16},{9,1},{17,9},{25,17},{10,2},{18,10},{26,18},{... | collective-permute-start | bytes 1572872 | tf_op jit(solution)/shard_map/ppermute | solution.py:520
  116.4 2.7 %copy-start = (f32[16,128,128]{2,1,0:T(8,128)}, f32[16,128,128]{2,1,0:T(8,128)S(1)}, u32[]{:S(2)}) copy-start(f32[16,128,128]{2,1,0:T(8,128)S(1)} %collective-permute-done.10.refs_7_.begin_there) | copy-start | bytes 3145732
  117.4 21.4 %copy-start.1 = (f32[16]{0:T(128)S(1)}, f32[16]{0:T(128)}, u32[]{:S(2)}) copy-start(f32[16]{0:T(128)} %gains.3) | copy-start | bytes 196
  119.1 25.6 %collective-permute-start.15 = (f32[256,512]{1,0:T(8,128)S(1)}, f32[256,512]{1,0:T(8,128)S(1)}, u32[]{:S(2)}, u32[]{:S(2)}) collective-permute-start(f32[256,512]{1,0:T(8,128)S(1)} %get-tuple-element.80), channel_id=1, source_target_pairs={{0,8},{8,16},{16,24},{1,9},{9,17},{17,25},{2,10},{10,18},{18,26},{... | collective-permute-start | bytes 1572872 | tf_op jit(solution)/shard_map/ppermute | solution.py:519
  123.6 3.7 %collective-permute-start.13 = (f32[8,128]{1,0:T(8,128)S(1)}, f32[8,128]{1,0:T(8,128)S(1)}, u32[]{:S(2)}, u32[]{:S(2)}) collective-permute-start(f32[8,128]{1,0:T(8,128)S(1)} %add.31.refs_6_), channel_id=1, source_target_pairs={{0,4},{4,0},{1,5},{5,1},{2,6},{6,2},{3,7},{7,3},{8,12},{12,8},{9,1... | collective-permute-start | bytes 12296 | tf_op jit(solution)/shard_map/ppermute | solution.py:373
  127.3 5.9 %collective-permute-start.14 = (f32[8,128]{1,0:T(8,128)S(1)}, f32[8,128]{1,0:T(8,128)S(1)}, u32[]{:S(2)}, u32[]{:S(2)}) collective-permute-start(f32[8,128]{1,0:T(8,128)S(1)} %add.32), channel_id=1, source_target_pairs={{0,8},{8,0},{16,24},{24,16},{1,9},{9,1},{17,25},{25,17},{2,10},{10... | collective-permute-start | bytes 12296 | tf_op jit(solution)/shard_map/ppermute | solution.py:373
  133.2 4.5 %collective-permute-start.17 = (f32[8,128]{1,0:T(8,128)S(1)}, f32[8,128]{1,0:T(8,128)S(1)}, u32[]{:S(2)}, u32[]{:S(2)}) collective-permute-start(f32[8,128]{1,0:T(8,128)S(1)} %add.33.refs_0_), channel_id=1, source_target_pairs={{0,16},{8,24},{16,0},{24,8},{1,17},{9,25},{17,1},{25,9},{2,18},{10... | collective-permute-start | bytes 12296 | tf_op jit(solution)/shard_map/ppermute | solution.py:373
Sparse Core Ops, SparseCore 0:
  20.3 36.0 all-gather.2

commit v2 on v1

--- a/solution.py
+++ b/solution.py
@@ -122,21 +122,75 @@
             down_first[state : 2 * state, :] = dot(reader_t, jnp.concatenate(grad_risen, axis=1))
 
 
-def combine_kernel(vocab, has_small, land, source, waits, *refs):
+def head_copies(source, target, row, sems):
+    heads, rows, width = source.shape
+    return [
+        pltpu.make_async_copy(
+            source.at[head],
+            target.at[pl.ds(row, rows), pl.ds(head * width, width)],
+            sems.at[head],
+        )
+        for head in range(heads)
+    ]
+
+
+def relay_kernel(last, meta, from_before, from_after, up_old, down_old, up, down, sems):
+    del up_old, down_old
+    for at, (source, target) in enumerate(((from_before, up), (from_after, down))):
+        copies = head_copies(source, target, 0, sems.at[at])
+
+        @pl.when(meta[2] != (0, last)[at])
+        def _():
+            for copy in copies:
+                copy.start()
+            for copy in copies:
+                copy.wait()
+
+
+def gather_kernel(last, meta, own, from_before, from_after, begin, sems):
+    place = meta[2]
+    trash = last + 1
+    copies = []
+    for at, (source, row) in enumerate((
+        (own, place),
+        (from_before, jnp.where(place == 0, trash, place - 1)),
+        (from_after, place + 1),
+    )):
+        copies += head_copies(source, begin.at[row], 0, sems.at[at])
+    for copy in copies:
+        copy.start()
+    for copy in copies:
+        copy.wait()
+
+
+def combine_kernel(vocab, has_small, has_begin, slot, tables, waits, *refs):
     meta, received, own, small, decays = refs[:5]
-    send, held, near, rounded, sems = refs[-5:]
+    near, rounded, sems = refs[-3:]
+    send, held = refs[-6:-4] if has_begin else refs[-5:-3]
     del waits
     state = own.shape[2]
+    land, source, forward, piece = (at + slot for at in tables)
     fetch = [
         pltpu.make_async_copy(own.at[meta[source], at], near.at[at], sems.at[at])
         for at in range(2)
     ]
     for copy in fetch:
         copy.start()
+    stores = []
+    if has_begin:
+        begin = refs[-4]
+        stores.append(
+            pltpu.make_async_copy(
+                received.at[0:state, 0 : begin.shape[2]], begin.at[meta[piece]], sems.at[3]
+            )
+        )
+        stores[-1].start()
     rounded[...] = received[0 : 2 * state, :].astype(BF16)
-    store = pltpu.make_async_copy(rounded, held.at[meta[land]], sems.at[2])
-    store.start()
-    decay = decays[meta[source], vocab : vocab + 1, :]
+    stores.append(pltpu.make_async_copy(rounded, held.at[meta[land]], sems.at[2]))
+    stores[-1].start()
+    passing = meta[forward] != 0
+    decay = jnp.where(passing, 1.0, decays[meta[source], vocab : vocab + 1, :])
+    adding = jnp.where(passing, 0.0, 1.0)
     if has_small:
         lines = small.shape[1]
         for at in range(small.shape[0]):
@@ -145,8 +199,9 @@
     for at in range(2):
         fetch[at].wait()
         rows = slice(at * state, (at + 1) * state)
-        send[rows, :] = decay * received[rows, :] + near[at]
-    store.wait()
+        send[rows, :] = decay * received[rows, :] + adding * near[at]
+    for store in stores:
+        store.wait()
 
 
 def inner_kernel(
@@ -247,13 +302,12 @@
     length = hid.shape[0]
     state = chain_in.shape[0] // 2
     live = live_rows(meta, (length, head_dim))
-    begins = jnp.concatenate(
-        [
-            jnp.where(meta[3] != 0, begin_here[at], begin_there[at]).T
-            for at in range(per_chunk)
-        ],
-        axis=1,
-    )
+    begins = []
+    for at in range(begin_here.shape[0]):
+        value = jnp.where(meta[3] != 0, begin_here[at], begin_there[at])
+        for lane in range(0, value.shape[1], state):
+            begins.append(value[:, lane : lane + state].T)
+    begins = jnp.concatenate(begins, axis=1)
     passed = jnp.where(meta[2] == 0, 1.0, earlier[vocab : vocab + 1, :])
     state_in = (chain_in[0:state].astype(F32) + passed * begins).astype(BF16)
     grad_in = chain_in[state:]
@@ -294,7 +348,7 @@
     meta, gains, hid, cot, writer, cmat, cols, mixed_in, back_in, reader_in, writer_in,
     held_up, held_down, begin_here, begin_there, earlier, *refs,
 ):
-    mixed, grad_hidden, acc_c, acc_w = refs[-4:]
+    mixed, grad_hidden, acc_c, acc_w = refs[-5:-1]
     chunk = pl.program_id(0)
 
     @pl.when(chunk == 0)
@@ -312,10 +366,16 @@
 def last_kernel(
     per_chunk, head_dim, vocab, bmat_scale, up_land, down_land, chunk,
     meta, gains, hid, cot, writer, cmat, cols, mixed_in, back_in, sum_c, sum_w,
-    held_up, held_down, begin_here, begin_there, earlier, got_up, got_down, mixed_old, hidden_old,
-    mixed, grad_hidden, grad_cmat, grad_bmat, acc_c, acc_w,
+    held_up, held_down, begin_here, begin_there, earlier, got_up, got_down, *refs,
 ):
-    del mixed_old, hidden_old
+    sums = refs[2:-8]
+    mixed, grad_hidden, grad_cmat, grad_bmat, grad_table, grad_skip, acc_c, acc_w = refs[-8:]
+    total = sums[0][...]
+    for value in sums[1:]:
+        total = total + value[...]
+    vocab_rows, heads = grad_table.shape[0], grad_skip.shape[1]
+    grad_table[...] = total[0:vocab_rows, :]
+    grad_skip[...] = total[vocab_rows : vocab_rows + 1, 0:heads]
     acc_c[...] = sum_c[...]
     acc_w[...] = sum_w[...]
     chain_in = jnp.where(meta[up_land] == chunk, got_up[...].astype(BF16), held_up[0])
@@ -360,20 +420,29 @@
 
 
 def sum_steps(axes):
-    steps = []
+    steps, last = [], []
     for axis in axes:
         count = lax.axis_size(axis)
         if count & (count - 1):
-            steps.append(lambda value, axis=axis: lax.psum(value, axis))
+            steps.append(functools.partial(lax.psum, axis_name=axis))
             continue
         hop = 1
         while hop < count:
-            swap = [(at, at ^ hop) for at in range(count)]
-            steps.append(
-                lambda value, axis=axis, swap=swap: value + lax.ppermute(value, axis, swap)
-            )
+            hops = [hop]
+            if axis == axes[-1] and 4 * hop >= count:
+                hops = range(hop, count, hop)
+            group = [
+                functools.partial(
+                    lax.ppermute, axis_name=axis, perm=[(at, at ^ far) for at in range(count)]
+                )
+                for far in hops
+            ]
+            if axis == axes[-1] and 4 * hop >= count:
+                last = group
+                break
+            steps.append(lambda value, group=group: value + group[0](value))
             hop *= 2
-    return steps
+    return steps, last
 
 
 def per_device(
@@ -411,22 +480,29 @@
     times = jnp.arange(slots, dtype=jnp.int32)
     from_last = count - 1 - place
     table_of = []
-    for far in (place, from_last):
+    for far, toward in ((place, -1), (from_last, 1)):
         lands = times - jnp.maximum(far, 1) + 1
+        pieces = place + toward * (times + 2)
         table_of.append(jnp.where((lands >= 0) & (lands < chunks), lands, chunks))
         table_of.append(jnp.clip(times + 1 - far, 0, chunks - 1))
+        table_of.append((times + 1 < far).astype(jnp.int32))
+        table_of.append(jnp.where((pieces >= 0) & (pieces < count), pieces, count))
     base = jnp.stack([place * length, suffix_start[0], place, here]).astype(jnp.int32)
     meta = jnp.concatenate([base] + table_of)
-    up_land, up_source, down_land, down_source = (4 + at * slots for at in range(4))
-
+    up_tables = [4 + at * slots for at in range(4)]
+    down_tables = [4 + at * slots for at in range(4, 8)]
+
+    upward = [(at, at + 1) for at in range(count - 1)]
+    downward = [(at + 1, at) for at in range(count - 1)]
     own_state = prev_state[0, 0]
-    if doms == 2:
-        begin_here = lax.all_gather(own_state, "ctx", tiled=True)
-    else:
+    local_heads = own_state.shape[0]
+    assert per_chunk % local_heads == 0
+    if doms != 2:
         own_state = lax.dynamic_index_in_dim(
             lax.all_gather(own_state, "dom"), ancestor, 0, keepdims=False
         )
-        begin_here = lax.all_gather(own_state, "ctx", tiled=True)
+    from_before = lax.ppermute(own_state, "ctx", upward)
+    from_after = lax.ppermute(own_state, "ctx", downward)
 
     anywhere = pl.BlockSpec(memory_space=pl.ANY)
     near = pl.BlockSpec(memory_space=pltpu.VMEM)
@@ -461,6 +537,31 @@
         ],
     )
 
+    up_first, down_first = call(
+        functools.partial(relay_kernel, count - 1),
+        (meta,), (),
+        [
+            (from_before, anywhere, None), (from_after, anywhere, None),
+            (up_first, near, CHIP), (down_first, near, CHIP),
+        ],
+        [
+            ((full_rows, part), F32, near, CHIP), ((full_rows, part), F32, near, CHIP),
+        ],
+        [pltpu.SemaphoreType.DMA((2, local_heads))],
+        aliases={3: 0, 4: 1},
+    )
+    begin_shape = (count + 1, head_dim, local_heads * state_dim)
+    (begin_here,) = call(
+        functools.partial(gather_kernel, count - 1),
+        (meta,), (),
+        [
+            (own_state, anywhere, None), (from_before, anywhere, None),
+            (from_after, anywhere, None),
+        ],
+        [(begin_shape, F32, anywhere, HBM)],
+        [pltpu.SemaphoreType.DMA((3, local_heads))],
+    )
+
     up, down, mixed_in, back_in, reader_in, writer_in, tab = call(
         functools.partial(inner_kernel, per_chunk, head_dim, vocab),
         (meta,), (chunks,),
@@ -480,49 +581,54 @@
         [pltpu.VMEM((length, length), F32)] * 3 + [pltpu.VMEM((state_dim, length), BF16)] * 2,
     )
 
-    def step_chain(slot, received, own, small, land, source, held, waits):
+    def step_chain(slot, received, own, small, tables, held, begin, waits):
         has_small = slot < count - 2
+        has_begin = slot < count - 2
         rows = full_rows if has_small else 2 * state_dim
         held_shape = (chunks + 1, 2 * state_dim, part)
         ins = [
             (received, near, CHIP), (own, anywhere, HBM), (small, near, CHIP),
             (down_small, near, CHIP),
         ]
+        outs = [((rows, part), F32, near, CHIP), (held_shape, BF16, anywhere, HBM)]
         aliases = {}
         if held is not None:
-            aliases = {1 + len(ins): 1}
+            aliases[1 + len(ins)] = 1
             ins.append((held, anywhere, HBM))
+        if has_begin:
+            aliases[1 + len(ins)] = 2
+            ins.append((begin, anywhere, HBM))
+            outs.append((begin_shape, F32, anywhere, HBM))
         ins += [(value, anywhere, None) for value in waits]
-        return call(
+        results = call(
             functools.partial(
-                combine_kernel, vocab, has_small, land + slot, source + slot, len(waits)
+                combine_kernel, vocab, has_small, has_begin, slot, tables, len(waits)
             ),
-            (meta,), (), ins,
-            [((rows, part), F32, near, CHIP), (held_shape, BF16, anywhere, HBM)],
+            (meta,), (), ins, outs,
             [
                 pltpu.VMEM((2, state_dim, part), F32), pltpu.VMEM((2 * state_dim, part), BF16),
-                pltpu.SemaphoreType.DMA((3,)),
+                pltpu.SemaphoreType.DMA((4,)),
             ],
             aliases=aliases,
         )
-
-    upward = [(at, at + 1) for at in range(count - 1)]
-    downward = [(at + 1, at) for at in range(count - 1)]
+        return results if has_begin else (*results, begin)
+
     lines_at = 2 * state_dim // lines
     from_slot = pl.BlockSpec((lines, part), lambda k, *_: (lines_at + k, 0))
     grad_part = pl.BlockSpec((1, 1, state_dim, part), lambda k, *_: (k, 1, 0, 0))
-    sums = sum_steps(("rep", "dom", "ctx"))
+    sums, exchanges = sum_steps(("rep", "dom", "ctx"))
     send_up, send_down, held_up, held_down = up_first, down_first, None, None
-    begin_there = begin_here
-    total = None
     for slot in range(slots):
-        got_up = lax.ppermute(send_up, "ctx", upward)
-        got_down = lax.ppermute(send_down, "ctx", downward)
-        waits = []
+        first_place = max(0, slot - chunks + 1)
+        got_down = lax.ppermute(
+            send_down, "ctx", [(count - 1 - at, count - 2 - at) for at in range(first_place, count - 1)]
+        )
+        got_up = lax.ppermute(send_up, "ctx", upward[first_place:])
+        waits_up, waits_down = [], []
         if slot == count - 2:
             earlier, later = got_up, got_down
-            waits.append(begin_here)
         if slot == count - 1:
+            begin_there = begin_here
             if doms == 2:
                 begin_there = lax.ppermute(begin_here, "dom", [(0, 1), (1, 0)])
             (total,) = call(
@@ -539,20 +645,25 @@
                 [((lines, state_dim), F32, whole((lines, state_dim)), None)],
                 [pltpu.VMEM((lines, state_dim), F32)],
             )
-            waits.append(total)
-        if slot >= count:
-            for step in sums[:2]:
-                total = step(total)
-            sums = sums[2:]
-            waits.append(total)
-            waits.append(begin_there)
         if slot == slots - 1:
             break
-        send_up, held_up = step_chain(
-            slot, got_up, up, up_small, up_land, up_source, held_up, waits
-        )
-        send_down, held_down = step_chain(
-            slot, got_down, down, down_small, down_land, down_source, held_down, []
+        if slot >= count - 1:
+            if slot > count - 1:
+                waits_down.append(begin_there)
+                for step in sums[:1]:
+                    total = step(total)
+                sums = sums[1:]
+            waits_down.append(total)
+        send_down, held_down, begin_here = step_chain(
+            slot, got_down, down, down_small, down_tables, held_down, begin_here, waits_down
+        )
+        if slot >= count - 1:
+            for step in sums[:1]:
+                total = step(total)
+            sums = sums[1:]
+            waits_up.append(total)
+        send_up, held_up, begin_here = step_chain(
+            slot, got_up, up, up_small, up_tables, held_up, begin_here, waits_up
         )
 
     def chunk_specs(at):
@@ -560,7 +671,10 @@
             pl.BlockSpec((length, part), lambda k, *_: (0, k + at)),
             pl.BlockSpec((1, length, 128), lambda k, *_: (k + at, 0, 0)),
             pl.BlockSpec((1, 2 * state_dim, part), lambda k, *_: (k + at, 0, 0)),
-            pl.BlockSpec((per_chunk, head_dim, state_dim), lambda k, *_: (k + at, 0, 0)),
+            pl.BlockSpec(
+                (per_chunk // local_heads, head_dim, local_heads * state_dim),
+                lambda k, *_: (k + at, 0, 0),
+            ),
             pl.BlockSpec((lines, part), lambda k, *_: (lines_at + k + at, 0)),
         )
 
@@ -574,43 +688,48 @@
             (begin_here, states, HBM), (begin_there, states, HBM), (earlier, small, None),
         ]
 
+    for step in sums:
+        total = step(total)
     slab = chunk_specs(0)[0]
-    mixed, grad_hidden, sum_c, sum_w = call(
+    mixed, grad_hidden, sum_c, sum_w, total = call(
         functools.partial(early_kernel, per_chunk, head_dim, vocab),
         (meta, skip_gain), (chunks - 1,),
-        finish_ins(0, reader_in, writer_in) + [(value, anywhere, None) for value in waits[:1]],
+        finish_ins(0, reader_in, writer_in) + [(total, anywhere, None)],
         [
             ((length, width), BF16, slab, HBM), ((length, width), BF16, slab, HBM),
             ((length, state_dim), F32, square, HBM), ((length, state_dim), F32, square, HBM),
-        ],
-    )
-    for step in sums:
-        total = step(total)
+            (total.shape, F32, anywhere, None),
+        ],
+        aliases={16: 4},
+    )
+    exchanged = [exchange(total) for exchange in exchanges]
     ins = finish_ins(chunks - 1, sum_c, sum_w) + [
         (got_up, whole(got_up.shape), None), (got_down, whole(got_down.shape), None),
         (mixed, anywhere, HBM), (grad_hidden, anywhere, HBM),
-    ]
+    ] + [(value, whole(value.shape), None) for value in [total] + exchanged]
     slab = chunk_specs(chunks - 1)[0]
-    mixed, grad_hidden, grad_cmat, grad_bmat = call(
+    mixed, grad_hidden, grad_cmat, grad_bmat, grad_table, grad_skip = call(
         functools.partial(
             last_kernel, per_chunk, head_dim, vocab, bmat_scale,
-            up_land + slots - 1, down_land + slots - 1, chunks - 1,
+            up_tables[0] + slots - 1, down_tables[0] + slots - 1, chunks - 1,
         ),
         (meta, skip_gain), (1,), ins,
         [
             ((length, width), BF16, slab, HBM), ((length, width), BF16, slab, HBM),
             ((length, state_dim), BF16, square, HBM), ((length, state_dim), BF16, square, HBM),
+            (table.shape, F32, whole(table.shape), HBM),
+            ((1, heads), F32, whole((1, heads)), HBM),
         ],
         [pltpu.VMEM((length, state_dim), F32)] * 2,
-        aliases={len(ins): 0, len(ins) + 1: 1},
+        aliases={18: 0, 19: 1},
     )
     return (
         mixed.reshape(hidden.shape),
         grad_hidden.reshape(hidden.shape),
         grad_bmat.reshape(bmat.shape),
         grad_cmat.reshape(cmat.shape),
-        total[:vocab, :],
-        total[vocab, :heads],
+        grad_table,
+        grad_skip.reshape(heads),
     )
 
 

time: 156 us -> 126 us (0.81)
  waiting for transfers between devices: 50 us -> 35.7 us
  between operations: 15.6 us -> 2.32 us
  starting transfers between devices: 46.5 us -> 42.5 us
  Pallas kernels: 41.7 us -> 44.4 us
    ppermute x17 -> x20, waiting for transfers between devices: 50 us -> 35.7 us  [the longest x6 17.7 us: per_device(): lax.ppermute(send_down, 'ctx', [(count - 1 - at, count - 2 - at) for at i...]
    ppermute x17 -> x20, starting transfers between devices: 44.9 us -> 40.9 us  [the longest x6 19.5 us: per_device(): got_up = lax.ppermute(send_up, 'ctx', upward[first_place:])]
    pallas_call x15 -> x17, Pallas kernels: 41.7 us -> 44.4 us  [call(): pl.pallas_call(body, out_shape=[jax.ShapeDtypeStruct(shape, kind) if plac...]
  transfers between devices with their start and end apart: 19 -> 21, of which waited for: 11 -> 13; matrix products, arithmetic and copies ran while one was open for 1% -> 0% of each run, Pallas kernels for 22% -> 31%
where the time goes in v2:
time: 126 us; the launch traced here: 125 us
  Pallas kernels  44.4 us (35%)
  starting transfers between devices  42.5 us (34%)
  waiting for transfers between devices  35.7 us (28%)
  between operations  2.32 us (2%)
    pallas_call x17, Pallas kernels, call(): pl.pallas_call(body, out_shape=[jax.ShapeDtypeStruct(shape, kind) if plac...  44.4 us
    ppermute x6, starting transfers between devices, per_device(): got_up = lax.ppermute(send_up, 'ctx', upward[first_place:])  19.5 us
    ppermute x6, waiting for transfers between devices, per_device(): lax.ppermute(send_down, 'ctx', [(count - 1 - at, count - 2 - at) for at i...  17.7 us
    ppermute x6, waiting for transfers between devices, per_device(): got_up = lax.ppermute(send_up, 'ctx', upward[first_place:])  8.46 us
    ppermute x6, starting transfers between devices, per_device(): lax.ppermute(send_down, 'ctx', [(count - 1 - at, count - 2 - at) for at i...  7.75 us
    ppermute x3, waiting for transfers between devices, sum_steps(): steps.append(lambda value, group=group: value + group[0](value))  6.16 us
    ppermute x1, starting transfers between devices, per_device(): from_before = lax.ppermute(own_state, 'ctx', upward)  5.58 us
    ppermute x3, starting transfers between devices, per_device(): exchanged = [exchange(total) for exchange in exchanges]  4.45 us
  transfers between devices with their start and end apart: 21, of which 13 were waited for; matrix products, arithmetic and copies ran while one was open for 0% of the time, Pallas kernels for 31%

profile of v2, /device:TPU:0, one launch (start us, length us, event | category | flops | bytes accessed | tf_op | source)
XLA Modules:
  0.0 125.0 jit_solution(2178864022855737084)
XLA Ops:
  1.9 5.6 %collective-permute-start = (f32[4,128,128]{2,1,0:T(8,128)}, f32[4,128,128]{2,1,0:T(8,128)S(1)}, u32[]{:S(2)}, u32[]{:S(2)}) collective-permute-start(f32[4,128,128]{2,1,0:T(8,128)} %bitcast.23), channel_id=1, source_target_pairs={{0,8},{8,16},{16,24},{1,9},{9,17},{17,25},{2,10},{10,18},{18,26},{... | collective-permute-start | bytes 786440 | tf_op jit(solution)/shard_map/ppermute | solution.py:504
  9.0 4.6 %shard_map.163 = (f32[288,512]{1,0:T(8,128)S(1)}, f32[288,512]{1,0:T(8,128)S(1)}, f32[4,8,512]{2,1,0:T(8,128)S(1)}, f32[4,8,512]{2,1,0:T(8,128)S(1)}, f32[4,128,128]{2,1,0:T(8,128)}, /*index=5*/bf16[128,128]{1,0:T(8,128)(2,1)}) custom-call(s32[52]{0:T(128)S(1)} %concatenate.3.meta.refs_0_, bf16[128,128]{1,0:T(8,128)(2,1)} %bitcast.39, ...), custom_call_target="tpu_custom_call" | custom-call | tf_op jit(solution)/shard_map/pallas_call | solution.py:397
  15.6 4.7 %collective-permute-start.2 = (f32[288,512]{1,0:T(8,128)S(1)}, f32[288,512]{1,0:T(8,128)S(1)}, u32[]{:S(2)}, u32[]{:S(2)}) collective-permute-start(f32[288,512]{1,0:T(8,128)S(1)} %get-tuple-element.64), channel_id=1, source_target_pairs={{0,8},{8,16},{16,24},{1,9},{9,17},{17,25},{2,10},{10,18},{18,26},{... | collective-permute-start | bytes 1769480 | tf_op jit(solution)/shard_map/ppermute | solution.py:626
  20.3 7.1 %shard_map.164 = (f32[4,2,128,512]{3,2,1,0:T(8,128)}, f32[4,2,128,512]{3,2,1,0:T(8,128)}, f32[128,2048]{1,0:T(8,128)}, f32[128,2048]{1,0:T(8,128)}, f32[128,128]...) custom-call(s32[52]{0:T(128)S(1)} %concatenate.3.meta.refs_0_, bf16[128,2048]{1,0:T(8,128)(2,1)} %bitcast.26, ...), custom_call_target="tpu_custom_call" | custom-call | tf_op jit(solution)/shard_map/pallas_call | solution.py:397
  29.0 2.0 %collective-permute-done.3.refs_1_ = f32[288,512]{1,0:T(8,128)S(1)} collective-permute-done((f32[288,512]{1,0:T(8,128)S(1)}, f32[288,512]{1,0:T(8,128)S(1)}, u32[]{:S(2)}, u32[]{:S(2)}) %collective-permute-start.3) | collective-permute-done | bytes 589856 | tf_op jit(solution)/shard_map/ppermute | solution.py:623
  31.0 1.8 %shard_map.167 = (f32[288,512]{1,0:T(8,128)S(1)}, bf16[5,256,512]{2,1,0:T(8,128)(2,1)}, f32[5,128,512]{2,1,0:T(8,128)}) custom-call(s32[52]{0:T(128)S(1)} %concatenate.3.meta.refs_0_, f32[288,512]{1,0:T(8,128)S(1)} %collective-permute-done.3.refs_1_, f32[4,2,128,512]{3,2,1,0:T(8,128)} %get-tuple-element.69.refs_2_.grad_down, ...), custom_call_target="tpu_custom_call", output_to_operand_aliasing={{2}: (5, {})} | custom-call | tf_op jit(solution)/shard_map/pallas_call | solution.py:397
  34.2 1.8 %shard_map.168 = (f32[288,512]{1,0:T(8,128)S(1)}, bf16[5,256,512]{2,1,0:T(8,128)(2,1)}, f32[5,128,512]{2,1,0:T(8,128)}) custom-call(s32[52]{0:T(128)S(1)} %concatenate.3.meta.refs_0_, f32[288,512]{1,0:T(8,128)S(1)} %collective-permute-done.2.refs_1_, f32[4,2,128,512]{3,2,1,0:T(8,128)} %get-tuple-element.65.refs_2_.grad_up, ...), custom_call_target="tpu_custom_call", output_to_operand_aliasing={{2}: (5, {})} | custom-call | tf_op jit(solution)/shard_map/pallas_call | solution.py:397
  36.0 4.6 %collective-permute-start.4 = (f32[288,512]{1,0:T(8,128)S(1)}, f32[288,512]{1,0:T(8,128)S(1)}, u32[]{:S(2)}, u32[]{:S(2)}) collective-permute-start(f32[288,512]{1,0:T(8,128)S(1)} %get-tuple-element.71), channel_id=1, source_target_pairs={{0,8},{8,16},{16,24},{1,9},{9,17},{17,25},{2,10},{10,18},{18,26},{... | collective-permute-start | bytes 1769480 | tf_op jit(solution)/shard_map/ppermute | solution.py:626
  40.6 7.9 %collective-permute-done.5.refs_1_ = f32[288,512]{1,0:T(8,128)S(1)} collective-permute-done((f32[288,512]{1,0:T(8,128)S(1)}, f32[288,512]{1,0:T(8,128)S(1)}, u32[]{:S(2)}, u32[]{:S(2)}) %collective-permute-start.5) | collective-permute-done | bytes 589856 | tf_op jit(solution)/shard_map/ppermute | solution.py:623
  48.5 1.8 %shard_map.169 = (f32[288,512]{1,0:T(8,128)S(1)}, bf16[5,256,512]{2,1,0:T(8,128)(2,1)}, f32[5,128,512]{2,1,0:T(8,128)}) custom-call(s32[52]{0:T(128)S(1)} %concatenate.3.meta.refs_0_, f32[288,512]{1,0:T(8,128)S(1)} %collective-permute-done.5.refs_1_, ...), custom_call_target="tpu_custom_call", output_to_operand_aliasing={{1}: (5, {}), {2}: (6, {})} | custom-call | tf_op jit(solution)/shard_map/pallas_call | solution.py:397
  51.5 1.8 %shard_map.170 = (f32[288,512]{1,0:T(8,128)S(1)}, bf16[5,256,512]{2,1,0:T(8,128)(2,1)}, f32[5,128,512]{2,1,0:T(8,128)}) custom-call(s32[52]{0:T(128)S(1)} %concatenate.3.meta.refs_0_, f32[288,512]{1,0:T(8,128)S(1)} %collective-permute-done.4.refs_1_, ...), custom_call_target="tpu_custom_call", output_to_operand_aliasing={{1}: (5, {}), {2}: (6, {})} | custom-call | tf_op jit(solution)/shard_map/pallas_call | solution.py:397
  53.4 4.4 %collective-permute-start.6 = (f32[288,512]{1,0:T(8,128)S(1)}, f32[288,512]{1,0:T(8,128)S(1)}, u32[]{:S(2)}, u32[]{:S(2)}) collective-permute-start(f32[288,512]{1,0:T(8,128)S(1)} %get-tuple-element.77), channel_id=1, source_target_pairs={{0,8},{8,16},{16,24},{1,9},{9,17},{17,25},{2,10},{10,18},{18,26},{... | collective-permute-start | bytes 1769480 | tf_op jit(solution)/shard_map/ppermute | solution.py:626
  60.7 7.2 %collective-permute-done.6.refs_1_.earlier = f32[288,512]{1,0:T(8,128)S(1)} collective-permute-done((f32[288,512]{1,0:T(8,128)S(1)}, f32[288,512]{1,0:T(8,128)S(1)}, u32[]{:S(2)}, u32[]{:S(2)}) %collective-permute-start.6) | collective-permute-done | bytes 589856 | tf_op jit(solution)/shard_map/ppermute | solution.py:626
  69.6 4.4 %collective-permute-start.7 = (f32[256,512]{1,0:T(8,128)S(1)}, f32[256,512]{1,0:T(8,128)S(1)}, u32[]{:S(2)}, u32[]{:S(2)}) collective-permute-start(f32[256,512]{1,0:T(8,128)S(1)} %get-tuple-element.79), channel_id=1, source_target_pairs={{0,8},{8,16},{16,24},{1,9},{9,17},{17,25},{2,10},{10,18},{18,26},{... | collective-permute-start | bytes 1572872 | tf_op jit(solution)/shard_map/ppermute | solution.py:626
  74.0 1.7 %shard_map.175 = (f32[256,512]{1,0:T(8,128)S(1)}, bf16[5,256,512]{2,1,0:T(8,128)(2,1)}) custom-call(s32[52]{0:T(128)S(1)} %concatenate.3.meta.refs_0_, f32[288,512]{1,0:T(8,128)S(1)} %collective-permute-done.8.later.refs_1_, f32[4,2,128,512]{3,2,1,0:T(8,128)} %get-tuple-element.69.refs_2_.grad_down, ...), custom_call_target="tpu_custom_call", output_to_operand_aliasing={{1}: (5, {})} | custom-call | tf_op jit(solution)/shard_map/pallas_call | solution.py:397
  77.1 3.3 %shard_map.172.refs_6_ = f32[8,128]{1,0:T(8,128)S(1)} custom-call(s32[52]{0:T(128)S(1)} %concatenate.3.meta.refs_0_, f32[288,512]{1,0:T(8,128)S(1)} %collective-permute-done.6.refs_1_.earlier, f32[288,512]{1,0:T(8,128)S(1)} %collective-permute-done.8.later.refs_1_, f32[4,8,512]{2,1,0:T(8,128)S(1)} %get-tuple-element.67.refs_3_.refs_4_.small, ...), custom_call_target="tpu_custom_call" | custom-call | tf_op jit(solution)/shard_map/pallas_call | solution.py:397
  84.2 3.5 %collective-permute-done.13.refs_1_ = f32[256,512]{1,0:T(8,128)S(1)} collective-permute-done((f32[256,512]{1,0:T(8,128)S(1)}, f32[256,512]{1,0:T(8,128)S(1)}, u32[]{:S(2)}, u32[]{:S(2)}) %collective-permute-start.13) | collective-permute-done | bytes 524320 | tf_op jit(solution)/shard_map/ppermute | solution.py:623
  91.8 2.5 %collective-permute-done.11 = f32[8,128]{1,0:T(8,128)S(1)} collective-permute-done((f32[8,128]{1,0:T(8,128)S(1)}, f32[8,128]{1,0:T(8,128)S(1)}, u32[]{:S(2)}, u32[]{:S(2)}) %collective-permute-start.11) | collective-permute-done | bytes 4128 | tf_op jit(solution)/shard_map/ppermute | solution.py:443
  95.5 2.5 %collective-permute-done.12 = f32[8,128]{1,0:T(8,128)S(1)} collective-permute-done((f32[8,128]{1,0:T(8,128)S(1)}, f32[8,128]{1,0:T(8,128)S(1)}, u32[]{:S(2)}, u32[]{:S(2)}) %collective-permute-start.12) | collective-permute-done | bytes 4128 | tf_op jit(solution)/shard_map/ppermute | solution.py:443
  100.4 4.3 %collective-permute-done.14.refs_1_ = f32[256,512]{1,0:T(8,128)S(1)} collective-permute-done((f32[256,512]{1,0:T(8,128)S(1)}, f32[256,512]{1,0:T(8,128)S(1)}, u32[]{:S(2)}, u32[]{:S(2)}) %collective-permute-start.14) | collective-permute-done | bytes 524320 | tf_op jit(solution)/shard_map/ppermute | solution.py:623
  107.8 5.9 %shard_map.178 = (bf16[128,2048]{1,0:T(8,128)(2,1)}, bf16[128,2048]{1,0:T(8,128)(2,1)}, f32[128,128]{1,0:T(8,128)}, f32[128,128]{1,0:T(8,128)}, f32[8,128]{1,0:T(8,128)S(1)}) custom-call(s32[52]{0:T(128)S(1)} %concatenate.3.meta.refs_0_, f32[16]{0:T(128)S(1)} %copy-done.2, bf16[128,2048]{1,0:T(8,128)(2,1)} %bitcast.27, ...), custom_call_target="tpu_custom_call", output_to_operand_aliasing={{4}: (16, {})} | custom-call | tf_op jit(solution)/shard_map/pallas_call | solution.py:397
  114.9 3.1 %collective-permute-start.19 = (f32[8,128]{1,0:T(8,128)S(1)}, f32[8,128]{1,0:T(8,128)S(1)}, u32[]{:S(2)}, u32[]{:S(2)}) collective-permute-start(f32[8,128]{1,0:T(8,128)S(1)} %get-tuple-element.99.refs_2_), channel_id=1, source_target_pairs={{0,16},{8,24},{16,0},{24,8},{1,17},{9,25},{17,1},{25,9},{2,18},{10... | collective-permute-start | bytes 12296 | tf_op jit(solution)/shard_map/ppermute | solution.py:705
  119.6 2.0 %collective-permute-done.18.refs_3_ = f32[8,128]{1,0:T(8,128)S(1)} collective-permute-done((f32[8,128]{1,0:T(8,128)S(1)}, f32[8,128]{1,0:T(8,128)S(1)}, u32[]{:S(2)}, u32[]{:S(2)}) %collective-permute-start.18) | collective-permute-done | bytes 4128 | tf_op jit(solution)/shard_map/ppermute | solution.py:705
  121.6 3.5 %shard_map.179 = (bf16[128,2048]{1,0:T(8,128)(2,1)}, bf16[128,2048]{1,0:T(8,128)(2,1)}, bf16[128,128]{1,0:T(8,128)(2,1)}, bf16[128,128]{1,0:T(8,128)(2,1)}, f32[4,128]{1,0:T(4,128)}, /*index=5*/f32[1,16]{1,0:T(1,128)}) custom-call(s32[52]{0:T(128)S(1)} %concatenate.3.meta.refs_0_, f32[16]{0:T(128)S(1)} %copy-done.2, ...), custom_call_target="tpu_custom_call", output_to_operand_aliasing={{0}: (18, {}), {1}: (19, {})} | custom-call | tf_op jit(solution)/shard_map/pallas_call | solution.py:397
  (49 shorter events, 30.5 us)
Async XLA Ops:
  0.6 13.0 %collective-permute-start.1 = (f32[4,128,128]{2,1,0:T(8,128)}, f32[4,128,128]{2,1,0:T(8,128)S(1)}, u32[]{:S(2)}, u32[]{:S(2)}) collective-permute-start(f32[4,128,128]{2,1,0:T(8,128)} %bitcast.22), channel_id=1, source_target_pairs={{8,0},{16,8},{24,16},{9,1},{17,9},{25,17},{10,2},{18,10},{26,18},{... | collective-permute-start | bytes 786440 | tf_op jit(solution)/shard_map/ppermute | solution.py:505
  1.9 11.7 %collective-permute-start = (f32[4,128,128]{2,1,0:T(8,128)}, f32[4,128,128]{2,1,0:T(8,128)S(1)}, u32[]{:S(2)}, u32[]{:S(2)}) collective-permute-start(f32[4,128,128]{2,1,0:T(8,128)} %bitcast.23), channel_id=1, source_target_pairs={{0,8},{8,16},{16,24},{1,9},{9,17},{17,25},{2,10},{10,18},{18,26},{... | collective-permute-start | bytes 786440 | tf_op jit(solution)/shard_map/ppermute | solution.py:504
  13.6 13.8 %copy-start.1 = (f32[1,1,4,128,128]{4,3,2,1,0:T(8,128)S(1)}, f32[1,1,4,128,128]{4,3,2,1,0:T(8,128)}, u32[]{:S(2)}) copy-start(f32[1,1,4,128,128]{4,3,2,1,0:T(8,128)} %param.20) | copy-start | bytes 786436
  14.3 16.7 %collective-permute-start.3 = (f32[288,512]{1,0:T(8,128)S(1)}, f32[288,512]{1,0:T(8,128)S(1)}, u32[]{:S(2)}, u32[]{:S(2)}) collective-permute-start(f32[288,512]{1,0:T(8,128)S(1)} %get-tuple-element.68), channel_id=1, source_target_pairs={{24,16},{16,8},{8,0},{25,17},{17,9},{9,1},{26,18},{18,10},{10,2},{... | collective-permute-start | bytes 1769480 | tf_op jit(solution)/shard_map/ppermute | solution.py:623
  15.6 18.5 %collective-permute-start.2 = (f32[288,512]{1,0:T(8,128)S(1)}, f32[288,512]{1,0:T(8,128)S(1)}, u32[]{:S(2)}, u32[]{:S(2)}) collective-permute-start(f32[288,512]{1,0:T(8,128)S(1)} %get-tuple-element.64), channel_id=1, source_target_pairs={{0,8},{8,16},{16,24},{1,9},{9,17},{17,25},{2,10},{10,18},{18,26},{... | collective-permute-start | bytes 1769480 | tf_op jit(solution)/shard_map/ppermute | solution.py:626
  32.8 15.7 %collective-permute-start.5 = (f32[288,512]{1,0:T(8,128)S(1)}, f32[288,512]{1,0:T(8,128)S(1)}, u32[]{:S(2)}, u32[]{:S(2)}) collective-permute-start(f32[288,512]{1,0:T(8,128)S(1)} %get-tuple-element.73), channel_id=1, source_target_pairs={{24,16},{16,8},{8,0},{25,17},{17,9},{9,1},{26,18},{18,10},{10,2},{... | collective-permute-start | bytes 1769480 | tf_op jit(solution)/shard_map/ppermute | solution.py:623
  36.0 15.5 %collective-permute-start.4 = (f32[288,512]{1,0:T(8,128)S(1)}, f32[288,512]{1,0:T(8,128)S(1)}, u32[]{:S(2)}, u32[]{:S(2)}) collective-permute-start(f32[288,512]{1,0:T(8,128)S(1)} %get-tuple-element.71), channel_id=1, source_target_pairs={{0,8},{8,16},{16,24},{1,9},{9,17},{17,25},{2,10},{10,18},{18,26},{... | collective-permute-start | bytes 1769480 | tf_op jit(solution)/shard_map/ppermute | solution.py:626
  53.4 14.5 %collective-permute-start.6 = (f32[288,512]{1,0:T(8,128)S(1)}, f32[288,512]{1,0:T(8,128)S(1)}, u32[]{:S(2)}, u32[]{:S(2)}) collective-permute-start(f32[288,512]{1,0:T(8,128)S(1)} %get-tuple-element.77), channel_id=1, source_target_pairs={{0,8},{8,16},{16,24},{1,9},{9,17},{17,25},{2,10},{10,18},{18,26},{... | collective-permute-start | bytes 1769480 | tf_op jit(solution)/shard_map/ppermute | solution.py:626
  57.8 16.2 %collective-permute-start.8 = (f32[288,512]{1,0:T(8,128)S(1)}, f32[288,512]{1,0:T(8,128)S(1)}, u32[]{:S(2)}, u32[]{:S(2)}) collective-permute-start(f32[288,512]{1,0:T(8,128)S(1)} %get-tuple-element.81), channel_id=1, source_target_pairs={{24,16},{16,8},{8,0},{25,17},{17,9},{9,1},{26,18},{18,10},{10,2},{... | collective-permute-start | bytes 1769480 | tf_op jit(solution)/shard_map/ppermute | solution.py:623
  59.1 41.3 %collective-permute-start.15 = (f32[5,128,512]{2,1,0:T(8,128)}, f32[5,128,512]{2,1,0:T(8,128)S(1)}, u32[]{:S(2)}, u32[]{:S(2)}) collective-permute-start(f32[5,128,512]{2,1,0:T(8,128)} %get-tuple-element.91.begin_here), channel_id=1, source_target_pairs={{0,4},{4,0},{1,5},{5,1},{2,6},{6,2},{3,7},{7,3},{8,12},{12,8},{9,1... | collective-permute-start | bytes 3932168 | tf_op jit(solution)/shard_map/ppermute | solution.py:633
  69.6 12.1 %collective-permute-start.7 = (f32[256,512]{1,0:T(8,128)S(1)}, f32[256,512]{1,0:T(8,128)S(1)}, u32[]{:S(2)}, u32[]{:S(2)}) collective-permute-start(f32[256,512]{1,0:T(8,128)S(1)} %get-tuple-element.79), channel_id=1, source_target_pairs={{0,8},{8,16},{16,24},{1,9},{9,17},{17,25},{2,10},{10,18},{18,26},{... | collective-permute-start | bytes 1572872 | tf_op jit(solution)/shard_map/ppermute | solution.py:626
  75.8 11.8 %collective-permute-start.13 = (f32[256,512]{1,0:T(8,128)S(1)}, f32[256,512]{1,0:T(8,128)S(1)}, u32[]{:S(2)}, u32[]{:S(2)}) collective-permute-start(f32[256,512]{1,0:T(8,128)S(1)} %get-tuple-element.87), channel_id=1, source_target_pairs={{24,16},{16,8},{8,0},{25,17},{17,9},{9,1},{26,18},{18,10},{10,2},{... | collective-permute-start | bytes 1572872 | tf_op jit(solution)/shard_map/ppermute | solution.py:623
  80.4 1.2 collective-permute-start.9
  83.5 14.5 %collective-permute-start.10 = (f32[256,512]{1,0:T(8,128)S(1)}, f32[256,512]{1,0:T(8,128)S(1)}, u32[]{:S(2)}, u32[]{:S(2)}) collective-permute-start(f32[256,512]{1,0:T(8,128)S(1)} %get-tuple-element.83), channel_id=1, source_target_pairs={{8,16},{16,24},{9,17},{17,25},{10,18},{18,26},{11,19},{19,27},{12,... | collective-permute-start | bytes 1572872 | tf_op jit(solution)/shard_map/ppermute | solution.py:626
  89.4 15.4 %collective-permute-start.14 = (f32[256,512]{1,0:T(8,128)S(1)}, f32[256,512]{1,0:T(8,128)S(1)}, u32[]{:S(2)}, u32[]{:S(2)}) collective-permute-start(f32[256,512]{1,0:T(8,128)S(1)} %get-tuple-element.89), channel_id=1, source_target_pairs={{16,8},{8,0},{17,9},{9,1},{18,10},{10,2},{19,11},{11,3},{20,12},{1... | collective-permute-start | bytes 1572872 | tf_op jit(solution)/shard_map/ppermute | solution.py:623
  90.7 3.7 %collective-permute-start.11 = (f32[8,128]{1,0:T(8,128)S(1)}, f32[8,128]{1,0:T(8,128)S(1)}, u32[]{:S(2)}, u32[]{:S(2)}) collective-permute-start(f32[8,128]{1,0:T(8,128)S(1)} %add.47.refs_6_), channel_id=1, source_target_pairs={{0,2},{1,3},{2,0},{3,1},{4,6},{5,7},{6,4},{7,5},{8,10},{9,11},{10,... | collective-permute-start | bytes 12296 | tf_op jit(solution)/shard_map/ppermute | solution.py:443
  94.3 3.6 %collective-permute-start.12 = (f32[8,128]{1,0:T(8,128)S(1)}, f32[8,128]{1,0:T(8,128)S(1)}, u32[]{:S(2)}, u32[]{:S(2)}) collective-permute-start(f32[8,128]{1,0:T(8,128)S(1)} %add.48.refs_7_), channel_id=1, source_target_pairs={{0,4},{4,0},{1,5},{5,1},{2,6},{6,2},{3,7},{7,3},{8,12},{12,8},{9,1... | collective-permute-start | bytes 12296 | tf_op jit(solution)/shard_map/ppermute | solution.py:443
  99.7 21.9 %collective-permute-start.16 = (f32[256,512]{1,0:T(8,128)S(1)}, f32[256,512]{1,0:T(8,128)S(1)}, u32[]{:S(2)}, u32[]{:S(2)}) collective-permute-start(f32[256,512]{1,0:T(8,128)S(1)} %get-tuple-element.95), channel_id=1, source_target_pairs={{16,24},{17,25},{18,26},{19,27},{20,28},{21,29},{22,30},{23,31}} | collective-permute-start | bytes 1572872 | tf_op jit(solution)/shard_map/ppermute | solution.py:626
  100.4 6.1 %copy-start = (f32[5,128,512]{2,1,0:T(8,128)}, f32[5,128,512]{2,1,0:T(8,128)S(1)}, u32[]{:S(2)}) copy-start(f32[5,128,512]{2,1,0:T(8,128)S(1)} %collective-permute-done.15.refs_6_.begin_there) | copy-start | bytes 3932164
  104.8 3.1 %copy-start.2 = (f32[16]{0:T(128)S(1)}, f32[16]{0:T(128)}, u32[]{:S(2)}) copy-start(f32[16]{0:T(128)} %gains.3) | copy-start | bytes 196
  106.5 15.1 %collective-permute-start.17 = (f32[256,512]{1,0:T(8,128)S(1)}, f32[256,512]{1,0:T(8,128)S(1)}, u32[]{:S(2)}, u32[]{:S(2)}) collective-permute-start(f32[256,512]{1,0:T(8,128)S(1)} %get-tuple-element.96), channel_id=1, source_target_pairs={{8,0},{9,1},{10,2},{11,3},{12,4},{13,5},{14,6},{15,7}} | collective-permute-start | bytes 1572872 | tf_op jit(solution)/shard_map/ppermute | solution.py:623
  113.8 5.6 %collective-permute-start.20 = (f32[8,128]{1,0:T(8,128)S(1)}, f32[8,128]{1,0:T(8,128)S(1)}, u32[]{:S(2)}, u32[]{:S(2)}) collective-permute-start(f32[8,128]{1,0:T(8,128)S(1)} %get-tuple-element.99.refs_2_), channel_id=1, source_target_pairs={{0,24},{8,16},{16,8},{24,0},{1,25},{9,17},{17,9},{25,1},{2,26},{10... | collective-permute-start | bytes 12296 | tf_op jit(solution)/shard_map/ppermute | solution.py:705
  114.9 4.7 %collective-permute-start.19 = (f32[8,128]{1,0:T(8,128)S(1)}, f32[8,128]{1,0:T(8,128)S(1)}, u32[]{:S(2)}, u32[]{:S(2)}) collective-permute-start(f32[8,128]{1,0:T(8,128)S(1)} %get-tuple-element.99.refs_2_), channel_id=1, source_target_pairs={{0,16},{8,24},{16,0},{24,8},{1,17},{9,25},{17,1},{25,9},{2,18},{10... | collective-permute-start | bytes 12296 | tf_op jit(solution)/shard_map/ppermute | solution.py:705
  118.0 3.6 %collective-permute-start.18 = (f32[8,128]{1,0:T(8,128)S(1)}, f32[8,128]{1,0:T(8,128)S(1)}, u32[]{:S(2)}, u32[]{:S(2)}) collective-permute-start(f32[8,128]{1,0:T(8,128)S(1)} %get-tuple-element.99.refs_2_), channel_id=1, source_target_pairs={{0,8},{8,0},{16,24},{24,16},{1,9},{9,1},{17,25},{25,17},{2,10},{10... | collective-permute-start | bytes 12296 | tf_op jit(solution)/shard_map/ppermute | solution.py:705

commit v3 on v2

--- a/solution.py
+++ b/solution.py
@@ -44,8 +44,7 @@
 def start_kernel(
     per_chunk, head_dim, vocab, chunks,
     meta, bmat, cmat, tokens, table, step_t, rate_t, hid_far, cot_far,
-    up_first, down_first, up_small, down_small, cols, writer,
-    hid, cot, sems,
+    up_first, down_first, up_small, down_small, cols, writer, hid, cot, sems,
 ):
     length = bmat.shape[0]
     state = bmat.shape[1]
@@ -165,29 +164,14 @@
 
 def combine_kernel(vocab, has_small, has_begin, slot, tables, waits, *refs):
     meta, received, own, small, decays = refs[:5]
-    near, rounded, sems = refs[-3:]
-    send, held = refs[-6:-4] if has_begin else refs[-5:-3]
+    send, held = refs[-3:-1] if has_begin else refs[-2:]
     del waits
     state = own.shape[2]
     land, source, forward, piece = (at + slot for at in tables)
-    fetch = [
-        pltpu.make_async_copy(own.at[meta[source], at], near.at[at], sems.at[at])
-        for at in range(2)
-    ]
-    for copy in fetch:
-        copy.start()
-    stores = []
     if has_begin:
-        begin = refs[-4]
-        stores.append(
-            pltpu.make_async_copy(
-                received.at[0:state, 0 : begin.shape[2]], begin.at[meta[piece]], sems.at[3]
-            )
-        )
-        stores[-1].start()
-    rounded[...] = received[0 : 2 * state, :].astype(BF16)
-    stores.append(pltpu.make_async_copy(rounded, held.at[meta[land]], sems.at[2]))
-    stores[-1].start()
+        begin = refs[-1]
+        begin[meta[piece]] = received[0:state, 0 : begin.shape[2]]
+    held[meta[land]] = received[0 : 2 * state, :].astype(BF16)
     passing = meta[forward] != 0
     decay = jnp.where(passing, 1.0, decays[meta[source], vocab : vocab + 1, :])
     adding = jnp.where(passing, 0.0, 1.0)
@@ -197,11 +181,8 @@
             rows = slice(2 * state + at * lines, 2 * state + (at + 1) * lines)
             send[rows, :] = decays[at, vocab : vocab + 1, :] * received[rows, :] + small[at]
     for at in range(2):
-        fetch[at].wait()
         rows = slice(at * state, (at + 1) * state)
-        send[rows, :] = decay * received[rows, :] + adding * near[at]
-    for store in stores:
-        store.wait()
+        send[rows, :] = decay * received[rows, :] + adding * own[meta[source], at]
 
 
 def inner_kernel(
@@ -514,9 +495,9 @@
     tok_spec = whole((1, length))
     full_rows = 2 * state_dim + chunks * lines
     small_shape = (chunks, lines, part)
-    first = ((full_rows, part), F32, whole((full_rows, part)), CHIP)
-
-    up_first, down_first, up_small, down_small, cols, writer = call(
+    first = ((full_rows, part), F32, near, CHIP)
+
+    up_first, down_first, up_small, down_small, cols, writer, hid, cot = call(
         functools.partial(start_kernel, per_chunk, head_dim, vocab, chunks),
         (meta,), (1,),
         [
@@ -526,15 +507,11 @@
         ],
         [
             first, first,
-            (small_shape, F32, whole(small_shape), CHIP),
-            (small_shape, F32, whole(small_shape), CHIP),
-            ((chunks, length, 128), F32, whole((chunks, length, 128)), HBM),
-            ((length, state_dim), BF16, square, HBM),
-        ],
-        [
-            pltpu.VMEM((length, width), BF16), pltpu.VMEM((length, width), BF16),
-            pltpu.SemaphoreType.DMA((chunks, 2)),
-        ],
+            (small_shape, F32, near, CHIP), (small_shape, F32, near, CHIP),
+            ((chunks, length, 128), F32, near, CHIP), ((length, state_dim), BF16, near, CHIP),
+            ((length, width), BF16, near, CHIP), ((length, width), BF16, near, CHIP),
+        ],
+        [pltpu.SemaphoreType.DMA((chunks, 2))],
     )
 
     up_first, down_first = call(
@@ -558,7 +535,7 @@
             (own_state, anywhere, None), (from_before, anywhere, None),
             (from_after, anywhere, None),
         ],
-        [(begin_shape, F32, anywhere, HBM)],
+        [(begin_shape, F32, near, CHIP)],
         [pltpu.SemaphoreType.DMA((3, local_heads))],
     )
 
@@ -566,17 +543,17 @@
         functools.partial(inner_kernel, per_chunk, head_dim, vocab),
         (meta,), (chunks,),
         [
-            (hid, by_chunk, HBM), (cot, by_chunk, HBM), (writer, square, HBM),
-            (reads, square, HBM), (toks, tok_spec, HBM), (cols, one_cols, HBM),
-        ],
-        [
-            ((chunks, 2, state_dim, part), F32, pair, HBM),
-            ((chunks, 2, state_dim, part), F32, pair, HBM),
-            ((length, width), F32, by_chunk, HBM),
-            ((length, width), F32, by_chunk, HBM),
-            ((length, state_dim), F32, square, HBM),
-            ((length, state_dim), F32, square, HBM),
-            ((lines, state_dim), F32, whole((lines, state_dim)), HBM),
+            (hid, by_chunk, CHIP), (cot, by_chunk, CHIP), (writer, square, CHIP),
+            (reads, square, HBM), (toks, tok_spec, HBM), (cols, one_cols, CHIP),
+        ],
+        [
+            ((chunks, 2, state_dim, part), F32, pair, CHIP),
+            ((chunks, 2, state_dim, part), F32, pair, CHIP),
+            ((length, width), F32, by_chunk, CHIP),
+            ((length, width), F32, by_chunk, CHIP),
+            ((length, state_dim), F32, square, CHIP),
+            ((length, state_dim), F32, square, CHIP),
+            ((lines, state_dim), F32, whole((lines, state_dim)), CHIP),
         ],
         [pltpu.VMEM((length, length), F32)] * 3 + [pltpu.VMEM((state_dim, length), BF16)] * 2,
     )
@@ -587,28 +564,24 @@
         rows = full_rows if has_small else 2 * state_dim
         held_shape = (chunks + 1, 2 * state_dim, part)
         ins = [
-            (received, near, CHIP), (own, anywhere, HBM), (small, near, CHIP),
+            (received, near, CHIP), (own, near, CHIP), (small, near, CHIP),
             (down_small, near, CHIP),
         ]
-        outs = [((rows, part), F32, near, CHIP), (held_shape, BF16, anywhere, HBM)]
+        outs = [((rows, part), F32, near, CHIP), (held_shape, BF16, near, CHIP)]
         aliases = {}
         if held is not None:
             aliases[1 + len(ins)] = 1
-            ins.append((held, anywhere, HBM))
+            ins.append((held, near, CHIP))
         if has_begin:
             aliases[1 + len(ins)] = 2
-            ins.append((begin, anywhere, HBM))
-            outs.append((begin_shape, F32, anywhere, HBM))
+            ins.append((begin, near, CHIP))
+            outs.append((begin_shape, F32, near, CHIP))
         ins += [(value, anywhere, None) for value in waits]
         results = call(
             functools.partial(
                 combine_kernel, vocab, has_small, has_begin, slot, tables, len(waits)
             ),
             (meta,), (), ins, outs,
-            [
-                pltpu.VMEM((2, state_dim, part), F32), pltpu.VMEM((2 * state_dim, part), BF16),
-                pltpu.SemaphoreType.DMA((4,)),
-            ],
             aliases=aliases,
         )
         return results if has_begin else (*results, begin)
@@ -639,8 +612,8 @@
                 (meta,), (chunks,),
                 [
                     (earlier, from_slot, None), (later, from_slot, None),
-                    (down_small, one_small, None), (up, grad_part, HBM),
-                    (down, grad_part, HBM), (tab, whole(tab.shape), HBM),
+                    (down_small, one_small, None), (up, grad_part, CHIP),
+                    (down, grad_part, CHIP), (tab, whole(tab.shape), CHIP),
                 ],
                 [((lines, state_dim), F32, whole((lines, state_dim)), None)],
                 [pltpu.VMEM((lines, state_dim), F32)],
@@ -681,11 +654,11 @@
     def finish_ins(at, sum_c, sum_w):
         slab, col, chain, states, small = chunk_specs(at)
         return [
-            (hid, slab, HBM), (cot, slab, HBM), (writer, square, HBM), (reads, square, HBM),
-            (cols, col, HBM), (mixed_in, slab, HBM), (back_in, slab, HBM),
-            (sum_c, square, HBM), (sum_w, square, HBM),
-            (held_up, chain, HBM), (held_down, chain, HBM),
-            (begin_here, states, HBM), (begin_there, states, HBM), (earlier, small, None),
+            (hid, slab, CHIP), (cot, slab, CHIP), (writer, square, CHIP), (reads, square, HBM),
+            (cols, col, CHIP), (mixed_in, slab, CHIP), (back_in, slab, CHIP),
+            (sum_c, square, CHIP), (sum_w, square, CHIP),
+            (held_up, chain, CHIP), (held_down, chain, CHIP),
+            (begin_here, states, CHIP), (begin_there, states, CHIP), (earlier, small, None),
         ]
 
     for step in sums:
@@ -697,7 +670,7 @@
         finish_ins(0, reader_in, writer_in) + [(total, anywhere, None)],
         [
             ((length, width), BF16, slab, HBM), ((length, width), BF16, slab, HBM),
-            ((length, state_dim), F32, square, HBM), ((length, state_dim), F32, square, HBM),
+            ((length, state_dim), F32, square, CHIP), ((length, state_dim), F32, square, CHIP),
             (total.shape, F32, anywhere, None),
         ],
         aliases={16: 4},

time: 126 us -> 113 us (0.90)
  Pallas kernels: 44.4 us -> 26.1 us
  waiting for transfers between devices: 35.7 us -> 41.9 us
    pallas_call x17, Pallas kernels: 44.4 us -> 26.1 us  [call(): pl.pallas_call(body, out_shape=[jax.ShapeDtypeStruct(shape, kind) if plac...]
    ppermute x6, waiting for transfers between devices: 8.46 us -> 11.8 us  [per_device(): got_up = lax.ppermute(send_up, 'ctx', upward[first_place:])]
    ppermute x6, waiting for transfers between devices: 17.7 us -> 19.8 us  [per_device(): lax.ppermute(send_down, 'ctx', [(count - 1 - at, count - 2 - at) for at i...]
  transfers between devices with their start and end apart: 21 -> 21, of which waited for: 13 -> 13; matrix products, arithmetic and copies ran while one was open for 0% -> 0% of each run, Pallas kernels for 31% -> 20%
where the time goes in v3:
time: 113 us; the launch traced here: 112 us
  waiting for transfers between devices  41.9 us (37%)
  starting transfers between devices  41.5 us (37%)
  Pallas kernels  26.1 us (23%)
  between operations  2.25 us (2%)
    pallas_call x17, Pallas kernels, call(): pl.pallas_call(body, out_shape=[jax.ShapeDtypeStruct(shape, kind) if plac...  26.1 us
    ppermute x6, waiting for transfers between devices, per_device(): lax.ppermute(send_down, 'ctx', [(count - 1 - at, count - 2 - at) for at i...  19.8 us
    ppermute x6, starting transfers between devices, per_device(): got_up = lax.ppermute(send_up, 'ctx', upward[first_place:])  19.4 us
    ppermute x6, waiting for transfers between devices, per_device(): got_up = lax.ppermute(send_up, 'ctx', upward[first_place:])  11.8 us
    ppermute x6, starting transfers between devices, per_device(): lax.ppermute(send_down, 'ctx', [(count - 1 - at, count - 2 - at) for at i...  7.75 us
    ppermute x3, waiting for transfers between devices, sum_steps(): steps.append(lambda value, group=group: value + group[0](value))  6.86 us
    ppermute x1, starting transfers between devices, per_device(): from_before = lax.ppermute(own_state, 'ctx', upward)  5.58 us
    ppermute x3, starting transfers between devices, per_device(): exchanged = [exchange(total) for exchange in exchanges]  4.39 us
  transfers between devices with their start and end apart: 21, of which 13 were waited for; matrix products, arithmetic and copies ran while one was open for 0% of the time, Pallas kernels for 20%

profile of v3, /device:TPU:0, one launch (start us, length us, event | category | flops | bytes accessed | tf_op | source)
XLA Modules:
  0.0 111.8 jit_solution(9533883083306509617)
XLA Ops:
  1.9 5.6 %collective-permute-start = (f32[4,128,128]{2,1,0:T(8,128)}, f32[4,128,128]{2,1,0:T(8,128)S(1)}, u32[]{:S(2)}, u32[]{:S(2)}) collective-permute-start(f32[4,128,128]{2,1,0:T(8,128)} %bitcast.23), channel_id=1, source_target_pairs={{0,8},{8,16},{16,24},{1,9},{9,17},{17,25},{2,10},{10,18},{18,26},{... | collective-permute-start | bytes 786440 | tf_op jit(solution)/shard_map/ppermute | solution.py:485
  9.0 4.7 %shard_map.163 = (f32[288,512]{1,0:T(8,128)S(1)}, f32[288,512]{1,0:T(8,128)S(1)}, f32[4,8,512]{2,1,0:T(8,128)S(1)}, f32[4,8,512]{2,1,0:T(8,128)S(1)}, f32[4,128,...) custom-call(s32[52]{0:T(128)S(1)} %concatenate.3.meta.refs_0_, ...), custom_call_target="tpu_custom_call" | custom-call | tf_op jit(solution)/shard_map/pallas_call | solution.py:378
  14.4 1.3 %collective-permute-start.3 = (f32[288,512]{1,0:T(8,128)S(1)}, f32[288,512]{1,0:T(8,128)S(1)}, u32[]{:S(2)}, u32[]{:S(2)}) collective-permute-start(f32[288,512]{1,0:T(8,128)S(1)} %get-tuple-element.72), channel_id=1, source_target_pairs={{24,16},{16,8},{8,0},{25,17},{17,9},{9,1},{26,18},{18,10},{10,2},{... | collective-permute-start | bytes 1769480 | tf_op jit(solution)/shard_map/ppermute | solution.py:596
  15.7 4.6 %collective-permute-start.2 = (f32[288,512]{1,0:T(8,128)S(1)}, f32[288,512]{1,0:T(8,128)S(1)}, u32[]{:S(2)}, u32[]{:S(2)}) collective-permute-start(f32[288,512]{1,0:T(8,128)S(1)} %get-tuple-element.68), channel_id=1, source_target_pairs={{0,8},{8,16},{16,24},{1,9},{9,17},{17,25},{2,10},{10,18},{18,26},{... | collective-permute-start | bytes 1769480 | tf_op jit(solution)/shard_map/ppermute | solution.py:599
  20.3 5.1 %shard_map.164 = (f32[4,2,128,512]{3,2,1,0:T(8,128)S(1)}, f32[4,2,128,512]{3,2,1,0:T(8,128)S(1)}, f32[128,2048]{1,0:T(8,128)S(1)}, f32[128,2048]{1,0:T(8,128)S(1...) custom-call(s32[52]{0:T(128)S(1)} %concatenate.3.meta.refs_0_, ...), custom_call_target="tpu_custom_call" | custom-call | tf_op jit(solution)/shard_map/pallas_call | solution.py:378
  26.2 4.9 %collective-permute-done.3.refs_1_ = f32[288,512]{1,0:T(8,128)S(1)} collective-permute-done((f32[288,512]{1,0:T(8,128)S(1)}, f32[288,512]{1,0:T(8,128)S(1)}, u32[]{:S(2)}, u32[]{:S(2)}) %collective-permute-start.3) | collective-permute-done | bytes 589856 | tf_op jit(solution)/shard_map/ppermute | solution.py:596
  31.8 1.3 %collective-permute-start.5 = (f32[288,512]{1,0:T(8,128)S(1)}, f32[288,512]{1,0:T(8,128)S(1)}, u32[]{:S(2)}, u32[]{:S(2)}) collective-permute-start(f32[288,512]{1,0:T(8,128)S(1)} %get-tuple-element.77), channel_id=1, source_target_pairs={{24,16},{16,8},{8,0},{25,17},{17,9},{9,1},{26,18},{18,10},{10,2},{... | collective-permute-start | bytes 1769480 | tf_op jit(solution)/shard_map/ppermute | solution.py:596
  33.8 4.6 %collective-permute-start.4 = (f32[288,512]{1,0:T(8,128)S(1)}, f32[288,512]{1,0:T(8,128)S(1)}, u32[]{:S(2)}, u32[]{:S(2)}) collective-permute-start(f32[288,512]{1,0:T(8,128)S(1)} %get-tuple-element.75), channel_id=1, source_target_pairs={{0,8},{8,16},{16,24},{1,9},{9,17},{17,25},{2,10},{10,18},{18,26},{... | collective-permute-start | bytes 1769480 | tf_op jit(solution)/shard_map/ppermute | solution.py:599
  38.4 9.2 %collective-permute-done.5.refs_1_ = f32[288,512]{1,0:T(8,128)S(1)} collective-permute-done((f32[288,512]{1,0:T(8,128)S(1)}, f32[288,512]{1,0:T(8,128)S(1)}, u32[]{:S(2)}, u32[]{:S(2)}) %collective-permute-start.5) | collective-permute-done | bytes 589856 | tf_op jit(solution)/shard_map/ppermute | solution.py:596
  50.1 4.4 %collective-permute-start.6 = (f32[288,512]{1,0:T(8,128)S(1)}, f32[288,512]{1,0:T(8,128)S(1)}, u32[]{:S(2)}, u32[]{:S(2)}) collective-permute-start(f32[288,512]{1,0:T(8,128)S(1)} %get-tuple-element.81), channel_id=1, source_target_pairs={{0,8},{8,16},{16,24},{1,9},{9,17},{17,25},{2,10},{10,18},{18,26},{... | collective-permute-start | bytes 1769480 | tf_op jit(solution)/shard_map/ppermute | solution.py:599
  55.8 1.4 %collective-permute-start.15 = (f32[5,128,512]{2,1,0:T(8,128)S(1)}, f32[5,128,512]{2,1,0:T(8,128)S(1)}, u32[]{:S(2)}, u32[]{:S(2)}) collective-permute-start(f32[5,128,512]{2,1,0:T(8,128)S(1)} %get-tuple-element.95.begin_here), channel_id=1, source_target_pairs={{0,4},{4,0},{1,5},{5,1},{2,6},{6,2},{3,7},{7,3},{8,12},{12,8},{9,1... | collective-permute-start | bytes 3932168 | tf_op jit(solution)/shard_map/ppermute | solution.py:606
  57.2 7.4 %collective-permute-done.6.refs_1_.earlier = f32[288,512]{1,0:T(8,128)S(1)} collective-permute-done((f32[288,512]{1,0:T(8,128)S(1)}, f32[288,512]{1,0:T(8,128)S(1)}, u32[]{:S(2)}, u32[]{:S(2)}) %collective-permute-start.6) | collective-permute-done | bytes 589856 | tf_op jit(solution)/shard_map/ppermute | solution.py:599
  65.3 4.4 %collective-permute-start.7 = (f32[256,512]{1,0:T(8,128)S(1)}, f32[256,512]{1,0:T(8,128)S(1)}, u32[]{:S(2)}, u32[]{:S(2)}) collective-permute-start(f32[256,512]{1,0:T(8,128)S(1)} %get-tuple-element.83), channel_id=1, source_target_pairs={{0,8},{8,16},{16,24},{1,9},{9,17},{17,25},{2,10},{10,18},{18,26},{... | collective-permute-start | bytes 1572872 | tf_op jit(solution)/shard_map/ppermute | solution.py:599
  70.4 1.3 %collective-permute-start.13 = (f32[256,512]{1,0:T(8,128)S(1)}, f32[256,512]{1,0:T(8,128)S(1)}, u32[]{:S(2)}, u32[]{:S(2)}) collective-permute-start(f32[256,512]{1,0:T(8,128)S(1)} %get-tuple-element.91), channel_id=1, source_target_pairs={{24,16},{16,8},{8,0},{25,17},{17,9},{9,1},{26,18},{18,10},{10,2},{... | collective-permute-start | bytes 1572872 | tf_op jit(solution)/shard_map/ppermute | solution.py:596
  71.7 1.4 %shard_map.172.refs_6_ = f32[8,128]{1,0:T(8,128)S(1)} custom-call(s32[52]{0:T(128)S(1)} %concatenate.3.meta.refs_0_, f32[288,512]{1,0:T(8,128)S(1)} %collective-permute-done.6.refs_1_.earlier, f32[288,512]{1,0:T(8,128)S(1)} %collective-permute-done.8.later.refs_1_, f32[4,8,512]{2,1,0:T(8,128)S(1)} %get-tuple-element.71.refs_3_.refs_4_.small, ...), custom_call_target="tpu_custom_call" | custom-call | tf_op jit(solution)/shard_map/pallas_call | solution.py:378
  74.3 3.2 %collective-permute-done.7.refs_1_ = f32[256,512]{1,0:T(8,128)S(1)} collective-permute-done((f32[256,512]{1,0:T(8,128)S(1)}, f32[256,512]{1,0:T(8,128)S(1)}, u32[]{:S(2)}, u32[]{:S(2)}) %collective-permute-start.7) | collective-permute-done | bytes 524320 | tf_op jit(solution)/shard_map/ppermute | solution.py:599
  78.9 3.4 %collective-permute-done.13.refs_1_ = f32[256,512]{1,0:T(8,128)S(1)} collective-permute-done((f32[256,512]{1,0:T(8,128)S(1)}, f32[256,512]{1,0:T(8,128)S(1)}, u32[]{:S(2)}, u32[]{:S(2)}) %collective-permute-start.13) | collective-permute-done | bytes 524320 | tf_op jit(solution)/shard_map/ppermute | solution.py:596
  85.1 2.9 %collective-permute-done.11 = f32[8,128]{1,0:T(8,128)S(1)} collective-permute-done((f32[8,128]{1,0:T(8,128)S(1)}, f32[8,128]{1,0:T(8,128)S(1)}, u32[]{:S(2)}, u32[]{:S(2)}) %collective-permute-start.11) | collective-permute-done | bytes 4128 | tf_op jit(solution)/shard_map/ppermute | solution.py:424
  88.7 2.8 %collective-permute-done.12 = f32[8,128]{1,0:T(8,128)S(1)} collective-permute-done((f32[8,128]{1,0:T(8,128)S(1)}, f32[8,128]{1,0:T(8,128)S(1)}, u32[]{:S(2)}, u32[]{:S(2)}) %collective-permute-start.12) | collective-permute-done | bytes 4128 | tf_op jit(solution)/shard_map/ppermute | solution.py:424
  92.9 2.3 %collective-permute-done.14.refs_1_ = f32[256,512]{1,0:T(8,128)S(1)} collective-permute-done((f32[256,512]{1,0:T(8,128)S(1)}, f32[256,512]{1,0:T(8,128)S(1)}, u32[]{:S(2)}, u32[]{:S(2)}) %collective-permute-start.14) | collective-permute-done | bytes 524320 | tf_op jit(solution)/shard_map/ppermute | solution.py:596
  97.1 4.3 %shard_map.178 = (bf16[128,2048]{1,0:T(8,128)(2,1)}, bf16[128,2048]{1,0:T(8,128)(2,1)}, f32[128,128]{1,0:T(8,128)S(1)}, f32[128,128]{1,0:T(8,128)S(1)}, f32[8,128]{1,0:T(8,128)S(1)}) custom-call(s32[52]{0:T(128)S(1)} %concatenate.3.meta.refs_0_, f32[16]{0:T(128)S(1)} %copy-done.1, ...), custom_call_target="tpu_custom_call", output_to_operand_aliasing={{4}: (16, {})} | custom-call | tf_op jit(solution)/shard_map/pallas_call | solution.py:378
  102.5 3.1 %collective-permute-start.19 = (f32[8,128]{1,0:T(8,128)S(1)}, f32[8,128]{1,0:T(8,128)S(1)}, u32[]{:S(2)}, u32[]{:S(2)}) collective-permute-start(f32[8,128]{1,0:T(8,128)S(1)} %get-tuple-element.103.refs_2_), channel_id=1, source_target_pairs={{0,16},{8,24},{16,0},{24,8},{1,17},{9,25},{17,1},{25,9},{2,18},{10... | collective-permute-start | bytes 12296 | tf_op jit(solution)/shard_map/ppermute | solution.py:678
  107.2 2.0 %collective-permute-done.18.refs_3_ = f32[8,128]{1,0:T(8,128)S(1)} collective-permute-done((f32[8,128]{1,0:T(8,128)S(1)}, f32[8,128]{1,0:T(8,128)S(1)}, u32[]{:S(2)}, u32[]{:S(2)}) %collective-permute-start.18) | collective-permute-done | bytes 4128 | tf_op jit(solution)/shard_map/ppermute | solution.py:678
  109.2 2.7 %shard_map.179 = (bf16[128,2048]{1,0:T(8,128)(2,1)}, bf16[128,2048]{1,0:T(8,128)(2,1)}, bf16[128,128]{1,0:T(8,128)(2,1)}, bf16[128,128]{1,0:T(8,128)(2,1)}, f32[4,128]{1,0:T(4,128)}, /*index=5*/f32[1,16]{1,0:T(1,128)}) custom-call(s32[52]{0:T(128)S(1)} %concatenate.3.meta.refs_0_, f32[16]{0:T(128)S(1)} %copy-done.1, ...), custom_call_target="tpu_custom_call", output_to_operand_aliasing={{0}: (18, {}), {1}: (19, {})} | custom-call | tf_op jit(solution)/shard_map/pallas_call | solution.py:378
  (47 shorter events, 21.2 us)
Async XLA Ops:
  0.6 13.1 %collective-permute-start.1 = (f32[4,128,128]{2,1,0:T(8,128)}, f32[4,128,128]{2,1,0:T(8,128)S(1)}, u32[]{:S(2)}, u32[]{:S(2)}) collective-permute-start(f32[4,128,128]{2,1,0:T(8,128)} %bitcast.22), channel_id=1, source_target_pairs={{8,0},{16,8},{24,16},{9,1},{17,9},{25,17},{10,2},{18,10},{26,18},{... | collective-permute-start | bytes 786440 | tf_op jit(solution)/shard_map/ppermute | solution.py:486
  1.9 11.8 %collective-permute-start = (f32[4,128,128]{2,1,0:T(8,128)}, f32[4,128,128]{2,1,0:T(8,128)S(1)}, u32[]{:S(2)}, u32[]{:S(2)}) collective-permute-start(f32[4,128,128]{2,1,0:T(8,128)} %bitcast.23), channel_id=1, source_target_pairs={{0,8},{8,16},{16,24},{1,9},{9,17},{17,25},{2,10},{10,18},{18,26},{... | collective-permute-start | bytes 786440 | tf_op jit(solution)/shard_map/ppermute | solution.py:485
  13.8 11.7 %copy-start = (f32[1,1,4,128,128]{4,3,2,1,0:T(8,128)S(1)}, f32[1,1,4,128,128]{4,3,2,1,0:T(8,128)}, u32[]{:S(2)}) copy-start(f32[1,1,4,128,128]{4,3,2,1,0:T(8,128)} %param.20) | copy-start | bytes 786436
  14.4 16.7 %collective-permute-start.3 = (f32[288,512]{1,0:T(8,128)S(1)}, f32[288,512]{1,0:T(8,128)S(1)}, u32[]{:S(2)}, u32[]{:S(2)}) collective-permute-start(f32[288,512]{1,0:T(8,128)S(1)} %get-tuple-element.72), channel_id=1, source_target_pairs={{24,16},{16,8},{8,0},{25,17},{17,9},{9,1},{26,18},{18,10},{10,2},{... | collective-permute-start | bytes 1769480 | tf_op jit(solution)/shard_map/ppermute | solution.py:596
  15.7 17.4 %collective-permute-start.2 = (f32[288,512]{1,0:T(8,128)S(1)}, f32[288,512]{1,0:T(8,128)S(1)}, u32[]{:S(2)}, u32[]{:S(2)}) collective-permute-start(f32[288,512]{1,0:T(8,128)S(1)} %get-tuple-element.68), channel_id=1, source_target_pairs={{0,8},{8,16},{16,24},{1,9},{9,17},{17,25},{2,10},{10,18},{18,26},{... | collective-permute-start | bytes 1769480 | tf_op jit(solution)/shard_map/ppermute | solution.py:599
  31.8 15.8 %collective-permute-start.5 = (f32[288,512]{1,0:T(8,128)S(1)}, f32[288,512]{1,0:T(8,128)S(1)}, u32[]{:S(2)}, u32[]{:S(2)}) collective-permute-start(f32[288,512]{1,0:T(8,128)S(1)} %get-tuple-element.77), channel_id=1, source_target_pairs={{24,16},{16,8},{8,0},{25,17},{17,9},{9,1},{26,18},{18,10},{10,2},{... | collective-permute-start | bytes 1769480 | tf_op jit(solution)/shard_map/ppermute | solution.py:596
  33.8 15.7 %collective-permute-start.4 = (f32[288,512]{1,0:T(8,128)S(1)}, f32[288,512]{1,0:T(8,128)S(1)}, u32[]{:S(2)}, u32[]{:S(2)}) collective-permute-start(f32[288,512]{1,0:T(8,128)S(1)} %get-tuple-element.75), channel_id=1, source_target_pairs={{0,8},{8,16},{16,24},{1,9},{9,17},{17,25},{2,10},{10,18},{18,26},{... | collective-permute-start | bytes 1769480 | tf_op jit(solution)/shard_map/ppermute | solution.py:599
  50.1 14.6 %collective-permute-start.6 = (f32[288,512]{1,0:T(8,128)S(1)}, f32[288,512]{1,0:T(8,128)S(1)}, u32[]{:S(2)}, u32[]{:S(2)}) collective-permute-start(f32[288,512]{1,0:T(8,128)S(1)} %get-tuple-element.81), channel_id=1, source_target_pairs={{0,8},{8,16},{16,24},{1,9},{9,17},{17,25},{2,10},{10,18},{18,26},{... | collective-permute-start | bytes 1769480 | tf_op jit(solution)/shard_map/ppermute | solution.py:599
  54.5 15.2 %collective-permute-start.8 = (f32[288,512]{1,0:T(8,128)S(1)}, f32[288,512]{1,0:T(8,128)S(1)}, u32[]{:S(2)}, u32[]{:S(2)}) collective-permute-start(f32[288,512]{1,0:T(8,128)S(1)} %get-tuple-element.85), channel_id=1, source_target_pairs={{24,16},{16,8},{8,0},{25,17},{17,9},{9,1},{26,18},{18,10},{10,2},{... | collective-permute-start | bytes 1769480 | tf_op jit(solution)/shard_map/ppermute | solution.py:596
  55.8 37.1 %collective-permute-start.15 = (f32[5,128,512]{2,1,0:T(8,128)S(1)}, f32[5,128,512]{2,1,0:T(8,128)S(1)}, u32[]{:S(2)}, u32[]{:S(2)}) collective-permute-start(f32[5,128,512]{2,1,0:T(8,128)S(1)} %get-tuple-element.95.begin_here), channel_id=1, source_target_pairs={{0,4},{4,0},{1,5},{5,1},{2,6},{6,2},{3,7},{7,3},{8,12},{12,8},{9,1... | collective-permute-start | bytes 3932168 | tf_op jit(solution)/shard_map/ppermute | solution.py:606
  65.3 12.2 %collective-permute-start.7 = (f32[256,512]{1,0:T(8,128)S(1)}, f32[256,512]{1,0:T(8,128)S(1)}, u32[]{:S(2)}, u32[]{:S(2)}) collective-permute-start(f32[256,512]{1,0:T(8,128)S(1)} %get-tuple-element.83), channel_id=1, source_target_pairs={{0,8},{8,16},{16,24},{1,9},{9,17},{17,25},{2,10},{10,18},{18,26},{... | collective-permute-start | bytes 1572872 | tf_op jit(solution)/shard_map/ppermute | solution.py:599
  70.4 12.0 %collective-permute-start.13 = (f32[256,512]{1,0:T(8,128)S(1)}, f32[256,512]{1,0:T(8,128)S(1)}, u32[]{:S(2)}, u32[]{:S(2)}) collective-permute-start(f32[256,512]{1,0:T(8,128)S(1)} %get-tuple-element.91), channel_id=1, source_target_pairs={{24,16},{16,8},{8,0},{25,17},{17,9},{9,1},{26,18},{18,10},{10,2},{... | collective-permute-start | bytes 1572872 | tf_op jit(solution)/shard_map/ppermute | solution.py:596
  73.1 1.2 %collective-permute-start.9 = (f32[8,128]{1,0:T(8,128)S(1)}, f32[8,128]{1,0:T(8,128)S(1)}, u32[]{:S(2)}, u32[]{:S(2)}) collective-permute-start(f32[8,128]{1,0:T(8,128)S(1)} %shard_map.172.refs_6_), channel_id=1, source_target_pairs={{0,1},{1,0},{2,3},{3,2},{4,5},{5,4},{6,7},{7,6},{8,9},{9,8},{10,11... | collective-permute-start | bytes 12296 | tf_op jit(solution)/shard_map/ppermute | solution.py:424
  78.2 13.4 %collective-permute-start.10 = (f32[256,512]{1,0:T(8,128)S(1)}, f32[256,512]{1,0:T(8,128)S(1)}, u32[]{:S(2)}, u32[]{:S(2)}) collective-permute-start(f32[256,512]{1,0:T(8,128)S(1)} %get-tuple-element.87), channel_id=1, source_target_pairs={{8,16},{16,24},{9,17},{17,25},{10,18},{18,26},{11,19},{19,27},{12,... | collective-permute-start | bytes 1572872 | tf_op jit(solution)/shard_map/ppermute | solution.py:599
  83.0 12.2 %collective-permute-start.14 = (f32[256,512]{1,0:T(8,128)S(1)}, f32[256,512]{1,0:T(8,128)S(1)}, u32[]{:S(2)}, u32[]{:S(2)}) collective-permute-start(f32[256,512]{1,0:T(8,128)S(1)} %get-tuple-element.93), channel_id=1, source_target_pairs={{16,8},{8,0},{17,9},{9,1},{18,10},{10,2},{19,11},{11,3},{20,12},{1... | collective-permute-start | bytes 1572872 | tf_op jit(solution)/shard_map/ppermute | solution.py:596
  84.3 3.7 %collective-permute-start.11 = (f32[8,128]{1,0:T(8,128)S(1)}, f32[8,128]{1,0:T(8,128)S(1)}, u32[]{:S(2)}, u32[]{:S(2)}) collective-permute-start(f32[8,128]{1,0:T(8,128)S(1)} %add.47.refs_6_), channel_id=1, source_target_pairs={{0,2},{1,3},{2,0},{3,1},{4,6},{5,7},{6,4},{7,5},{8,10},{9,11},{10,... | collective-permute-start | bytes 12296 | tf_op jit(solution)/shard_map/ppermute | solution.py:424
  87.9 3.6 %collective-permute-start.12 = (f32[8,128]{1,0:T(8,128)S(1)}, f32[8,128]{1,0:T(8,128)S(1)}, u32[]{:S(2)}, u32[]{:S(2)}) collective-permute-start(f32[8,128]{1,0:T(8,128)S(1)} %add.48.refs_7_), channel_id=1, source_target_pairs={{0,4},{4,0},{1,5},{5,1},{2,6},{6,2},{3,7},{7,3},{8,12},{12,8},{9,1... | collective-permute-start | bytes 12296 | tf_op jit(solution)/shard_map/ppermute | solution.py:424
  92.2 16.9 %collective-permute-start.16 = (f32[256,512]{1,0:T(8,128)S(1)}, f32[256,512]{1,0:T(8,128)S(1)}, u32[]{:S(2)}, u32[]{:S(2)}) collective-permute-start(f32[256,512]{1,0:T(8,128)S(1)} %get-tuple-element.99), channel_id=1, source_target_pairs={{16,24},{17,25},{18,26},{19,27},{20,28},{21,29},{22,30},{23,31}} | collective-permute-start | bytes 1572872 | tf_op jit(solution)/shard_map/ppermute | solution.py:599
  95.2 1.9 %copy-start.1 = (f32[16]{0:T(128)S(1)}, f32[16]{0:T(128)}, u32[]{:S(2)}) copy-start(f32[16]{0:T(128)} %gains.3) | copy-start | bytes 196
  95.8 13.3 %collective-permute-start.17 = (f32[256,512]{1,0:T(8,128)S(1)}, f32[256,512]{1,0:T(8,128)S(1)}, u32[]{:S(2)}, u32[]{:S(2)}) collective-permute-start(f32[256,512]{1,0:T(8,128)S(1)} %get-tuple-element.100), channel_id=1, source_target_pairs={{8,0},{9,1},{10,2},{11,3},{12,4},{13,5},{14,6},{15,7}} | collective-permute-start | bytes 1572872 | tf_op jit(solution)/shard_map/ppermute | solution.py:596
  101.4 5.5 %collective-permute-start.20 = (f32[8,128]{1,0:T(8,128)S(1)}, f32[8,128]{1,0:T(8,128)S(1)}, u32[]{:S(2)}, u32[]{:S(2)}) collective-permute-start(f32[8,128]{1,0:T(8,128)S(1)} %get-tuple-element.103.refs_2_), channel_id=1, source_target_pairs={{0,24},{8,16},{16,8},{24,0},{1,25},{9,17},{17,9},{25,1},{2,26},{10... | collective-permute-start | bytes 12296 | tf_op jit(solution)/shard_map/ppermute | solution.py:678
  102.5 4.7 %collective-permute-start.19 = (f32[8,128]{1,0:T(8,128)S(1)}, f32[8,128]{1,0:T(8,128)S(1)}, u32[]{:S(2)}, u32[]{:S(2)}) collective-permute-start(f32[8,128]{1,0:T(8,128)S(1)} %get-tuple-element.103.refs_2_), channel_id=1, source_target_pairs={{0,16},{8,24},{16,0},{24,8},{1,17},{9,25},{17,1},{25,9},{2,18},{10... | collective-permute-start | bytes 12296 | tf_op jit(solution)/shard_map/ppermute | solution.py:678
  105.5 3.6 %collective-permute-start.18 = (f32[8,128]{1,0:T(8,128)S(1)}, f32[8,128]{1,0:T(8,128)S(1)}, u32[]{:S(2)}, u32[]{:S(2)}) collective-permute-start(f32[8,128]{1,0:T(8,128)S(1)} %get-tuple-element.103.refs_2_), channel_id=1, source_target_pairs={{0,8},{8,0},{16,24},{24,16},{1,9},{9,1},{17,25},{25,17},{2,10},{10... | collective-permute-start | bytes 12296 | tf_op jit(solution)/shard_map/ppermute | solution.py:678

commit v4 on v3

--- a/solution.py
+++ b/solution.py
@@ -133,12 +133,24 @@
     ]
 
 
-def relay_kernel(last, meta, from_before, from_after, up_old, down_old, up, down, sems):
-    del up_old, down_old
-    for at, (source, target) in enumerate(((from_before, up), (from_after, down))):
-        copies = head_copies(source, target, 0, sems.at[at])
-
-        @pl.when(meta[2] != (0, last)[at])
+def relay_kernel(last, paired, meta, *refs):
+    sources, (up, down, sems) = refs[:-5], refs[-3:]
+    if paired:
+        plans = [
+            (meta[2] == target, message, pieces)
+            for target, message, pieces in ((1, up, sources), (2, down, sources))
+        ]
+    else:
+        plans = [
+            (meta[2] != (0, last)[at], message, sources[at : at + 1])
+            for at, message in enumerate((up, down))
+        ]
+    for at, (wanted, message, pieces) in enumerate(plans):
+        copies = []
+        for half, source in enumerate(pieces):
+            copies += head_copies(source, message, half * source.shape[1], sems.at[at, half])
+
+        @pl.when(wanted)
         def _():
             for copy in copies:
                 copy.start()
@@ -146,15 +158,15 @@
                 copy.wait()
 
 
-def gather_kernel(last, meta, own, from_before, from_after, begin, sems):
+def gather_kernel(last, paired, meta, *refs):
+    sources, begin, sems = refs[:-2], refs[-2], refs[-1]
     place = meta[2]
-    trash = last + 1
+    if paired:
+        rows = (lax.bitwise_xor(place, 1), place)
+    else:
+        rows = (jnp.where(place == 0, last + 1, place - 1), place + 1, place)
     copies = []
-    for at, (source, row) in enumerate((
-        (own, place),
-        (from_before, jnp.where(place == 0, trash, place - 1)),
-        (from_after, place + 1),
-    )):
+    for at, (source, row) in enumerate(zip(sources, rows, strict=True)):
         copies += head_copies(source, begin.at[row], 0, sems.at[at])
     for copy in copies:
         copy.start()
@@ -167,10 +179,11 @@
     send, held = refs[-3:-1] if has_begin else refs[-2:]
     del waits
     state = own.shape[2]
-    land, source, forward, piece = (at + slot for at in tables)
+    land, source, forward, piece, other = (at + slot for at in tables)
     if has_begin:
         begin = refs[-1]
         begin[meta[piece]] = received[0:state, 0 : begin.shape[2]]
+        begin[meta[other]] = received[state : 2 * state, 0 : begin.shape[2]]
     held[meta[land]] = received[0 : 2 * state, :].astype(BF16)
     passing = meta[forward] != 0
     decay = jnp.where(passing, 1.0, decays[meta[source], vocab : vocab + 1, :])
@@ -447,6 +460,7 @@
     total_scale = 1.0 / math.sqrt(total_rows)
     lines = -(-(vocab + 2) // 8) * 8
     slots = chunks + count - 2
+    paired = count == 4
 
     hid = hidden.reshape(length, width)
     cot = cotangent.reshape(length, width)
@@ -464,14 +478,20 @@
     for far, toward in ((place, -1), (from_last, 1)):
         lands = times - jnp.maximum(far, 1) + 1
         pieces = place + toward * (times + 2)
+        others = jnp.full_like(times, count)
+        if paired:
+            arrives = times + 2 == far
+            pieces = jnp.where(arrives, 0 if toward < 0 else 3, count)
+            others = jnp.where(arrives, 1 if toward < 0 else 2, count)
         table_of.append(jnp.where((lands >= 0) & (lands < chunks), lands, chunks))
         table_of.append(jnp.clip(times + 1 - far, 0, chunks - 1))
         table_of.append((times + 1 < far).astype(jnp.int32))
         table_of.append(jnp.where((pieces >= 0) & (pieces < count), pieces, count))
-    base = jnp.stack([place * length, suffix_start[0], place, here]).astype(jnp.int32)
-    meta = jnp.concatenate([base] + table_of)
-    up_tables = [4 + at * slots for at in range(4)]
-    down_tables = [4 + at * slots for at in range(4, 8)]
+        table_of.append(others)
+    base = [place * length, suffix_start[0], place, here]
+    meta = jnp.concatenate([jnp.stack(base).astype(jnp.int32)] + table_of)
+    up_tables = [4 + at * slots for at in range(5)]
+    down_tables = [4 + at * slots for at in range(5, 10)]
 
     upward = [(at, at + 1) for at in range(count - 1)]
     downward = [(at + 1, at) for at in range(count - 1)]
@@ -482,8 +502,11 @@
         own_state = lax.dynamic_index_in_dim(
             lax.all_gather(own_state, "dom"), ancestor, 0, keepdims=False
         )
-    from_before = lax.ppermute(own_state, "ctx", upward)
-    from_after = lax.ppermute(own_state, "ctx", downward)
+    if paired:
+        swap = [(at, at ^ 1) for at in range(count)]
+        pieces = [lax.ppermute(own_state, "ctx", swap), own_state]
+    else:
+        pieces = [lax.ppermute(own_state, "ctx", way) for way in (upward, downward)]
 
     anywhere = pl.BlockSpec(memory_space=pl.ANY)
     near = pl.BlockSpec(memory_space=pltpu.VMEM)
@@ -515,25 +538,22 @@
     )
 
     up_first, down_first = call(
-        functools.partial(relay_kernel, count - 1),
+        functools.partial(relay_kernel, count - 1, paired),
+        (meta,), (),
+        [(piece, anywhere, None) for piece in pieces]
+        + [(up_first, near, CHIP), (down_first, near, CHIP)],
+        [
+            ((full_rows, part), F32, near, CHIP), ((full_rows, part), F32, near, CHIP),
+        ],
+        [pltpu.SemaphoreType.DMA((2, 2, local_heads))],
+        aliases={3: 0, 4: 1},
+    )
+    begin_shape = (count + 1, head_dim, local_heads * state_dim)
+    (begin_here,) = call(
+        functools.partial(gather_kernel, count - 1, paired),
         (meta,), (),
         [
-            (from_before, anywhere, None), (from_after, anywhere, None),
-            (up_first, near, CHIP), (down_first, near, CHIP),
-        ],
-        [
-            ((full_rows, part), F32, near, CHIP), ((full_rows, part), F32, near, CHIP),
-        ],
-        [pltpu.SemaphoreType.DMA((2, local_heads))],
-        aliases={3: 0, 4: 1},
-    )
-    begin_shape = (count + 1, head_dim, local_heads * state_dim)
-    (begin_here,) = call(
-        functools.partial(gather_kernel, count - 1),
-        (meta,), (),
-        [
-            (own_state, anywhere, None), (from_before, anywhere, None),
-            (from_after, anywhere, None),
+            (piece, anywhere, None) for piece in (pieces if paired else pieces + [own_state])
         ],
         [(begin_shape, F32, near, CHIP)],
         [pltpu.SemaphoreType.DMA((3, local_heads))],

time: 113 us -> 108 us (0.956)
  starting transfers between devices: 41.5 us -> 38.1 us
    ppermute x2 -> x1, starting transfers between devices: 6.87 us -> 3.09 us  [per_device(): pieces = [lax.ppermute(own_state, 'ctx', swap), own_state]]
  transfers between devices with their start and end apart: 21 -> 20, of which waited for: 13 -> 14; matrix products, arithmetic and copies ran while one was open for 0% -> 0% of each run, Pallas kernels for 20% -> 21%
where the time goes in v4:
time: 108 us; the launch traced here: 107 us
  waiting for transfers between devices  41 us (38%)
  starting transfers between devices  38.1 us (35%)
  Pallas kernels  26.1 us (24%)
  between operations  2.21 us (2%)
    pallas_call x17, Pallas kernels, call(): pl.pallas_call(body, out_shape=[jax.ShapeDtypeStruct(shape, kind) if plac...  26.1 us
    ppermute x6, waiting for transfers between devices, per_device(): lax.ppermute(send_down, 'ctx', [(count - 1 - at, count - 2 - at) for at i...  19.6 us
    ppermute x6, starting transfers between devices, per_device(): got_up = lax.ppermute(send_up, 'ctx', upward[first_place:])  19.4 us
    ppermute x6, waiting for transfers between devices, per_device(): got_up = lax.ppermute(send_up, 'ctx', upward[first_place:])  11.3 us
    ppermute x6, starting transfers between devices, per_device(): lax.ppermute(send_down, 'ctx', [(count - 1 - at, count - 2 - at) for at i...  7.75 us
    ppermute x3, waiting for transfers between devices, sum_steps(): steps.append(lambda value, group=group: value + group[0](value))  6.43 us
    ppermute x3, starting transfers between devices, per_device(): exchanged = [exchange(total) for exchange in exchanges]  4.39 us
    ppermute x3, waiting for transfers between devices, per_device(): exchanged = [exchange(total) for exchange in exchanges]  3.35 us
  transfers between devices with their start and end apart: 20, of which 14 were waited for; matrix products, arithmetic and copies ran while one was open for 0% of the time, Pallas kernels for 21%

profile of v4, /device:TPU:0, one launch (start us, length us, event | category | flops | bytes accessed | tf_op | source)
XLA Modules:
  0.0 107.5 jit_solution(5768150644266620674)
XLA Ops:
  0.6 3.1 %collective-permute-start = (f32[4,128,128]{2,1,0:T(8,128)}, f32[4,128,128]{2,1,0:T(8,128)S(1)}, u32[]{:S(2)}, u32[]{:S(2)}) collective-permute-start(f32[4,128,128]{2,1,0:T(8,128)} %bitcast.22), channel_id=1, source_target_pairs={{0,8},{8,0},{16,24},{24,16},{1,9},{9,1},{17,25},{25,17},{2,10},{10... | collective-permute-start | bytes 786440 | tf_op jit(solution)/shard_map/ppermute | solution.py:507
  5.2 4.7 %shard_map.163 = (f32[288,512]{1,0:T(8,128)S(1)}, f32[288,512]{1,0:T(8,128)S(1)}, f32[4,8,512]{2,1,0:T(8,128)S(1)}, f32[4,8,512]{2,1,0:T(8,128)S(1)}, f32[4,128,...) custom-call(s32[64]{0:T(128)S(1)} %concatenate.3.meta.refs_0_, ...), custom_call_target="tpu_custom_call" | custom-call | tf_op jit(solution)/shard_map/pallas_call | solution.py:391
  12.3 4.6 %collective-permute-start.1 = (f32[288,512]{1,0:T(8,128)S(1)}, f32[288,512]{1,0:T(8,128)S(1)}, u32[]{:S(2)}, u32[]{:S(2)}) collective-permute-start(f32[288,512]{1,0:T(8,128)S(1)} %get-tuple-element.68), channel_id=1, source_target_pairs={{0,8},{8,16},{16,24},{1,9},{9,17},{17,25},{2,10},{10,18},{18,26},{... | collective-permute-start | bytes 1769480 | tf_op jit(solution)/shard_map/ppermute | solution.py:619
  16.8 5.1 %shard_map.164 = (f32[4,2,128,512]{3,2,1,0:T(8,128)S(1)}, f32[4,2,128,512]{3,2,1,0:T(8,128)S(1)}, f32[128,2048]{1,0:T(8,128)S(1)}, f32[128,2048]{1,0:T(8,128)S(1...) custom-call(s32[64]{0:T(128)S(1)} %concatenate.3.meta.refs_0_, ...), custom_call_target="tpu_custom_call" | custom-call | tf_op jit(solution)/shard_map/pallas_call | solution.py:391
  22.7 4.7 %collective-permute-done.2.refs_1_ = f32[288,512]{1,0:T(8,128)S(1)} collective-permute-done((f32[288,512]{1,0:T(8,128)S(1)}, f32[288,512]{1,0:T(8,128)S(1)}, u32[]{:S(2)}, u32[]{:S(2)}) %collective-permute-start.2) | collective-permute-done | bytes 589856 | tf_op jit(solution)/shard_map/ppermute | solution.py:616
  28.0 1.3 %collective-permute-start.4 = (f32[288,512]{1,0:T(8,128)S(1)}, f32[288,512]{1,0:T(8,128)S(1)}, u32[]{:S(2)}, u32[]{:S(2)}) collective-permute-start(f32[288,512]{1,0:T(8,128)S(1)} %get-tuple-element.77), channel_id=1, source_target_pairs={{24,16},{16,8},{8,0},{25,17},{17,9},{9,1},{26,18},{18,10},{10,2},{... | collective-permute-start | bytes 1769480 | tf_op jit(solution)/shard_map/ppermute | solution.py:616
  30.0 4.6 %collective-permute-start.3 = (f32[288,512]{1,0:T(8,128)S(1)}, f32[288,512]{1,0:T(8,128)S(1)}, u32[]{:S(2)}, u32[]{:S(2)}) collective-permute-start(f32[288,512]{1,0:T(8,128)S(1)} %get-tuple-element.75), channel_id=1, source_target_pairs={{0,8},{8,16},{16,24},{1,9},{9,17},{17,25},{2,10},{10,18},{18,26},{... | collective-permute-start | bytes 1769480 | tf_op jit(solution)/shard_map/ppermute | solution.py:619
  34.6 8.9 %collective-permute-done.4.refs_1_ = f32[288,512]{1,0:T(8,128)S(1)} collective-permute-done((f32[288,512]{1,0:T(8,128)S(1)}, f32[288,512]{1,0:T(8,128)S(1)}, u32[]{:S(2)}, u32[]{:S(2)}) %collective-permute-start.4) | collective-permute-done | bytes 589856 | tf_op jit(solution)/shard_map/ppermute | solution.py:616
  46.0 4.4 %collective-permute-start.5 = (f32[288,512]{1,0:T(8,128)S(1)}, f32[288,512]{1,0:T(8,128)S(1)}, u32[]{:S(2)}, u32[]{:S(2)}) collective-permute-start(f32[288,512]{1,0:T(8,128)S(1)} %get-tuple-element.81), channel_id=1, source_target_pairs={{0,8},{8,16},{16,24},{1,9},{9,17},{17,25},{2,10},{10,18},{18,26},{... | collective-permute-start | bytes 1769480 | tf_op jit(solution)/shard_map/ppermute | solution.py:619
  51.8 1.4 %collective-permute-start.14 = (f32[5,128,512]{2,1,0:T(8,128)S(1)}, f32[5,128,512]{2,1,0:T(8,128)S(1)}, u32[]{:S(2)}, u32[]{:S(2)}) collective-permute-start(f32[5,128,512]{2,1,0:T(8,128)S(1)} %get-tuple-element.95.begin_here), channel_id=1, source_target_pairs={{0,4},{4,0},{1,5},{5,1},{2,6},{6,2},{3,7},{7,3},{8,12},{12,8},{9,1... | collective-permute-start | bytes 3932168 | tf_op jit(solution)/shard_map/ppermute | solution.py:626
  53.2 7.2 %collective-permute-done.5.refs_1_.earlier = f32[288,512]{1,0:T(8,128)S(1)} collective-permute-done((f32[288,512]{1,0:T(8,128)S(1)}, f32[288,512]{1,0:T(8,128)S(1)}, u32[]{:S(2)}, u32[]{:S(2)}) %collective-permute-start.5) | collective-permute-done | bytes 589856 | tf_op jit(solution)/shard_map/ppermute | solution.py:619
  61.0 4.4 %collective-permute-start.6 = (f32[256,512]{1,0:T(8,128)S(1)}, f32[256,512]{1,0:T(8,128)S(1)}, u32[]{:S(2)}, u32[]{:S(2)}) collective-permute-start(f32[256,512]{1,0:T(8,128)S(1)} %get-tuple-element.83), channel_id=1, source_target_pairs={{0,8},{8,16},{16,24},{1,9},{9,17},{17,25},{2,10},{10,18},{18,26},{... | collective-permute-start | bytes 1572872 | tf_op jit(solution)/shard_map/ppermute | solution.py:619
  66.0 1.3 %collective-permute-start.12 = (f32[256,512]{1,0:T(8,128)S(1)}, f32[256,512]{1,0:T(8,128)S(1)}, u32[]{:S(2)}, u32[]{:S(2)}) collective-permute-start(f32[256,512]{1,0:T(8,128)S(1)} %get-tuple-element.91), channel_id=1, source_target_pairs={{24,16},{16,8},{8,0},{25,17},{17,9},{9,1},{26,18},{18,10},{10,2},{... | collective-permute-start | bytes 1572872 | tf_op jit(solution)/shard_map/ppermute | solution.py:616
  67.3 1.4 %shard_map.172.refs_6_ = f32[8,128]{1,0:T(8,128)S(1)} custom-call(s32[64]{0:T(128)S(1)} %concatenate.3.meta.refs_0_, f32[288,512]{1,0:T(8,128)S(1)} %collective-permute-done.5.refs_1_.earlier, f32[288,512]{1,0:T(8,128)S(1)} %collective-permute-done.7.later.refs_1_, f32[4,8,512]{2,1,0:T(8,128)S(1)} %get-tuple-element.71.refs_3_.refs_4_.small, ...), custom_call_target="tpu_custom_call" | custom-call | tf_op jit(solution)/shard_map/pallas_call | solution.py:391
  70.0 2.9 %collective-permute-done.6.refs_1_ = f32[256,512]{1,0:T(8,128)S(1)} collective-permute-done((f32[256,512]{1,0:T(8,128)S(1)}, f32[256,512]{1,0:T(8,128)S(1)}, u32[]{:S(2)}, u32[]{:S(2)}) %collective-permute-start.6) | collective-permute-done | bytes 524320 | tf_op jit(solution)/shard_map/ppermute | solution.py:619
  74.3 3.4 %collective-permute-done.12.refs_1_ = f32[256,512]{1,0:T(8,128)S(1)} collective-permute-done((f32[256,512]{1,0:T(8,128)S(1)}, f32[256,512]{1,0:T(8,128)S(1)}, u32[]{:S(2)}, u32[]{:S(2)}) %collective-permute-start.12) | collective-permute-done | bytes 524320 | tf_op jit(solution)/shard_map/ppermute | solution.py:616
  80.7 2.7 %collective-permute-done.10 = f32[8,128]{1,0:T(8,128)S(1)} collective-permute-done((f32[8,128]{1,0:T(8,128)S(1)}, f32[8,128]{1,0:T(8,128)S(1)}, u32[]{:S(2)}, u32[]{:S(2)}) %collective-permute-start.10) | collective-permute-done | bytes 4128 | tf_op jit(solution)/shard_map/ppermute | solution.py:437
  84.3 2.6 %collective-permute-done.11 = f32[8,128]{1,0:T(8,128)S(1)} collective-permute-done((f32[8,128]{1,0:T(8,128)S(1)}, f32[8,128]{1,0:T(8,128)S(1)}, u32[]{:S(2)}, u32[]{:S(2)}) %collective-permute-start.11) | collective-permute-done | bytes 4128 | tf_op jit(solution)/shard_map/ppermute | solution.py:437
  88.3 2.6 %collective-permute-done.13.refs_1_ = f32[256,512]{1,0:T(8,128)S(1)} collective-permute-done((f32[256,512]{1,0:T(8,128)S(1)}, f32[256,512]{1,0:T(8,128)S(1)}, u32[]{:S(2)}, u32[]{:S(2)}) %collective-permute-start.13) | collective-permute-done | bytes 524320 | tf_op jit(solution)/shard_map/ppermute | solution.py:616
  92.8 4.3 %shard_map.178 = (bf16[128,2048]{1,0:T(8,128)(2,1)}, bf16[128,2048]{1,0:T(8,128)(2,1)}, f32[128,128]{1,0:T(8,128)S(1)}, f32[128,128]{1,0:T(8,128)S(1)}, f32[8,128]{1,0:T(8,128)S(1)}) custom-call(s32[64]{0:T(128)S(1)} %concatenate.3.meta.refs_0_, f32[16]{0:T(128)S(1)} %copy-done.1, ...), custom_call_target="tpu_custom_call", output_to_operand_aliasing={{4}: (16, {})} | custom-call | tf_op jit(solution)/shard_map/pallas_call | solution.py:391
  97.1 1.5 %collective-permute-start.19 = (f32[8,128]{1,0:T(8,128)S(1)}, f32[8,128]{1,0:T(8,128)S(1)}, u32[]{:S(2)}, u32[]{:S(2)}) collective-permute-start(f32[8,128]{1,0:T(8,128)S(1)} %get-tuple-element.103.refs_2_), channel_id=1, source_target_pairs={{0,24},{8,16},{16,8},{24,0},{1,25},{9,17},{17,9},{25,1},{2,26},{10... | collective-permute-start | bytes 12296 | tf_op jit(solution)/shard_map/ppermute | solution.py:698
  98.5 2.7 %collective-permute-start.18 = (f32[8,128]{1,0:T(8,128)S(1)}, f32[8,128]{1,0:T(8,128)S(1)}, u32[]{:S(2)}, u32[]{:S(2)}) collective-permute-start(f32[8,128]{1,0:T(8,128)S(1)} %get-tuple-element.103.refs_2_), channel_id=1, source_target_pairs={{0,16},{8,24},{16,0},{24,8},{1,17},{9,25},{17,1},{25,9},{2,18},{10... | collective-permute-start | bytes 12296 | tf_op jit(solution)/shard_map/ppermute | solution.py:698
  103.0 1.8 %collective-permute-done.17.refs_3_ = f32[8,128]{1,0:T(8,128)S(1)} collective-permute-done((f32[8,128]{1,0:T(8,128)S(1)}, f32[8,128]{1,0:T(8,128)S(1)}, u32[]{:S(2)}, u32[]{:S(2)}) %collective-permute-start.17) | collective-permute-done | bytes 4128 | tf_op jit(solution)/shard_map/ppermute | solution.py:698
  104.8 2.7 %shard_map.179 = (bf16[128,2048]{1,0:T(8,128)(2,1)}, bf16[128,2048]{1,0:T(8,128)(2,1)}, bf16[128,128]{1,0:T(8,128)(2,1)}, bf16[128,128]{1,0:T(8,128)(2,1)}, f32[4,128]{1,0:T(4,128)}, /*index=5*/f32[1,16]{1,0:T(1,128)}) custom-call(s32[64]{0:T(128)S(1)} %concatenate.3.meta.refs_0_, f32[16]{0:T(128)S(1)} %copy-done.1, ...), custom_call_target="tpu_custom_call", output_to_operand_aliasing={{0}: (18, {}), {1}: (19, {})} | custom-call | tf_op jit(solution)/shard_map/pallas_call | solution.py:391
  (46 shorter events, 21.1 us)
Async XLA Ops:
  0.6 9.6 %copy-start = (f32[1,1,4,128,128]{4,3,2,1,0:T(8,128)S(1)}, f32[1,1,4,128,128]{4,3,2,1,0:T(8,128)}, u32[]{:S(2)}) copy-start(f32[1,1,4,128,128]{4,3,2,1,0:T(8,128)} %param.20) | copy-start | bytes 786436
  0.6 9.6 %collective-permute-start = (f32[4,128,128]{2,1,0:T(8,128)}, f32[4,128,128]{2,1,0:T(8,128)S(1)}, u32[]{:S(2)}, u32[]{:S(2)}) collective-permute-start(f32[4,128,128]{2,1,0:T(8,128)} %bitcast.22), channel_id=1, source_target_pairs={{0,8},{8,0},{16,24},{24,16},{1,9},{9,1},{17,25},{25,17},{2,10},{10... | collective-permute-start | bytes 786440 | tf_op jit(solution)/shard_map/ppermute | solution.py:507
  11.0 16.4 %collective-permute-start.2 = (f32[288,512]{1,0:T(8,128)S(1)}, f32[288,512]{1,0:T(8,128)S(1)}, u32[]{:S(2)}, u32[]{:S(2)}) collective-permute-start(f32[288,512]{1,0:T(8,128)S(1)} %get-tuple-element.72), channel_id=1, source_target_pairs={{24,16},{16,8},{8,0},{25,17},{17,9},{9,1},{26,18},{18,10},{10,2},{... | collective-permute-start | bytes 1769480 | tf_op jit(solution)/shard_map/ppermute | solution.py:616
  12.3 17.1 %collective-permute-start.1 = (f32[288,512]{1,0:T(8,128)S(1)}, f32[288,512]{1,0:T(8,128)S(1)}, u32[]{:S(2)}, u32[]{:S(2)}) collective-permute-start(f32[288,512]{1,0:T(8,128)S(1)} %get-tuple-element.68), channel_id=1, source_target_pairs={{0,8},{8,16},{16,24},{1,9},{9,17},{17,25},{2,10},{10,18},{18,26},{... | collective-permute-start | bytes 1769480 | tf_op jit(solution)/shard_map/ppermute | solution.py:619
  28.0 15.5 %collective-permute-start.4 = (f32[288,512]{1,0:T(8,128)S(1)}, f32[288,512]{1,0:T(8,128)S(1)}, u32[]{:S(2)}, u32[]{:S(2)}) collective-permute-start(f32[288,512]{1,0:T(8,128)S(1)} %get-tuple-element.77), channel_id=1, source_target_pairs={{24,16},{16,8},{8,0},{25,17},{17,9},{9,1},{26,18},{18,10},{10,2},{... | collective-permute-start | bytes 1769480 | tf_op jit(solution)/shard_map/ppermute | solution.py:616
  30.0 15.4 %collective-permute-start.3 = (f32[288,512]{1,0:T(8,128)S(1)}, f32[288,512]{1,0:T(8,128)S(1)}, u32[]{:S(2)}, u32[]{:S(2)}) collective-permute-start(f32[288,512]{1,0:T(8,128)S(1)} %get-tuple-element.75), channel_id=1, source_target_pairs={{0,8},{8,16},{16,24},{1,9},{9,17},{17,25},{2,10},{10,18},{18,26},{... | collective-permute-start | bytes 1769480 | tf_op jit(solution)/shard_map/ppermute | solution.py:619
  46.0 14.3 %collective-permute-start.5 = (f32[288,512]{1,0:T(8,128)S(1)}, f32[288,512]{1,0:T(8,128)S(1)}, u32[]{:S(2)}, u32[]{:S(2)}) collective-permute-start(f32[288,512]{1,0:T(8,128)S(1)} %get-tuple-element.81), channel_id=1, source_target_pairs={{0,8},{8,16},{16,24},{1,9},{9,17},{17,25},{2,10},{10,18},{18,26},{... | collective-permute-start | bytes 1769480 | tf_op jit(solution)/shard_map/ppermute | solution.py:619
  50.5 14.9 %collective-permute-start.7 = (f32[288,512]{1,0:T(8,128)S(1)}, f32[288,512]{1,0:T(8,128)S(1)}, u32[]{:S(2)}, u32[]{:S(2)}) collective-permute-start(f32[288,512]{1,0:T(8,128)S(1)} %get-tuple-element.85), channel_id=1, source_target_pairs={{24,16},{16,8},{8,0},{25,17},{17,9},{9,1},{26,18},{18,10},{10,2},{... | collective-permute-start | bytes 1769480 | tf_op jit(solution)/shard_map/ppermute | solution.py:616
  51.8 36.5 %collective-permute-start.14 = (f32[5,128,512]{2,1,0:T(8,128)S(1)}, f32[5,128,512]{2,1,0:T(8,128)S(1)}, u32[]{:S(2)}, u32[]{:S(2)}) collective-permute-start(f32[5,128,512]{2,1,0:T(8,128)S(1)} %get-tuple-element.95.begin_here), channel_id=1, source_target_pairs={{0,4},{4,0},{1,5},{5,1},{2,6},{6,2},{3,7},{7,3},{8,12},{12,8},{9,1... | collective-permute-start | bytes 3932168 | tf_op jit(solution)/shard_map/ppermute | solution.py:626
  61.0 12.0 %collective-permute-start.6 = (f32[256,512]{1,0:T(8,128)S(1)}, f32[256,512]{1,0:T(8,128)S(1)}, u32[]{:S(2)}, u32[]{:S(2)}) collective-permute-start(f32[256,512]{1,0:T(8,128)S(1)} %get-tuple-element.83), channel_id=1, source_target_pairs={{0,8},{8,16},{16,24},{1,9},{9,17},{17,25},{2,10},{10,18},{18,26},{... | collective-permute-start | bytes 1572872 | tf_op jit(solution)/shard_map/ppermute | solution.py:619
  66.0 11.7 %collective-permute-start.12 = (f32[256,512]{1,0:T(8,128)S(1)}, f32[256,512]{1,0:T(8,128)S(1)}, u32[]{:S(2)}, u32[]{:S(2)}) collective-permute-start(f32[256,512]{1,0:T(8,128)S(1)} %get-tuple-element.91), channel_id=1, source_target_pairs={{24,16},{16,8},{8,0},{25,17},{17,9},{9,1},{26,18},{18,10},{10,2},{... | collective-permute-start | bytes 1572872 | tf_op jit(solution)/shard_map/ppermute | solution.py:616
  68.8 1.2 %collective-permute-start.8 = (f32[8,128]{1,0:T(8,128)S(1)}, f32[8,128]{1,0:T(8,128)S(1)}, u32[]{:S(2)}, u32[]{:S(2)}) collective-permute-start(f32[8,128]{1,0:T(8,128)S(1)} %shard_map.172.refs_6_), channel_id=1, source_target_pairs={{0,1},{1,0},{2,3},{3,2},{4,5},{5,4},{6,7},{7,6},{8,9},{9,8},{10,11... | collective-permute-start | bytes 12296 | tf_op jit(solution)/shard_map/ppermute | solution.py:437
  73.6 13.4 %collective-permute-start.9 = (f32[256,512]{1,0:T(8,128)S(1)}, f32[256,512]{1,0:T(8,128)S(1)}, u32[]{:S(2)}, u32[]{:S(2)}) collective-permute-start(f32[256,512]{1,0:T(8,128)S(1)} %get-tuple-element.87), channel_id=1, source_target_pairs={{8,16},{16,24},{9,17},{17,25},{10,18},{18,26},{11,19},{19,27},{12,... | collective-permute-start | bytes 1572872 | tf_op jit(solution)/shard_map/ppermute | solution.py:619
  78.4 12.5 %collective-permute-start.13 = (f32[256,512]{1,0:T(8,128)S(1)}, f32[256,512]{1,0:T(8,128)S(1)}, u32[]{:S(2)}, u32[]{:S(2)}) collective-permute-start(f32[256,512]{1,0:T(8,128)S(1)} %get-tuple-element.93), channel_id=1, source_target_pairs={{16,8},{8,0},{17,9},{9,1},{18,10},{10,2},{19,11},{11,3},{20,12},{1... | collective-permute-start | bytes 1572872 | tf_op jit(solution)/shard_map/ppermute | solution.py:616
  79.7 3.7 %collective-permute-start.10 = (f32[8,128]{1,0:T(8,128)S(1)}, f32[8,128]{1,0:T(8,128)S(1)}, u32[]{:S(2)}, u32[]{:S(2)}) collective-permute-start(f32[8,128]{1,0:T(8,128)S(1)} %add.37.refs_6_), channel_id=1, source_target_pairs={{0,2},{1,3},{2,0},{3,1},{4,6},{5,7},{6,4},{7,5},{8,10},{9,11},{10,... | collective-permute-start | bytes 12296 | tf_op jit(solution)/shard_map/ppermute | solution.py:437
  83.3 3.6 %collective-permute-start.11 = (f32[8,128]{1,0:T(8,128)S(1)}, f32[8,128]{1,0:T(8,128)S(1)}, u32[]{:S(2)}, u32[]{:S(2)}) collective-permute-start(f32[8,128]{1,0:T(8,128)S(1)} %add.38.refs_7_), channel_id=1, source_target_pairs={{0,4},{4,0},{1,5},{5,1},{2,6},{6,2},{3,7},{7,3},{8,12},{12,8},{9,1... | collective-permute-start | bytes 12296 | tf_op jit(solution)/shard_map/ppermute | solution.py:437
  87.6 17.2 %collective-permute-start.15 = (f32[256,512]{1,0:T(8,128)S(1)}, f32[256,512]{1,0:T(8,128)S(1)}, u32[]{:S(2)}, u32[]{:S(2)}) collective-permute-start(f32[256,512]{1,0:T(8,128)S(1)} %get-tuple-element.99), channel_id=1, source_target_pairs={{16,24},{17,25},{18,26},{19,27},{20,28},{21,29},{22,30},{23,31}} | collective-permute-start | bytes 1572872 | tf_op jit(solution)/shard_map/ppermute | solution.py:619
  90.9 1.9 %copy-start.1 = (f32[16]{0:T(128)S(1)}, f32[16]{0:T(128)}, u32[]{:S(2)}) copy-start(f32[16]{0:T(128)} %gains.3) | copy-start | bytes 196
  91.5 13.3 %collective-permute-start.16 = (f32[256,512]{1,0:T(8,128)S(1)}, f32[256,512]{1,0:T(8,128)S(1)}, u32[]{:S(2)}, u32[]{:S(2)}) collective-permute-start(f32[256,512]{1,0:T(8,128)S(1)} %get-tuple-element.100), channel_id=1, source_target_pairs={{8,0},{9,1},{10,2},{11,3},{12,4},{13,5},{14,6},{15,7}} | collective-permute-start | bytes 1572872 | tf_op jit(solution)/shard_map/ppermute | solution.py:616
  97.1 5.5 %collective-permute-start.19 = (f32[8,128]{1,0:T(8,128)S(1)}, f32[8,128]{1,0:T(8,128)S(1)}, u32[]{:S(2)}, u32[]{:S(2)}) collective-permute-start(f32[8,128]{1,0:T(8,128)S(1)} %get-tuple-element.103.refs_2_), channel_id=1, source_target_pairs={{0,24},{8,16},{16,8},{24,0},{1,25},{9,17},{17,9},{25,1},{2,26},{10... | collective-permute-start | bytes 12296 | tf_op jit(solution)/shard_map/ppermute | solution.py:698
  98.5 4.5 %collective-permute-start.18 = (f32[8,128]{1,0:T(8,128)S(1)}, f32[8,128]{1,0:T(8,128)S(1)}, u32[]{:S(2)}, u32[]{:S(2)}) collective-permute-start(f32[8,128]{1,0:T(8,128)S(1)} %get-tuple-element.103.refs_2_), channel_id=1, source_target_pairs={{0,16},{8,24},{16,0},{24,8},{1,17},{9,25},{17,1},{25,9},{2,18},{10... | collective-permute-start | bytes 12296 | tf_op jit(solution)/shard_map/ppermute | solution.py:698
  101.2 3.6 %collective-permute-start.17 = (f32[8,128]{1,0:T(8,128)S(1)}, f32[8,128]{1,0:T(8,128)S(1)}, u32[]{:S(2)}, u32[]{:S(2)}) collective-permute-start(f32[8,128]{1,0:T(8,128)S(1)} %get-tuple-element.103.refs_2_), channel_id=1, source_target_pairs={{0,8},{8,0},{16,24},{24,16},{1,9},{9,1},{17,25},{25,17},{2,10},{10... | collective-permute-start | bytes 12296 | tf_op jit(solution)/shard_map/ppermute | solution.py:698

commit v5 on v4

--- a/solution.py
+++ b/solution.py
@@ -44,12 +44,13 @@
 def start_kernel(
     per_chunk, head_dim, vocab, chunks,
     meta, bmat, cmat, tokens, table, step_t, rate_t, hid_far, cot_far,
-    up_first, down_first, up_small, down_small, cols, writer, hid, cot, sems,
+    x_first, y_first, small, cols, writer, hid, cot, sems,
 ):
     length = bmat.shape[0]
     state = bmat.shape[1]
     part = per_chunk * head_dim
-    lines = up_small.shape[1]
+    lines = small.shape[2]
+    odd = meta[4] != 0
     copies = []
     for chunk in range(chunks):
         span = slice(chunk * part, (chunk + 1) * part)
@@ -108,17 +109,19 @@
         down_lines = jnp.where(
             kinds == vocab, gone, jnp.where(kinds == vocab + 1, skips, dot(chosen, risen))
         )
-        up_small[chunk] = up_lines
-        down_small[chunk] = down_lines
+        small[0, chunk] = up_lines
+        small[1, chunk] = down_lines
         small_rows = slice(2 * state + chunk * lines, 2 * state + (chunk + 1) * lines)
-        up_first[small_rows, :] = up_lines
-        down_first[small_rows, :] = down_lines
+        x_first[small_rows, :] = jnp.where(odd, down_lines, up_lines)
+        y_first[small_rows, :] = jnp.where(odd, up_lines, down_lines)
         if chunk == 0:
-            writer_t, reader_t = rows.T, cmat[...].T
-            up_first[0:state, :] = dot(writer_t, fallen)
-            down_first[0:state, :] = dot(writer_t, risen)
-            up_first[state : 2 * state, :] = dot(reader_t, jnp.concatenate(grad_fallen, axis=1))
-            down_first[state : 2 * state, :] = dot(reader_t, jnp.concatenate(grad_risen, axis=1))
+            ends = jnp.where(odd, risen, fallen)
+            grad_ends = jnp.where(
+                odd, jnp.concatenate(grad_risen, axis=1), jnp.concatenate(grad_fallen, axis=1)
+            )
+            x_first[0:state, :] = dot(rows.T, ends)
+            x_first[state : 2 * state, :] = dot(cmat[...].T, grad_ends)
+            y_first[0 : 2 * state, :] = jnp.zeros((2 * state, part), F32)
 
 
 def head_copies(source, target, row, sems):
@@ -134,16 +137,16 @@
 
 
 def relay_kernel(last, paired, meta, *refs):
-    sources, (up, down, sems) = refs[:-5], refs[-3:]
+    sources, (x, y, sems) = refs[:-5], refs[-3:]
+    place, odd = meta[2], meta[4] != 0
     if paired:
+        plans = [((place == 1) | (place == 2), y, sources)]
+    else:
+        before, after = sources
+        inside, ahead = place > 0, place < last
         plans = [
-            (meta[2] == target, message, pieces)
-            for target, message, pieces in ((1, up, sources), (2, down, sources))
-        ]
-    else:
-        plans = [
-            (meta[2] != (0, last)[at], message, sources[at : at + 1])
-            for at, message in enumerate((up, down))
+            (inside & jnp.logical_not(odd), x, [before]), (inside & odd, y, [before]),
+            (ahead & odd, x, [after]), (ahead & jnp.logical_not(odd), y, [after]),
         ]
     for at, (wanted, message, pieces) in enumerate(plans):
         copies = []
@@ -174,34 +177,39 @@
         copy.wait()
 
 
-def combine_kernel(vocab, has_small, has_begin, slot, tables, waits, *refs):
-    meta, received, own, small, decays = refs[:5]
-    send, held = refs[-3:-1] if has_begin else refs[-2:]
-    del waits
-    state = own.shape[2]
+def combine_kernel(vocab, has_small, has_begin, sends, slot, side, tables, *refs):
+    meta, received, own, small = refs[:4]
+    held = refs[-1 - has_begin]
+    way = meta[4] if side else 1 - meta[4]
+    state = own.shape[3]
     land, source, forward, piece, other = (at + slot for at in tables)
     if has_begin:
         begin = refs[-1]
         begin[meta[piece]] = received[0:state, 0 : begin.shape[2]]
         begin[meta[other]] = received[state : 2 * state, 0 : begin.shape[2]]
-    held[meta[land]] = received[0 : 2 * state, :].astype(BF16)
+    held[way, meta[land]] = received[0 : 2 * state, :].astype(BF16)
+    if not sends:
+        return
+    send = refs[-2 - has_begin]
     passing = meta[forward] != 0
-    decay = jnp.where(passing, 1.0, decays[meta[source], vocab : vocab + 1, :])
+    decay = jnp.where(passing, 1.0, small[1, meta[source], vocab : vocab + 1, :])
     adding = jnp.where(passing, 0.0, 1.0)
     if has_small:
-        lines = small.shape[1]
-        for at in range(small.shape[0]):
+        lines = small.shape[2]
+        for at in range(small.shape[1]):
             rows = slice(2 * state + at * lines, 2 * state + (at + 1) * lines)
-            send[rows, :] = decays[at, vocab : vocab + 1, :] * received[rows, :] + small[at]
+            send[rows, :] = (
+                small[1, at, vocab : vocab + 1, :] * received[rows, :] + small[way, at]
+            )
     for at in range(2):
         rows = slice(at * state, (at + 1) * state)
-        send[rows, :] = decay * received[rows, :] + adding * own[meta[source], at]
+        send[rows, :] = decay * received[rows, :] + adding * own[way, meta[source], at]
 
 
 def inner_kernel(
     per_chunk, head_dim, vocab,
     meta, hid, cot, writer, cmat, tokens, cols,
-    up, down, mixed_in, back_in, reader_in, writer_in, tab,
+    ends, mixed_in, back_in, reader_in, writer_in, tab,
     inner, inner_t, cross, writer_t, reader_t,
 ):
     chunk = pl.program_id(0)
@@ -238,10 +246,10 @@
         mixed_in[:, at] = dot((decay * inner[...]).astype(BF16), scaled)
         back_in[:, at] = dot((decay * inner_t[...]).astype(BF16), grads)
         cross[...] += decay * dot(grads, scaled, NT)
-    up[0, 0] = dot(writer_t[...], jnp.concatenate(fallen, axis=1))
-    up[0, 1] = dot(reader_t[...], jnp.concatenate(grad_fallen, axis=1))
-    down[0, 0] = dot(writer_t[...], jnp.concatenate(risen, axis=1))
-    down[0, 1] = dot(reader_t[...], jnp.concatenate(grad_risen, axis=1))
+    ends[0, 0, 0] = dot(writer_t[...], jnp.concatenate(fallen, axis=1))
+    ends[0, 0, 1] = dot(reader_t[...], jnp.concatenate(grad_fallen, axis=1))
+    ends[1, 0, 0] = dot(writer_t[...], jnp.concatenate(risen, axis=1))
+    ends[1, 0, 1] = dot(reader_t[...], jnp.concatenate(grad_risen, axis=1))
 
     @pl.when(chunk == pl.num_programs(0) - 1)
     def _():
@@ -255,10 +263,13 @@
 
 def sums_kernel(
     per_chunk, head_dim, vocab, table_scale, skip_scale,
-    meta, earlier, later, small, grad_up, grad_down, tab, total, acc,
+    meta, from_x, from_y, small, grad_up, grad_down, tab, total, acc,
 ):
     chunk = pl.program_id(0)
-    lines, width = earlier.shape
+    lines, width = from_x.shape
+    odd = meta[4] != 0
+    earlier = jnp.where(odd, from_x[...], from_y[...])
+    later = jnp.where(odd, from_y[...], from_x[...])
 
     @pl.when(chunk == 0)
     def _():
@@ -275,8 +286,8 @@
         head_of == lax.broadcasted_iota(jnp.int32, (128, width), 0), 1.0, 0.0
     ).astype(F32)
     kinds = lax.broadcasted_iota(jnp.int32, (lines, 128), 0)
-    tables = split(later[...], grad_up[0, 0]) + split(earlier[...], grad_down[0, 0])
-    skips = jnp.broadcast_to(small[0, vocab + 1 : vocab + 2, :], (lines, width))
+    tables = split(later, grad_up[0, 0, 0]) + split(earlier, grad_down[0, 0, 0])
+    skips = jnp.broadcast_to(small[0, 0, vocab + 1 : vocab + 2, :], (lines, width))
     acc[...] += jnp.where(kinds < vocab, tables, split(skips, picks))
 
     @pl.when(chunk == pl.num_programs(0) - 1)
@@ -290,7 +301,7 @@
 
 def finish_chunk(
     per_chunk, head_dim, vocab, meta, chunk, gains, hid, cot, writer, cmat, mine,
-    mixed_in, back_in, chain_in, chain_back, begin_here, begin_there, earlier,
+    mixed_in, back_in, chain_in, chain_back, begin_here, begin_there, from_x, from_y,
     mixed, grad_hidden, acc_c, acc_w,
 ):
     length = hid.shape[0]
@@ -302,7 +313,9 @@
         for lane in range(0, value.shape[1], state):
             begins.append(value[:, lane : lane + state].T)
     begins = jnp.concatenate(begins, axis=1)
-    passed = jnp.where(meta[2] == 0, 1.0, earlier[vocab : vocab + 1, :])
+    row = slice(vocab, vocab + 1)
+    passed = jnp.where(meta[4] != 0, from_x[row, :], from_y[row, :])
+    passed = jnp.where(meta[2] == 0, 1.0, passed)
     state_in = (chain_in[0:state].astype(F32) + passed * begins).astype(BF16)
     grad_in = chain_in[state:]
     state_back = chain_back[0:state]
@@ -340,7 +353,7 @@
 def early_kernel(
     per_chunk, head_dim, vocab,
     meta, gains, hid, cot, writer, cmat, cols, mixed_in, back_in, reader_in, writer_in,
-    held_up, held_down, begin_here, begin_there, earlier, *refs,
+    held_up, held_down, begin_here, begin_there, from_x, from_y, *refs,
 ):
     mixed, grad_hidden, acc_c, acc_w = refs[-5:-1]
     chunk = pl.program_id(0)
@@ -352,15 +365,15 @@
 
     finish_chunk(
         per_chunk, head_dim, vocab, meta, chunk, gains, hid, cot, writer[...], cmat[...],
-        cols[0], mixed_in, back_in, held_up[0], held_down[0], begin_here, begin_there, earlier,
+        cols[0], mixed_in, back_in, held_up[0, 0], held_down[0, 0], begin_here, begin_there, from_x, from_y,
         mixed, grad_hidden, acc_c, acc_w,
     )
 
 
 def last_kernel(
-    per_chunk, head_dim, vocab, bmat_scale, up_land, down_land, chunk,
+    per_chunk, head_dim, vocab, bmat_scale, land, chunk,
     meta, gains, hid, cot, writer, cmat, cols, mixed_in, back_in, sum_c, sum_w,
-    held_up, held_down, begin_here, begin_there, earlier, got_up, got_down, *refs,
+    held_up, held_down, begin_here, begin_there, from_x, from_y, got, *refs,
 ):
     sums = refs[2:-8]
     mixed, grad_hidden, grad_cmat, grad_bmat, grad_table, grad_skip, acc_c, acc_w = refs[-8:]
@@ -372,11 +385,13 @@
     grad_skip[...] = total[vocab_rows : vocab_rows + 1, 0:heads]
     acc_c[...] = sum_c[...]
     acc_w[...] = sum_w[...]
-    chain_in = jnp.where(meta[up_land] == chunk, got_up[...].astype(BF16), held_up[0])
-    chain_back = jnp.where(meta[down_land] == chunk, got_down[...].astype(BF16), held_down[0])
+    fresh, odd = meta[land] == chunk, meta[4] != 0
+    arrived = got[...].astype(BF16)
+    chain_in = jnp.where(fresh & odd, arrived, held_up[0, 0])
+    chain_back = jnp.where(fresh & jnp.logical_not(odd), arrived, held_down[0, 0])
     finish_chunk(
         per_chunk, head_dim, vocab, meta, chunk, gains, hid, cot, writer[...], cmat[...],
-        cols[0], mixed_in, back_in, chain_in, chain_back, begin_here, begin_there, earlier,
+        cols[0], mixed_in, back_in, chain_in, chain_back, begin_here, begin_there, from_x, from_y,
         mixed, grad_hidden, acc_c, acc_w,
     )
     grad_cmat[...] = acc_c[...].astype(BF16)
@@ -474,24 +489,29 @@
 
     times = jnp.arange(slots, dtype=jnp.int32)
     from_last = count - 1 - place
+    odd = place % 2
     table_of = []
-    for far, toward in ((place, -1), (from_last, 1)):
+    for upward_here in (odd == 1, odd == 0):
+        far = jnp.where(upward_here, place, from_last)
         lands = times - jnp.maximum(far, 1) + 1
-        pieces = place + toward * (times + 2)
-        others = jnp.full_like(times, count)
         if paired:
             arrives = times + 2 == far
-            pieces = jnp.where(arrives, 0 if toward < 0 else 3, count)
-            others = jnp.where(arrives, 1 if toward < 0 else 2, count)
-        table_of.append(jnp.where((lands >= 0) & (lands < chunks), lands, chunks))
-        table_of.append(jnp.clip(times + 1 - far, 0, chunks - 1))
-        table_of.append((times + 1 < far).astype(jnp.int32))
-        table_of.append(jnp.where((pieces >= 0) & (pieces < count), pieces, count))
-        table_of.append(others)
-    base = [place * length, suffix_start[0], place, here]
-    meta = jnp.concatenate([jnp.stack(base).astype(jnp.int32)] + table_of)
-    up_tables = [4 + at * slots for at in range(5)]
-    down_tables = [4 + at * slots for at in range(5, 10)]
+            pieces = jnp.where(arrives, jnp.where(upward_here, 0, 3), count)
+            others = jnp.where(arrives, jnp.where(upward_here, 1, 2), count)
+        else:
+            pieces = place + jnp.where(upward_here, -1, 1) * (times + 2)
+            pieces = jnp.where((pieces >= 0) & (pieces < count), pieces, count)
+            others = jnp.full_like(times, count)
+        table_of += [
+            jnp.where((lands >= 0) & (lands < chunks), lands, chunks),
+            jnp.clip(times + 1 - far, 0, chunks - 1),
+            (times + 1 < far).astype(jnp.int32),
+            pieces, others,
+        ]
+    base = [place * length, suffix_start[0], place, here, odd]
+    base = jnp.stack([jnp.asarray(value, jnp.int32) for value in base])
+    meta = jnp.concatenate([base] + [value.astype(jnp.int32) for value in table_of])
+    tables = [[5 + (5 * side + at) * slots for at in range(5)] for side in range(2)]
 
     upward = [(at, at + 1) for at in range(count - 1)]
     downward = [(at + 1, at) for at in range(count - 1)]
@@ -512,15 +532,15 @@
     near = pl.BlockSpec(memory_space=pltpu.VMEM)
     by_chunk = pl.BlockSpec((length, part), lambda k, *_: (0, k))
     one_cols = pl.BlockSpec((1, length, 128), lambda k, *_: (k, 0, 0))
-    pair = pl.BlockSpec((1, 2, state_dim, part), lambda k, *_: (k, 0, 0, 0))
-    one_small = pl.BlockSpec((1, lines, part), lambda k, *_: (k, 0, 0))
+    pair = pl.BlockSpec((2, 1, 2, state_dim, part), lambda k, *_: (0, k, 0, 0, 0))
+    one_small = pl.BlockSpec((1, 1, lines, part), lambda k, *_: (1, k, 0, 0))
     square = whole((length, state_dim))
     tok_spec = whole((1, length))
     full_rows = 2 * state_dim + chunks * lines
-    small_shape = (chunks, lines, part)
+    small_shape = (2, chunks, lines, part)
     first = ((full_rows, part), F32, near, CHIP)
 
-    up_first, down_first, up_small, down_small, cols, writer, hid, cot = call(
+    x_first, y_first, small, cols, writer, hid, cot = call(
         functools.partial(start_kernel, per_chunk, head_dim, vocab, chunks),
         (meta,), (1,),
         [
@@ -530,22 +550,22 @@
         ],
         [
             first, first,
-            (small_shape, F32, near, CHIP), (small_shape, F32, near, CHIP),
+            (small_shape, F32, near, CHIP),
             ((chunks, length, 128), F32, near, CHIP), ((length, state_dim), BF16, near, CHIP),
             ((length, width), BF16, near, CHIP), ((length, width), BF16, near, CHIP),
         ],
         [pltpu.SemaphoreType.DMA((chunks, 2))],
     )
 
-    up_first, down_first = call(
+    x_first, y_first = call(
         functools.partial(relay_kernel, count - 1, paired),
         (meta,), (),
         [(piece, anywhere, None) for piece in pieces]
-        + [(up_first, near, CHIP), (down_first, near, CHIP)],
+        + [(x_first, near, CHIP), (y_first, near, CHIP)],
         [
             ((full_rows, part), F32, near, CHIP), ((full_rows, part), F32, near, CHIP),
         ],
-        [pltpu.SemaphoreType.DMA((2, 2, local_heads))],
+        [pltpu.SemaphoreType.DMA((4, 2, local_heads))],
         aliases={3: 0, 4: 1},
     )
     begin_shape = (count + 1, head_dim, local_heads * state_dim)
@@ -559,7 +579,7 @@
         [pltpu.SemaphoreType.DMA((3, local_heads))],
     )
 
-    up, down, mixed_in, back_in, reader_in, writer_in, tab = call(
+    ends, mixed_in, back_in, reader_in, writer_in, tab = call(
         functools.partial(inner_kernel, per_chunk, head_dim, vocab),
         (meta,), (chunks,),
         [
@@ -567,8 +587,7 @@
             (reads, square, HBM), (toks, tok_spec, HBM), (cols, one_cols, CHIP),
         ],
         [
-            ((chunks, 2, state_dim, part), F32, pair, CHIP),
-            ((chunks, 2, state_dim, part), F32, pair, CHIP),
+            ((2, chunks, 2, state_dim, part), F32, pair, CHIP),
             ((length, width), F32, by_chunk, CHIP),
             ((length, width), F32, by_chunk, CHIP),
             ((length, state_dim), F32, square, CHIP),
@@ -578,48 +597,52 @@
         [pltpu.VMEM((length, length), F32)] * 3 + [pltpu.VMEM((state_dim, length), BF16)] * 2,
     )
 
-    def step_chain(slot, received, own, small, tables, held, begin, waits):
+    def step_chain(slot, side, received, held, begin, waits):
         has_small = slot < count - 2
         has_begin = slot < count - 2
+        sends = side == 1 or slot + 1 < slots - 1
         rows = full_rows if has_small else 2 * state_dim
-        held_shape = (chunks + 1, 2 * state_dim, part)
-        ins = [
-            (received, near, CHIP), (own, near, CHIP), (small, near, CHIP),
-            (down_small, near, CHIP),
-        ]
-        outs = [((rows, part), F32, near, CHIP), (held_shape, BF16, near, CHIP)]
+        held_shape = (2, chunks + 1, 2 * state_dim, part)
+        ins = [(received, near, CHIP), (ends, near, CHIP), (small, near, CHIP)]
+        outs = [((rows, part), F32, near, CHIP)] if sends else []
+        outs.append((held_shape, BF16, near, CHIP))
         aliases = {}
         if held is not None:
-            aliases[1 + len(ins)] = 1
+            aliases[1 + len(ins)] = len(outs) - 1
             ins.append((held, near, CHIP))
         if has_begin:
-            aliases[1 + len(ins)] = 2
+            aliases[1 + len(ins)] = len(outs)
             ins.append((begin, near, CHIP))
             outs.append((begin_shape, F32, near, CHIP))
         ins += [(value, anywhere, None) for value in waits]
         results = call(
             functools.partial(
-                combine_kernel, vocab, has_small, has_begin, slot, tables, len(waits)
+                combine_kernel, vocab, has_small, has_begin, sends, slot, side, tables[side]
             ),
             (meta,), (), ins, outs,
             aliases=aliases,
         )
-        return results if has_begin else (*results, begin)
+        results = list(results) if has_begin else [*results, begin]
+        return results if sends else [None, *results]
 
     lines_at = 2 * state_dim // lines
     from_slot = pl.BlockSpec((lines, part), lambda k, *_: (lines_at + k, 0))
-    grad_part = pl.BlockSpec((1, 1, state_dim, part), lambda k, *_: (k, 1, 0, 0))
+    grad_parts = [
+        pl.BlockSpec((1, 1, 1, state_dim, part), lambda k, *_, way=way: (way, k, 1, 0, 0))
+        for way in range(2)
+    ]
     sums, exchanges = sum_steps(("rep", "dom", "ctx"))
-    send_up, send_down, held_up, held_down = up_first, down_first, None, None
+    assert count % 2 == 0
+    even_links = [(at, at ^ 1) for at in range(count)]
+    odd_links = [(at, (at - 1 ^ 1) + 1) for at in range(1, count - 1)]
+    send_x, send_y, held = x_first, y_first, None
     for slot in range(slots):
-        first_place = max(0, slot - chunks + 1)
-        got_down = lax.ppermute(
-            send_down, "ctx", [(count - 1 - at, count - 2 - at) for at in range(first_place, count - 1)]
-        )
-        got_up = lax.ppermute(send_up, "ctx", upward[first_place:])
+        got_x = lax.ppermute(send_x, "ctx", even_links)
+        if slot < slots - 1:
+            got_y = lax.ppermute(send_y, "ctx", odd_links)
         waits_up, waits_down = [], []
         if slot == count - 2:
-            earlier, later = got_up, got_down
+            from_x, from_y = got_x, got_y
         if slot == count - 1:
             begin_there = begin_here
             if doms == 2:
@@ -631,9 +654,9 @@
                 ),
                 (meta,), (chunks,),
                 [
-                    (earlier, from_slot, None), (later, from_slot, None),
-                    (down_small, one_small, None), (up, grad_part, CHIP),
-                    (down, grad_part, CHIP), (tab, whole(tab.shape), CHIP),
+                    (from_x, from_slot, None), (from_y, from_slot, None),
+                    (small, one_small, CHIP), (ends, grad_parts[0], CHIP),
+                    (ends, grad_parts[1], CHIP), (tab, whole(tab.shape), CHIP),
                 ],
                 [((lines, state_dim), F32, whole((lines, state_dim)), None)],
                 [pltpu.VMEM((lines, state_dim), F32)],
@@ -647,23 +670,24 @@
                     total = step(total)
                 sums = sums[1:]
             waits_down.append(total)
-        send_down, held_down, begin_here = step_chain(
-            slot, got_down, down, down_small, down_tables, held_down, begin_here, waits_down
-        )
+        send_y, held, begin_here = step_chain(slot, 0, got_x, held, begin_here, waits_down)
         if slot >= count - 1:
             for step in sums[:1]:
                 total = step(total)
             sums = sums[1:]
             waits_up.append(total)
-        send_up, held_up, begin_here = step_chain(
-            slot, got_up, up, up_small, up_tables, held_up, begin_here, waits_up
-        )
+        send_x, held, begin_here = step_chain(slot, 1, got_y, held, begin_here, waits_up)
 
     def chunk_specs(at):
         return (
             pl.BlockSpec((length, part), lambda k, *_: (0, k + at)),
             pl.BlockSpec((1, length, 128), lambda k, *_: (k + at, 0, 0)),
-            pl.BlockSpec((1, 2 * state_dim, part), lambda k, *_: (k + at, 0, 0)),
+            [
+                pl.BlockSpec(
+                    (1, 1, 2 * state_dim, part), lambda k, *_, way=way: (way, k + at, 0, 0)
+                )
+                for way in range(2)
+            ],
             pl.BlockSpec(
                 (per_chunk // local_heads, head_dim, local_heads * state_dim),
                 lambda k, *_: (k + at, 0, 0),
@@ -672,13 +696,13 @@
         )
 
     def finish_ins(at, sum_c, sum_w):
-        slab, col, chain, states, small = chunk_specs(at)
+        slab, col, chain, states, rows = chunk_specs(at)
         return [
             (hid, slab, CHIP), (cot, slab, CHIP), (writer, square, CHIP), (reads, square, HBM),
             (cols, col, CHIP), (mixed_in, slab, CHIP), (back_in, slab, CHIP),
             (sum_c, square, CHIP), (sum_w, square, CHIP),
-            (held_up, chain, CHIP), (held_down, chain, CHIP),
-            (begin_here, states, CHIP), (begin_there, states, CHIP), (earlier, small, None),
+            (held, chain[0], CHIP), (held, chain[1], CHIP),
+            (begin_here, states, CHIP), (begin_there, states, CHIP), (from_x, rows, None), (from_y, rows, None),
         ]
 
     for step in sums:
@@ -693,18 +717,18 @@
             ((length, state_dim), F32, square, CHIP), ((length, state_dim), F32, square, CHIP),
             (total.shape, F32, anywhere, None),
         ],
-        aliases={16: 4},
+        aliases={17: 4},
     )
     exchanged = [exchange(total) for exchange in exchanges]
     ins = finish_ins(chunks - 1, sum_c, sum_w) + [
-        (got_up, whole(got_up.shape), None), (got_down, whole(got_down.shape), None),
+        (got_x, whole(got_x.shape), None),
         (mixed, anywhere, HBM), (grad_hidden, anywhere, HBM),
     ] + [(value, whole(value.shape), None) for value in [total] + exchanged]
     slab = chunk_specs(chunks - 1)[0]
     mixed, grad_hidden, grad_cmat, grad_bmat, grad_table, grad_skip = call(
         functools.partial(
             last_kernel, per_chunk, head_dim, vocab, bmat_scale,
-            up_tables[0] + slots - 1, down_tables[0] + slots - 1, chunks - 1,
+            tables[0][0] + slots - 1, chunks - 1,
         ),
         (meta, skip_gain), (1,), ins,
         [

time: 108 us -> 102 us (0.944)
  starting transfers between devices: 38.1 us -> 33 us
  waiting for transfers between devices: 41 us -> 39.2 us
    ppermute x12 -> x11, starting transfers between devices: 27.1 us -> 20.9 us  [the longest x6 17.4 us: per_device(): got_x = lax.ppermute(send_x, 'ctx', even_links)]
    ppermute x12 -> x11, waiting for transfers between devices: 30.9 us -> 30 us  [the longest x6 30 us: per_device(): got_x = lax.ppermute(send_x, 'ctx', even_links)]
  transfers between devices with their start and end apart: 20 -> 19, of which waited for: 14 -> 10; matrix products, arithmetic and copies ran while one was open for 0% -> 0% of each run, Pallas kernels for 21% -> 21%
where the time goes in v5:
time: 102 us
  waiting for transfers between devices  39.2 us (38%)
  starting transfers between devices  33 us (32%)
  Pallas kernels  26.4 us (26%)
  between operations  2.2 us (2%)
  local copies, waits for them, and re-layouts  1.05 us (1%)
    ppermute x6, waiting for transfers between devices, per_device(): got_x = lax.ppermute(send_x, 'ctx', even_links)  30 us
    pallas_call x17, Pallas kernels, call(): pl.pallas_call(body, out_shape=[jax.ShapeDtypeStruct(shape, kind) if plac...  26.4 us
    ppermute x6, starting transfers between devices, per_device(): got_x = lax.ppermute(send_x, 'ctx', even_links)  17.4 us
    ppermute x3, waiting for transfers between devices, sum_steps(): steps.append(lambda value, group=group: value + group[0](value))  5.36 us
    ppermute x3, starting transfers between devices, per_device(): exchanged = [exchange(total) for exchange in exchanges]  4.39 us
    ppermute x5, starting transfers between devices, per_device(): got_y = lax.ppermute(send_y, 'ctx', odd_links)  3.42 us
    ppermute x3, waiting for transfers between devices, per_device(): exchanged = [exchange(total) for exchange in exchanges]  3.37 us
    ppermute x3, starting transfers between devices, sum_steps(): steps.append(lambda value, group=group: value + group[0](value))  3.11 us
  transfers between devices with their start and end apart: 19, of which 10 were waited for; matrix products, arithmetic and copies ran while one was open for 0% of the time, Pallas kernels for 21%

profile of v5, /device:TPU:0, one launch (start us, length us, event | category | flops | bytes accessed | tf_op | source)
XLA Modules:
  0.0 101.8 jit_solution(3091927340379011649)
XLA Ops:
  0.6 3.1 %collective-permute-start = (f32[4,128,128]{2,1,0:T(8,128)}, f32[4,128,128]{2,1,0:T(8,128)S(1)}, u32[]{:S(2)}, u32[]{:S(2)}) collective-permute-start(f32[4,128,128]{2,1,0:T(8,128)} %bitcast.23), channel_id=1, source_target_pairs={{0,8},{8,0},{16,24},{24,16},{1,9},{9,1},{17,25},{25,17},{2,10},{10... | collective-permute-start | bytes 786440 | tf_op jit(solution)/shard_map/ppermute | solution.py:527
  5.2 4.6 %shard_map.163 = (f32[288,512]{1,0:T(8,128)S(1)}, f32[288,512]{1,0:T(8,128)S(1)}, f32[2,4,8,512]{3,2,1,0:T(8,128)S(1)}, f32[4,128,128]{2,1,0:T(8,128)S(1)}, bf16...) custom-call(s32[65]{0:T(128)S(1)} %concatenate.3.meta.refs_0_, ...), custom_call_target="tpu_custom_call" | custom-call | tf_op jit(solution)/shard_map/pallas_call | solution.py:406
  12.0 1.9 %collective-permute-start.2 = (f32[288,512]{1,0:T(8,128)S(1)}, f32[288,512]{1,0:T(8,128)S(1)}, u32[]{:S(2)}, u32[]{:S(2)}) collective-permute-start(f32[288,512]{1,0:T(8,128)S(1)} %get-tuple-element.67), channel_id=1, source_target_pairs={{0,8},{8,0},{16,24},{24,16},{1,9},{9,1},{17,25},{25,17},{2,10},{10... | collective-permute-start | bytes 1769480 | tf_op jit(solution)/shard_map/ppermute | solution.py:640
  14.6 5.4 %shard_map.164 = (f32[2,4,2,128,512]{4,3,2,1,0:T(8,128)S(1)}, f32[128,2048]{1,0:T(8,128)S(1)}, f32[128,2048]{1,0:T(8,128)S(1)}, f32[128,128]{1,0:T(8,128)S(1)}, ...) custom-call(s32[65]{0:T(128)S(1)} %concatenate.3.meta.refs_0_, bf16[128,2048]{1,0:T(8,128)(2,1)S(1)} %get-tuple-element.54.hid, ...), custom_call_target="tpu_custom_call" | custom-call | tf_op jit(solution)/shard_map/pallas_call | solution.py:406
  20.7 5.9 %collective-permute-done.2.refs_1_ = f32[288,512]{1,0:T(8,128)S(1)} collective-permute-done((f32[288,512]{1,0:T(8,128)S(1)}, f32[288,512]{1,0:T(8,128)S(1)}, u32[]{:S(2)}, u32[]{:S(2)}) %collective-permute-start.2) | collective-permute-done | bytes 589856 | tf_op jit(solution)/shard_map/ppermute | solution.py:640
  27.9 3.8 %collective-permute-start.3 = (f32[288,512]{1,0:T(8,128)S(1)}, f32[288,512]{1,0:T(8,128)S(1)}, u32[]{:S(2)}, u32[]{:S(2)}) collective-permute-start(f32[288,512]{1,0:T(8,128)S(1)} %get-tuple-element.70), channel_id=1, source_target_pairs={{0,8},{8,0},{16,24},{24,16},{1,9},{9,1},{17,25},{25,17},{2,10},{10... | collective-permute-start | bytes 1769480 | tf_op jit(solution)/shard_map/ppermute | solution.py:640
  32.5 10.8 %collective-permute-done.3.refs_1_ = f32[288,512]{1,0:T(8,128)S(1)} collective-permute-done((f32[288,512]{1,0:T(8,128)S(1)}, f32[288,512]{1,0:T(8,128)S(1)}, u32[]{:S(2)}, u32[]{:S(2)}) %collective-permute-start.3) | collective-permute-done | bytes 589856 | tf_op jit(solution)/shard_map/ppermute | solution.py:640
  44.6 3.0 %collective-permute-start.6 = (f32[288,512]{1,0:T(8,128)S(1)}, f32[288,512]{1,0:T(8,128)S(1)}, u32[]{:S(2)}, u32[]{:S(2)}) collective-permute-start(f32[288,512]{1,0:T(8,128)S(1)} %get-tuple-element.77), channel_id=1, source_target_pairs={{0,8},{8,0},{16,24},{24,16},{1,9},{9,1},{17,25},{25,17},{2,10},{10... | collective-permute-start | bytes 1769480 | tf_op jit(solution)/shard_map/ppermute | solution.py:640
  48.4 1.6 %collective-permute-start.12 = (f32[5,128,512]{2,1,0:T(8,128)S(1)}, f32[5,128,512]{2,1,0:T(8,128)S(1)}, u32[]{:S(2)}, u32[]{:S(2)}) collective-permute-start(f32[5,128,512]{2,1,0:T(8,128)S(1)} %get-tuple-element.88.begin_here), channel_id=1, source_target_pairs={{0,4},{4,0},{1,5},{5,1},{2,6},{6,2},{3,7},{7,3},{8,12},{12,8},{9,1... | collective-permute-start | bytes 3932168 | tf_op jit(solution)/shard_map/ppermute | solution.py:649
  50.0 8.3 %collective-permute-done.6.refs_1_.from_x = f32[288,512]{1,0:T(8,128)S(1)} collective-permute-done((f32[288,512]{1,0:T(8,128)S(1)}, f32[288,512]{1,0:T(8,128)S(1)}, u32[]{:S(2)}, u32[]{:S(2)}) %collective-permute-start.6) | collective-permute-done | bytes 589856 | tf_op jit(solution)/shard_map/ppermute | solution.py:640
  59.6 3.1 %collective-permute-start.7 = (f32[256,512]{1,0:T(8,128)S(1)}, f32[256,512]{1,0:T(8,128)S(1)}, u32[]{:S(2)}, u32[]{:S(2)}) collective-permute-start(f32[256,512]{1,0:T(8,128)S(1)} %get-tuple-element.80), channel_id=1, source_target_pairs={{0,8},{8,0},{16,24},{24,16},{1,9},{9,1},{17,25},{25,17},{2,10},{10... | collective-permute-start | bytes 1572872 | tf_op jit(solution)/shard_map/ppermute | solution.py:640
  63.3 1.5 %shard_map.173.refs_5_ = f32[8,128]{1,0:T(8,128)S(1)} custom-call(s32[65]{0:T(128)S(1)} %concatenate.3.meta.refs_0_, f32[288,512]{1,0:T(8,128)S(1)} %collective-permute-done.6.refs_1_.from_x, f32[288,512]{1,0:T(8,128)S(1)} %collective-permute-done.4.refs_1_.from_y, f32[2,4,8,512]{3,2,1,0:T(8,128)S(1)} %get-tuple-element.66.refs_3_.small, ...), custom_call_target="tpu_custom_call" | custom-call | tf_op jit(solution)/shard_map/pallas_call | solution.py:406
  66.0 4.9 %collective-permute-done.7.refs_1_ = f32[256,512]{1,0:T(8,128)S(1)} collective-permute-done((f32[256,512]{1,0:T(8,128)S(1)}, f32[256,512]{1,0:T(8,128)S(1)}, u32[]{:S(2)}, u32[]{:S(2)}) %collective-permute-start.7) | collective-permute-done | bytes 524320 | tf_op jit(solution)/shard_map/ppermute | solution.py:640
  72.2 3.1 %collective-permute-start.11 = (f32[256,512]{1,0:T(8,128)S(1)}, f32[256,512]{1,0:T(8,128)S(1)}, u32[]{:S(2)}, u32[]{:S(2)}) collective-permute-start(f32[256,512]{1,0:T(8,128)S(1)} %get-tuple-element.86), channel_id=1, source_target_pairs={{0,8},{8,0},{16,24},{24,16},{1,9},{9,1},{17,25},{25,17},{2,10},{10... | collective-permute-start | bytes 1572872 | tf_op jit(solution)/shard_map/ppermute | solution.py:640
  76.0 1.6 %collective-permute-start.13 = (f32[8,128]{1,0:T(8,128)S(1)}, f32[8,128]{1,0:T(8,128)S(1)}, u32[]{:S(2)}, u32[]{:S(2)}) collective-permute-start(f32[8,128]{1,0:T(8,128)S(1)} %add.42.refs_5_), channel_id=1, source_target_pairs={{0,2},{1,3},{2,0},{3,1},{4,6},{5,7},{6,4},{7,5},{8,10},{9,11},{10,... | collective-permute-start | bytes 12296 | tf_op jit(solution)/shard_map/ppermute | solution.py:452
  77.5 2.1 %collective-permute-done.13 = f32[8,128]{1,0:T(8,128)S(1)} collective-permute-done((f32[8,128]{1,0:T(8,128)S(1)}, f32[8,128]{1,0:T(8,128)S(1)}, u32[]{:S(2)}, u32[]{:S(2)}) %collective-permute-start.13) | collective-permute-done | bytes 4128 | tf_op jit(solution)/shard_map/ppermute | solution.py:452
  79.6 1.5 %collective-permute-start.14 = (f32[8,128]{1,0:T(8,128)S(1)}, f32[8,128]{1,0:T(8,128)S(1)}, u32[]{:S(2)}, u32[]{:S(2)}) collective-permute-start(f32[8,128]{1,0:T(8,128)S(1)} %add.43.refs_6_), channel_id=1, source_target_pairs={{0,4},{4,0},{1,5},{5,1},{2,6},{6,2},{3,7},{7,3},{8,12},{12,8},{9,1... | collective-permute-start | bytes 12296 | tf_op jit(solution)/shard_map/ppermute | solution.py:452
  81.2 2.1 %collective-permute-done.14 = f32[8,128]{1,0:T(8,128)S(1)} collective-permute-done((f32[8,128]{1,0:T(8,128)S(1)}, f32[8,128]{1,0:T(8,128)S(1)}, u32[]{:S(2)}, u32[]{:S(2)}) %collective-permute-start.14) | collective-permute-done | bytes 4128 | tf_op jit(solution)/shard_map/ppermute | solution.py:452
  84.5 2.6 %collective-permute-start.15 = (f32[256,512]{1,0:T(8,128)S(1)}, f32[256,512]{1,0:T(8,128)S(1)}, u32[]{:S(2)}, u32[]{:S(2)}) collective-permute-start(f32[256,512]{1,0:T(8,128)S(1)} %get-tuple-element.92), channel_id=1, source_target_pairs={{0,8},{8,0},{16,24},{24,16},{1,9},{9,1},{17,25},{25,17},{2,10},{10... | collective-permute-start | bytes 1572872 | tf_op jit(solution)/shard_map/ppermute | solution.py:640
  87.1 4.3 %shard_map.178 = (bf16[128,2048]{1,0:T(8,128)(2,1)}, bf16[128,2048]{1,0:T(8,128)(2,1)}, f32[128,128]{1,0:T(8,128)S(1)}, f32[128,128]{1,0:T(8,128)S(1)}, f32[8,128]{1,0:T(8,128)S(1)}) custom-call(s32[65]{0:T(128)S(1)} %concatenate.3.meta.refs_0_, f32[16]{0:T(128)S(1)} %copy-done.1, ...), custom_call_target="tpu_custom_call", output_to_operand_aliasing={{4}: (17, {})} | custom-call | tf_op jit(solution)/shard_map/pallas_call | solution.py:406
  91.4 2.3 %collective-permute-start.17 = (f32[8,128]{1,0:T(8,128)S(1)}, f32[8,128]{1,0:T(8,128)S(1)}, u32[]{:S(2)}, u32[]{:S(2)}) collective-permute-start(f32[8,128]{1,0:T(8,128)S(1)} %get-tuple-element.95.refs_2_), channel_id=1, source_target_pairs={{0,16},{8,24},{16,0},{24,8},{1,17},{9,25},{17,1},{25,9},{2,18},{10... | collective-permute-start | bytes 12296 | tf_op jit(solution)/shard_map/ppermute | solution.py:722
  93.8 2.0 %collective-permute-start.18 = (f32[8,128]{1,0:T(8,128)S(1)}, f32[8,128]{1,0:T(8,128)S(1)}, u32[]{:S(2)}, u32[]{:S(2)}) collective-permute-start(f32[8,128]{1,0:T(8,128)S(1)} %get-tuple-element.95.refs_2_), channel_id=1, source_target_pairs={{0,24},{8,16},{16,8},{24,0},{1,25},{9,17},{17,9},{25,1},{2,26},{10... | collective-permute-start | bytes 12296 | tf_op jit(solution)/shard_map/ppermute | solution.py:722
  96.0 3.2 %collective-permute-done.18.refs_5_ = f32[8,128]{1,0:T(8,128)S(1)} collective-permute-done((f32[8,128]{1,0:T(8,128)S(1)}, f32[8,128]{1,0:T(8,128)S(1)}, u32[]{:S(2)}, u32[]{:S(2)}) %collective-permute-start.18) | collective-permute-done | bytes 4128 | tf_op jit(solution)/shard_map/ppermute | solution.py:722
  99.2 2.7 %shard_map.179 = (bf16[128,2048]{1,0:T(8,128)(2,1)}, bf16[128,2048]{1,0:T(8,128)(2,1)}, bf16[128,128]{1,0:T(8,128)(2,1)}, bf16[128,128]{1,0:T(8,128)(2,1)}, f32[4,128]{1,0:T(4,128)}, /*index=5*/f32[1,16]{1,0:T(1,128)}) custom-call(s32[65]{0:T(128)S(1)} %concatenate.3.meta.refs_0_, f32[16]{0:T(128)S(1)} %copy-done.1, ...), custom_call_target="tpu_custom_call", output_to_operand_aliasing={{0}: (18, {}), {1}: (19, {})} | custom-call | tf_op jit(solution)/shard_map/pallas_call | solution.py:406
  (44 shorter events, 14.2 us)
Async XLA Ops:
  0.6 9.6 %collective-permute-start = (f32[4,128,128]{2,1,0:T(8,128)}, f32[4,128,128]{2,1,0:T(8,128)S(1)}, u32[]{:S(2)}, u32[]{:S(2)}) collective-permute-start(f32[4,128,128]{2,1,0:T(8,128)} %bitcast.23), channel_id=1, source_target_pairs={{0,8},{8,0},{16,24},{24,16},{1,9},{9,1},{17,25},{25,17},{2,10},{10... | collective-permute-start | bytes 786440 | tf_op jit(solution)/shard_map/ppermute | solution.py:527
  10.2 1.0 copy-start
  12.0 14.6 %collective-permute-start.2 = (f32[288,512]{1,0:T(8,128)S(1)}, f32[288,512]{1,0:T(8,128)S(1)}, u32[]{:S(2)}, u32[]{:S(2)}) collective-permute-start(f32[288,512]{1,0:T(8,128)S(1)} %get-tuple-element.67), channel_id=1, source_target_pairs={{0,8},{8,0},{16,24},{24,16},{1,9},{9,1},{17,25},{25,17},{2,10},{10... | collective-permute-start | bytes 1769480 | tf_op jit(solution)/shard_map/ppermute | solution.py:640
  13.9 13.4 %collective-permute-start.1 = (f32[288,512]{1,0:T(8,128)S(1)}, f32[288,512]{1,0:T(8,128)S(1)}, u32[]{:S(2)}, u32[]{:S(2)}) collective-permute-start(f32[288,512]{1,0:T(8,128)S(1)} %get-tuple-element.64), channel_id=1, source_target_pairs={{8,16},{16,8},{9,17},{17,9},{10,18},{18,10},{11,19},{19,11},{12,20... | collective-permute-start | bytes 1769480 | tf_op jit(solution)/shard_map/ppermute | solution.py:642
  27.9 15.4 %collective-permute-start.3 = (f32[288,512]{1,0:T(8,128)S(1)}, f32[288,512]{1,0:T(8,128)S(1)}, u32[]{:S(2)}, u32[]{:S(2)}) collective-permute-start(f32[288,512]{1,0:T(8,128)S(1)} %get-tuple-element.70), channel_id=1, source_target_pairs={{0,8},{8,0},{16,24},{24,16},{1,9},{9,1},{17,25},{25,17},{2,10},{10... | collective-permute-start | bytes 1769480 | tf_op jit(solution)/shard_map/ppermute | solution.py:640
  31.8 12.2 %collective-permute-start.5 = (f32[288,512]{1,0:T(8,128)S(1)}, f32[288,512]{1,0:T(8,128)S(1)}, u32[]{:S(2)}, u32[]{:S(2)}) collective-permute-start(f32[288,512]{1,0:T(8,128)S(1)} %get-tuple-element.74), channel_id=1, source_target_pairs={{8,16},{16,8},{9,17},{17,9},{10,18},{18,10},{11,19},{19,11},{12,20... | collective-permute-start | bytes 1769480 | tf_op jit(solution)/shard_map/ppermute | solution.py:642
  44.6 13.7 %collective-permute-start.6 = (f32[288,512]{1,0:T(8,128)S(1)}, f32[288,512]{1,0:T(8,128)S(1)}, u32[]{:S(2)}, u32[]{:S(2)}) collective-permute-start(f32[288,512]{1,0:T(8,128)S(1)} %get-tuple-element.77), channel_id=1, source_target_pairs={{0,8},{8,0},{16,24},{24,16},{1,9},{9,1},{17,25},{25,17},{2,10},{10... | collective-permute-start | bytes 1769480 | tf_op jit(solution)/shard_map/ppermute | solution.py:640
  47.7 11.3 %collective-permute-start.4 = (f32[288,512]{1,0:T(8,128)S(1)}, f32[288,512]{1,0:T(8,128)S(1)}, u32[]{:S(2)}, u32[]{:S(2)}) collective-permute-start(f32[288,512]{1,0:T(8,128)S(1)} %get-tuple-element.73), channel_id=1, source_target_pairs={{8,16},{16,8},{9,17},{17,9},{10,18},{18,10},{11,19},{19,11},{12,20... | collective-permute-start | bytes 1769480 | tf_op jit(solution)/shard_map/ppermute | solution.py:642
  48.4 34.9 %collective-permute-start.12 = (f32[5,128,512]{2,1,0:T(8,128)S(1)}, f32[5,128,512]{2,1,0:T(8,128)S(1)}, u32[]{:S(2)}, u32[]{:S(2)}) collective-permute-start(f32[5,128,512]{2,1,0:T(8,128)S(1)} %get-tuple-element.88.begin_here), channel_id=1, source_target_pairs={{0,4},{4,0},{1,5},{5,1},{2,6},{6,2},{3,7},{7,3},{8,12},{12,8},{9,1... | collective-permute-start | bytes 3932168 | tf_op jit(solution)/shard_map/ppermute | solution.py:649
  59.6 11.4 %collective-permute-start.7 = (f32[256,512]{1,0:T(8,128)S(1)}, f32[256,512]{1,0:T(8,128)S(1)}, u32[]{:S(2)}, u32[]{:S(2)}) collective-permute-start(f32[256,512]{1,0:T(8,128)S(1)} %get-tuple-element.80), channel_id=1, source_target_pairs={{0,8},{8,0},{16,24},{24,16},{1,9},{9,1},{17,25},{25,17},{2,10},{10... | collective-permute-start | bytes 1572872 | tf_op jit(solution)/shard_map/ppermute | solution.py:640
  62.6 8.9 %collective-permute-start.9 = (f32[256,512]{1,0:T(8,128)S(1)}, f32[256,512]{1,0:T(8,128)S(1)}, u32[]{:S(2)}, u32[]{:S(2)}) collective-permute-start(f32[256,512]{1,0:T(8,128)S(1)} %get-tuple-element.84), channel_id=1, source_target_pairs={{8,16},{16,8},{9,17},{17,9},{10,18},{18,10},{11,19},{19,11},{12,20... | collective-permute-start | bytes 1572872 | tf_op jit(solution)/shard_map/ppermute | solution.py:642
  64.8 1.2 %collective-permute-start.10 = (f32[8,128]{1,0:T(8,128)S(1)}, f32[8,128]{1,0:T(8,128)S(1)}, u32[]{:S(2)}, u32[]{:S(2)}) collective-permute-start(f32[8,128]{1,0:T(8,128)S(1)} %shard_map.173.refs_5_), channel_id=1, source_target_pairs={{0,1},{1,0},{2,3},{3,2},{4,5},{5,4},{6,7},{7,6},{8,9},{9,8},{10,11... | collective-permute-start | bytes 12296 | tf_op jit(solution)/shard_map/ppermute | solution.py:452
  72.2 11.0 %collective-permute-start.11 = (f32[256,512]{1,0:T(8,128)S(1)}, f32[256,512]{1,0:T(8,128)S(1)}, u32[]{:S(2)}, u32[]{:S(2)}) collective-permute-start(f32[256,512]{1,0:T(8,128)S(1)} %get-tuple-element.86), channel_id=1, source_target_pairs={{0,8},{8,0},{16,24},{24,16},{1,9},{9,1},{17,25},{25,17},{2,10},{10... | collective-permute-start | bytes 1572872 | tf_op jit(solution)/shard_map/ppermute | solution.py:640
  75.3 8.6 %collective-permute-start.8 = (f32[256,512]{1,0:T(8,128)S(1)}, f32[256,512]{1,0:T(8,128)S(1)}, u32[]{:S(2)}, u32[]{:S(2)}) collective-permute-start(f32[256,512]{1,0:T(8,128)S(1)} %get-tuple-element.83), channel_id=1, source_target_pairs={{8,16},{16,8},{9,17},{17,9},{10,18},{18,10},{11,19},{19,11},{12,20... | collective-permute-start | bytes 1572872 | tf_op jit(solution)/shard_map/ppermute | solution.py:642
  76.0 3.7 %collective-permute-start.13 = (f32[8,128]{1,0:T(8,128)S(1)}, f32[8,128]{1,0:T(8,128)S(1)}, u32[]{:S(2)}, u32[]{:S(2)}) collective-permute-start(f32[8,128]{1,0:T(8,128)S(1)} %add.42.refs_5_), channel_id=1, source_target_pairs={{0,2},{1,3},{2,0},{3,1},{4,6},{5,7},{6,4},{7,5},{8,10},{9,11},{10,... | collective-permute-start | bytes 12296 | tf_op jit(solution)/shard_map/ppermute | solution.py:452
  79.6 3.6 %collective-permute-start.14 = (f32[8,128]{1,0:T(8,128)S(1)}, f32[8,128]{1,0:T(8,128)S(1)}, u32[]{:S(2)}, u32[]{:S(2)}) collective-permute-start(f32[8,128]{1,0:T(8,128)S(1)} %add.43.refs_6_), channel_id=1, source_target_pairs={{0,4},{4,0},{1,5},{5,1},{2,6},{6,2},{3,7},{7,3},{8,12},{12,8},{9,1... | collective-permute-start | bytes 12296 | tf_op jit(solution)/shard_map/ppermute | solution.py:452
  83.8 3.2 %copy-start.1 = (f32[16]{0:T(128)S(1)}, f32[16]{0:T(128)}, u32[]{:S(2)}) copy-start(f32[16]{0:T(128)} %gains.3) | copy-start | bytes 196
  84.5 14.7 %collective-permute-start.15 = (f32[256,512]{1,0:T(8,128)S(1)}, f32[256,512]{1,0:T(8,128)S(1)}, u32[]{:S(2)}, u32[]{:S(2)}) collective-permute-start(f32[256,512]{1,0:T(8,128)S(1)} %get-tuple-element.92), channel_id=1, source_target_pairs={{0,8},{8,0},{16,24},{24,16},{1,9},{9,1},{17,25},{25,17},{2,10},{10... | collective-permute-start | bytes 1572872 | tf_op jit(solution)/shard_map/ppermute | solution.py:640
  91.4 4.4 %collective-permute-start.16 = (f32[8,128]{1,0:T(8,128)S(1)}, f32[8,128]{1,0:T(8,128)S(1)}, u32[]{:S(2)}, u32[]{:S(2)}) collective-permute-start(f32[8,128]{1,0:T(8,128)S(1)} %get-tuple-element.95.refs_2_), channel_id=1, source_target_pairs={{0,8},{8,0},{16,24},{24,16},{1,9},{9,1},{17,25},{25,17},{2,10},{10... | collective-permute-start | bytes 12296 | tf_op jit(solution)/shard_map/ppermute | solution.py:722
  91.4 4.5 %collective-permute-start.17 = (f32[8,128]{1,0:T(8,128)S(1)}, f32[8,128]{1,0:T(8,128)S(1)}, u32[]{:S(2)}, u32[]{:S(2)}) collective-permute-start(f32[8,128]{1,0:T(8,128)S(1)} %get-tuple-element.95.refs_2_), channel_id=1, source_target_pairs={{0,16},{8,24},{16,0},{24,8},{1,17},{9,25},{17,1},{25,9},{2,18},{10... | collective-permute-start | bytes 12296 | tf_op jit(solution)/shard_map/ppermute | solution.py:722
  93.8 5.4 %collective-permute-start.18 = (f32[8,128]{1,0:T(8,128)S(1)}, f32[8,128]{1,0:T(8,128)S(1)}, u32[]{:S(2)}, u32[]{:S(2)}) collective-permute-start(f32[8,128]{1,0:T(8,128)S(1)} %get-tuple-element.95.refs_2_), channel_id=1, source_target_pairs={{0,24},{8,16},{16,8},{24,0},{1,25},{9,17},{17,9},{25,1},{2,26},{10... | collective-permute-start | bytes 12296 | tf_op jit(solution)/shard_map/ppermute | solution.py:722

commit v6 on v5

--- a/solution.py
+++ b/solution.py
@@ -43,8 +43,8 @@
 
 def start_kernel(
     per_chunk, head_dim, vocab, chunks,
-    meta, bmat, cmat, tokens, table, step_t, rate_t, hid_far, cot_far,
-    x_first, y_first, small, cols, writer, hid, cot, sems,
+    meta, bmat, cmat, tokens, table, step_t, rate_t, hid_far, cot_far, state_far,
+    x_first, y_first, small, cols, writer, hid, cot, state_near, sems,
 ):
     length = bmat.shape[0]
     state = bmat.shape[1]
@@ -61,6 +61,8 @@
         for copy in pair:
             copy.start()
         copies.append(pair)
+    keep = pltpu.make_async_copy(state_far, state_near, sems.at[chunks, 0])
+    keep.start()
 
     row = lax.broadcasted_iota(jnp.int32, (length, length), 0)
     col = lax.broadcasted_iota(jnp.int32, (length, length), 1)
@@ -122,6 +124,7 @@
             x_first[0:state, :] = dot(rows.T, ends)
             x_first[state : 2 * state, :] = dot(cmat[...].T, grad_ends)
             y_first[0 : 2 * state, :] = jnp.zeros((2 * state, part), F32)
+    keep.wait()
 
 
 def head_copies(source, target, row, sems):
@@ -540,27 +543,31 @@
     small_shape = (2, chunks, lines, part)
     first = ((full_rows, part), F32, near, CHIP)
 
-    x_first, y_first, small, cols, writer, hid, cot = call(
+    x_first, y_first, small, cols, writer, hid, cot, kept = call(
         functools.partial(start_kernel, per_chunk, head_dim, vocab, chunks),
         (meta,), (1,),
         [
             (writes, square, HBM), (reads, square, HBM), (toks, tok_spec, HBM),
             (table, whole(table.shape), HBM), (steps_t, whole(steps_t.shape), HBM),
             (rates_t, whole(rates_t.shape), HBM), (hid, anywhere, HBM), (cot, anywhere, HBM),
+            (own_state, anywhere, HBM),
         ],
         [
             first, first,
             (small_shape, F32, near, CHIP),
             ((chunks, length, 128), F32, near, CHIP), ((length, state_dim), BF16, near, CHIP),
             ((length, width), BF16, near, CHIP), ((length, width), BF16, near, CHIP),
-        ],
-        [pltpu.SemaphoreType.DMA((chunks, 2))],
-    )
-
+            (own_state.shape, F32, near, CHIP),
+        ],
+        [pltpu.SemaphoreType.DMA((chunks + 1, 2))],
+    )
+
+    if paired:
+        pieces[1] = kept
     x_first, y_first = call(
         functools.partial(relay_kernel, count - 1, paired),
         (meta,), (),
-        [(piece, anywhere, None) for piece in pieces]
+        [(piece, anywhere, CHIP if piece is kept else None) for piece in pieces]
         + [(x_first, near, CHIP), (y_first, near, CHIP)],
         [
             ((full_rows, part), F32, near, CHIP), ((full_rows, part), F32, near, CHIP),
@@ -573,7 +580,8 @@
         functools.partial(gather_kernel, count - 1, paired),
         (meta,), (),
         [
-            (piece, anywhere, None) for piece in (pieces if paired else pieces + [own_state])
+            (piece, anywhere, CHIP if piece is kept else None)
+            for piece in (pieces if paired else pieces + [kept])
         ],
         [(begin_shape, F32, near, CHIP)],
         [pltpu.SemaphoreType.DMA((3, local_heads))],

time: 102 us -> 101 us (level)
  transfers between devices with their start and end apart: 19 -> 19, of which waited for: 10 -> 10; matrix products, arithmetic and copies ran while one was open for 0% -> 0% of each run, Pallas kernels for 21% -> 20%
where the time goes in v6:
time: 101 us
  waiting for transfers between devices  39.5 us (39%)
  starting transfers between devices  33 us (33%)
  Pallas kernels  26.1 us (26%)
  between operations  2.2 us (2%)
    ppermute x6, waiting for transfers between devices, per_device(): got_x = lax.ppermute(send_x, 'ctx', even_links)  30 us
    pallas_call x17, Pallas kernels, call(): pl.pallas_call(body, out_shape=[jax.ShapeDtypeStruct(shape, kind) if plac...  26.1 us
    ppermute x6, starting transfers between devices, per_device(): got_x = lax.ppermute(send_x, 'ctx', even_links)  17.4 us
    ppermute x3, waiting for transfers between devices, sum_steps(): steps.append(lambda value, group=group: value + group[0](value))  5.36 us
    ppermute x3, starting transfers between devices, per_device(): exchanged = [exchange(total) for exchange in exchanges]  4.39 us
    ppermute x5, starting transfers between devices, per_device(): got_y = lax.ppermute(send_y, 'ctx', odd_links)  3.42 us
    ppermute x3, waiting for transfers between devices, per_device(): exchanged = [exchange(total) for exchange in exchanges]  3.37 us
    ppermute x3, starting transfers between devices, sum_steps(): steps.append(lambda value, group=group: value + group[0](value))  3.11 us
  transfers between devices with their start and end apart: 19, of which 10 were waited for; matrix products, arithmetic and copies ran while one was open for 0% of the time, Pallas kernels for 20%

profile of v6, /device:TPU:0, one launch (start us, length us, event | category | flops | bytes accessed | tf_op | source)
XLA Modules:
  0.0 100.9 jit_solution(934940014871498102)
XLA Ops:
  0.6 3.1 %collective-permute-start = (f32[4,128,128]{2,1,0:T(8,128)}, f32[4,128,128]{2,1,0:T(8,128)S(1)}, u32[]{:S(2)}, u32[]{:S(2)}) collective-permute-start(f32[4,128,128]{2,1,0:T(8,128)} %bitcast.31), channel_id=1, source_target_pairs={{0,8},{8,0},{16,24},{24,16},{1,9},{9,1},{17,25},{25,17},{2,10},{10... | collective-permute-start | bytes 786440 | tf_op jit(solution)/shard_map/ppermute | solution.py:530
  5.2 4.3 %shard_map.163 = (f32[288,512]{1,0:T(8,128)S(1)}, f32[288,512]{1,0:T(8,128)S(1)}, f32[2,4,8,512]{3,2,1,0:T(8,128)S(1)}, f32[4,128,128]{2,1,0:T(8,128)S(1)}, bf16...) custom-call(s32[65]{0:T(128)S(1)} %concatenate.3.meta.refs_0_, ...), custom_call_target="tpu_custom_call" | custom-call | tf_op jit(solution)/shard_map/pallas_call | solution.py:409
  11.1 1.9 %collective-permute-start.2 = (f32[288,512]{1,0:T(8,128)S(1)}, f32[288,512]{1,0:T(8,128)S(1)}, u32[]{:S(2)}, u32[]{:S(2)}) collective-permute-start(f32[288,512]{1,0:T(8,128)S(1)} %get-tuple-element.69), channel_id=1, source_target_pairs={{0,8},{8,0},{16,24},{24,16},{1,9},{9,1},{17,25},{25,17},{2,10},{10... | collective-permute-start | bytes 1769480 | tf_op jit(solution)/shard_map/ppermute | solution.py:648
  13.7 5.4 %shard_map.164 = (f32[2,4,2,128,512]{4,3,2,1,0:T(8,128)S(1)}, f32[128,2048]{1,0:T(8,128)S(1)}, f32[128,2048]{1,0:T(8,128)S(1)}, f32[128,128]{1,0:T(8,128)S(1)}, ...) custom-call(s32[65]{0:T(128)S(1)} %concatenate.3.meta.refs_0_, bf16[128,2048]{1,0:T(8,128)(2,1)S(1)} %get-tuple-element.55.hid, ...), custom_call_target="tpu_custom_call" | custom-call | tf_op jit(solution)/shard_map/pallas_call | solution.py:409
  19.8 5.9 %collective-permute-done.2.refs_1_ = f32[288,512]{1,0:T(8,128)S(1)} collective-permute-done((f32[288,512]{1,0:T(8,128)S(1)}, f32[288,512]{1,0:T(8,128)S(1)}, u32[]{:S(2)}, u32[]{:S(2)}) %collective-permute-start.2) | collective-permute-done | bytes 589856 | tf_op jit(solution)/shard_map/ppermute | solution.py:648
  27.0 3.8 %collective-permute-start.3 = (f32[288,512]{1,0:T(8,128)S(1)}, f32[288,512]{1,0:T(8,128)S(1)}, u32[]{:S(2)}, u32[]{:S(2)}) collective-permute-start(f32[288,512]{1,0:T(8,128)S(1)} %get-tuple-element.72), channel_id=1, source_target_pairs={{0,8},{8,0},{16,24},{24,16},{1,9},{9,1},{17,25},{25,17},{2,10},{10... | collective-permute-start | bytes 1769480 | tf_op jit(solution)/shard_map/ppermute | solution.py:648
  31.5 10.8 %collective-permute-done.3.refs_1_ = f32[288,512]{1,0:T(8,128)S(1)} collective-permute-done((f32[288,512]{1,0:T(8,128)S(1)}, f32[288,512]{1,0:T(8,128)S(1)}, u32[]{:S(2)}, u32[]{:S(2)}) %collective-permute-start.3) | collective-permute-done | bytes 589856 | tf_op jit(solution)/shard_map/ppermute | solution.py:648
  43.7 3.0 %collective-permute-start.6 = (f32[288,512]{1,0:T(8,128)S(1)}, f32[288,512]{1,0:T(8,128)S(1)}, u32[]{:S(2)}, u32[]{:S(2)}) collective-permute-start(f32[288,512]{1,0:T(8,128)S(1)} %get-tuple-element.79), channel_id=1, source_target_pairs={{0,8},{8,0},{16,24},{24,16},{1,9},{9,1},{17,25},{25,17},{2,10},{10... | collective-permute-start | bytes 1769480 | tf_op jit(solution)/shard_map/ppermute | solution.py:648
  47.4 1.6 %collective-permute-start.12 = (f32[5,128,512]{2,1,0:T(8,128)S(1)}, f32[5,128,512]{2,1,0:T(8,128)S(1)}, u32[]{:S(2)}, u32[]{:S(2)}) collective-permute-start(f32[5,128,512]{2,1,0:T(8,128)S(1)} %get-tuple-element.90.begin_here), channel_id=1, source_target_pairs={{0,4},{4,0},{1,5},{5,1},{2,6},{6,2},{3,7},{7,3},{8,12},{12,8},{9,1... | collective-permute-start | bytes 3932168 | tf_op jit(solution)/shard_map/ppermute | solution.py:657
  49.0 8.3 %collective-permute-done.6.refs_1_.from_x = f32[288,512]{1,0:T(8,128)S(1)} collective-permute-done((f32[288,512]{1,0:T(8,128)S(1)}, f32[288,512]{1,0:T(8,128)S(1)}, u32[]{:S(2)}, u32[]{:S(2)}) %collective-permute-start.6) | collective-permute-done | bytes 589856 | tf_op jit(solution)/shard_map/ppermute | solution.py:648
  58.6 3.1 %collective-permute-start.7 = (f32[256,512]{1,0:T(8,128)S(1)}, f32[256,512]{1,0:T(8,128)S(1)}, u32[]{:S(2)}, u32[]{:S(2)}) collective-permute-start(f32[256,512]{1,0:T(8,128)S(1)} %get-tuple-element.82), channel_id=1, source_target_pairs={{0,8},{8,0},{16,24},{24,16},{1,9},{9,1},{17,25},{25,17},{2,10},{10... | collective-permute-start | bytes 1572872 | tf_op jit(solution)/shard_map/ppermute | solution.py:648
  62.4 1.5 %shard_map.173.refs_5_ = f32[8,128]{1,0:T(8,128)S(1)} custom-call(s32[65]{0:T(128)S(1)} %concatenate.3.meta.refs_0_, f32[288,512]{1,0:T(8,128)S(1)} %collective-permute-done.6.refs_1_.from_x, f32[288,512]{1,0:T(8,128)S(1)} %collective-permute-done.4.refs_1_.from_y, f32[2,4,8,512]{3,2,1,0:T(8,128)S(1)} %get-tuple-element.68.refs_3_.small, ...), custom_call_target="tpu_custom_call" | custom-call | tf_op jit(solution)/shard_map/pallas_call | solution.py:409
  65.0 4.9 %collective-permute-done.7.refs_1_ = f32[256,512]{1,0:T(8,128)S(1)} collective-permute-done((f32[256,512]{1,0:T(8,128)S(1)}, f32[256,512]{1,0:T(8,128)S(1)}, u32[]{:S(2)}, u32[]{:S(2)}) %collective-permute-start.7) | collective-permute-done | bytes 524320 | tf_op jit(solution)/shard_map/ppermute | solution.py:648
  71.3 3.1 %collective-permute-start.11 = (f32[256,512]{1,0:T(8,128)S(1)}, f32[256,512]{1,0:T(8,128)S(1)}, u32[]{:S(2)}, u32[]{:S(2)}) collective-permute-start(f32[256,512]{1,0:T(8,128)S(1)} %get-tuple-element.88), channel_id=1, source_target_pairs={{0,8},{8,0},{16,24},{24,16},{1,9},{9,1},{17,25},{25,17},{2,10},{10... | collective-permute-start | bytes 1572872 | tf_op jit(solution)/shard_map/ppermute | solution.py:648
  75.0 1.6 %collective-permute-start.13 = (f32[8,128]{1,0:T(8,128)S(1)}, f32[8,128]{1,0:T(8,128)S(1)}, u32[]{:S(2)}, u32[]{:S(2)}) collective-permute-start(f32[8,128]{1,0:T(8,128)S(1)} %add.42.refs_5_), channel_id=1, source_target_pairs={{0,2},{1,3},{2,0},{3,1},{4,6},{5,7},{6,4},{7,5},{8,10},{9,11},{10,... | collective-permute-start | bytes 12296 | tf_op jit(solution)/shard_map/ppermute | solution.py:455
  76.6 2.1 %collective-permute-done.13 = f32[8,128]{1,0:T(8,128)S(1)} collective-permute-done((f32[8,128]{1,0:T(8,128)S(1)}, f32[8,128]{1,0:T(8,128)S(1)}, u32[]{:S(2)}, u32[]{:S(2)}) %collective-permute-start.13) | collective-permute-done | bytes 4128 | tf_op jit(solution)/shard_map/ppermute | solution.py:455
  78.7 1.5 %collective-permute-start.14 = (f32[8,128]{1,0:T(8,128)S(1)}, f32[8,128]{1,0:T(8,128)S(1)}, u32[]{:S(2)}, u32[]{:S(2)}) collective-permute-start(f32[8,128]{1,0:T(8,128)S(1)} %add.43.refs_6_), channel_id=1, source_target_pairs={{0,4},{4,0},{1,5},{5,1},{2,6},{6,2},{3,7},{7,3},{8,12},{12,8},{9,1... | collective-permute-start | bytes 12296 | tf_op jit(solution)/shard_map/ppermute | solution.py:455
  80.2 2.1 %collective-permute-done.14 = f32[8,128]{1,0:T(8,128)S(1)} collective-permute-done((f32[8,128]{1,0:T(8,128)S(1)}, f32[8,128]{1,0:T(8,128)S(1)}, u32[]{:S(2)}, u32[]{:S(2)}) %collective-permute-start.14) | collective-permute-done | bytes 4128 | tf_op jit(solution)/shard_map/ppermute | solution.py:455
  83.6 2.6 %collective-permute-start.15 = (f32[256,512]{1,0:T(8,128)S(1)}, f32[256,512]{1,0:T(8,128)S(1)}, u32[]{:S(2)}, u32[]{:S(2)}) collective-permute-start(f32[256,512]{1,0:T(8,128)S(1)} %get-tuple-element.94), channel_id=1, source_target_pairs={{0,8},{8,0},{16,24},{24,16},{1,9},{9,1},{17,25},{25,17},{2,10},{10... | collective-permute-start | bytes 1572872 | tf_op jit(solution)/shard_map/ppermute | solution.py:648
  86.1 4.3 %shard_map.178 = (bf16[128,2048]{1,0:T(8,128)(2,1)}, bf16[128,2048]{1,0:T(8,128)(2,1)}, f32[128,128]{1,0:T(8,128)S(1)}, f32[128,128]{1,0:T(8,128)S(1)}, f32[8,128]{1,0:T(8,128)S(1)}) custom-call(s32[65]{0:T(128)S(1)} %concatenate.3.meta.refs_0_, f32[16]{0:T(128)S(1)} %copy-done, ...), custom_call_target="tpu_custom_call", output_to_operand_aliasing={{4}: (17, {})} | custom-call | tf_op jit(solution)/shard_map/pallas_call | solution.py:409
  90.5 2.3 %collective-permute-start.17 = (f32[8,128]{1,0:T(8,128)S(1)}, f32[8,128]{1,0:T(8,128)S(1)}, u32[]{:S(2)}, u32[]{:S(2)}) collective-permute-start(f32[8,128]{1,0:T(8,128)S(1)} %get-tuple-element.97.refs_2_), channel_id=1, source_target_pairs={{0,16},{8,24},{16,0},{24,8},{1,17},{9,25},{17,1},{25,9},{2,18},{10... | collective-permute-start | bytes 12296 | tf_op jit(solution)/shard_map/ppermute | solution.py:730
  92.8 2.0 %collective-permute-start.18 = (f32[8,128]{1,0:T(8,128)S(1)}, f32[8,128]{1,0:T(8,128)S(1)}, u32[]{:S(2)}, u32[]{:S(2)}) collective-permute-start(f32[8,128]{1,0:T(8,128)S(1)} %get-tuple-element.97.refs_2_), channel_id=1, source_target_pairs={{0,24},{8,16},{16,8},{24,0},{1,25},{9,17},{17,9},{25,1},{2,26},{10... | collective-permute-start | bytes 12296 | tf_op jit(solution)/shard_map/ppermute | solution.py:730
  95.0 3.2 %collective-permute-done.18.refs_5_ = f32[8,128]{1,0:T(8,128)S(1)} collective-permute-done((f32[8,128]{1,0:T(8,128)S(1)}, f32[8,128]{1,0:T(8,128)S(1)}, u32[]{:S(2)}, u32[]{:S(2)}) %collective-permute-start.18) | collective-permute-done | bytes 4128 | tf_op jit(solution)/shard_map/ppermute | solution.py:730
  98.2 2.7 %shard_map.179 = (bf16[128,2048]{1,0:T(8,128)(2,1)}, bf16[128,2048]{1,0:T(8,128)(2,1)}, bf16[128,128]{1,0:T(8,128)(2,1)}, bf16[128,128]{1,0:T(8,128)(2,1)}, f32[4,128]{1,0:T(4,128)}, /*index=5*/f32[1,16]{1,0:T(1,128)}) custom-call(s32[65]{0:T(128)S(1)} %concatenate.3.meta.refs_0_, f32[16]{0:T(128)S(1)} %copy-done, ...), custom_call_target="tpu_custom_call", output_to_operand_aliasing={{0}: (18, {}), {1}: (19, {})} | custom-call | tf_op jit(solution)/shard_map/pallas_call | solution.py:409
  (42 shorter events, 13.6 us)
Async XLA Ops:
  0.6 9.6 %collective-permute-start = (f32[4,128,128]{2,1,0:T(8,128)}, f32[4,128,128]{2,1,0:T(8,128)S(1)}, u32[]{:S(2)}, u32[]{:S(2)}) collective-permute-start(f32[4,128,128]{2,1,0:T(8,128)} %bitcast.31), channel_id=1, source_target_pairs={{0,8},{8,0},{16,24},{24,16},{1,9},{9,1},{17,25},{25,17},{2,10},{10... | collective-permute-start | bytes 786440 | tf_op jit(solution)/shard_map/ppermute | solution.py:530
  11.1 14.6 %collective-permute-start.2 = (f32[288,512]{1,0:T(8,128)S(1)}, f32[288,512]{1,0:T(8,128)S(1)}, u32[]{:S(2)}, u32[]{:S(2)}) collective-permute-start(f32[288,512]{1,0:T(8,128)S(1)} %get-tuple-element.69), channel_id=1, source_target_pairs={{0,8},{8,0},{16,24},{24,16},{1,9},{9,1},{17,25},{25,17},{2,10},{10... | collective-permute-start | bytes 1769480 | tf_op jit(solution)/shard_map/ppermute | solution.py:648
  13.0 13.4 %collective-permute-start.1 = (f32[288,512]{1,0:T(8,128)S(1)}, f32[288,512]{1,0:T(8,128)S(1)}, u32[]{:S(2)}, u32[]{:S(2)}) collective-permute-start(f32[288,512]{1,0:T(8,128)S(1)} %get-tuple-element.66), channel_id=1, source_target_pairs={{8,16},{16,8},{9,17},{17,9},{10,18},{18,10},{11,19},{19,11},{12,20... | collective-permute-start | bytes 1769480 | tf_op jit(solution)/shard_map/ppermute | solution.py:650
  27.0 15.4 %collective-permute-start.3 = (f32[288,512]{1,0:T(8,128)S(1)}, f32[288,512]{1,0:T(8,128)S(1)}, u32[]{:S(2)}, u32[]{:S(2)}) collective-permute-start(f32[288,512]{1,0:T(8,128)S(1)} %get-tuple-element.72), channel_id=1, source_target_pairs={{0,8},{8,0},{16,24},{24,16},{1,9},{9,1},{17,25},{25,17},{2,10},{10... | collective-permute-start | bytes 1769480 | tf_op jit(solution)/shard_map/ppermute | solution.py:648
  30.8 12.2 %collective-permute-start.5 = (f32[288,512]{1,0:T(8,128)S(1)}, f32[288,512]{1,0:T(8,128)S(1)}, u32[]{:S(2)}, u32[]{:S(2)}) collective-permute-start(f32[288,512]{1,0:T(8,128)S(1)} %get-tuple-element.76), channel_id=1, source_target_pairs={{8,16},{16,8},{9,17},{17,9},{10,18},{18,10},{11,19},{19,11},{12,20... | collective-permute-start | bytes 1769480 | tf_op jit(solution)/shard_map/ppermute | solution.py:650
  43.7 13.7 %collective-permute-start.6 = (f32[288,512]{1,0:T(8,128)S(1)}, f32[288,512]{1,0:T(8,128)S(1)}, u32[]{:S(2)}, u32[]{:S(2)}) collective-permute-start(f32[288,512]{1,0:T(8,128)S(1)} %get-tuple-element.79), channel_id=1, source_target_pairs={{0,8},{8,0},{16,24},{24,16},{1,9},{9,1},{17,25},{25,17},{2,10},{10... | collective-permute-start | bytes 1769480 | tf_op jit(solution)/shard_map/ppermute | solution.py:648
  46.7 11.3 %collective-permute-start.4 = (f32[288,512]{1,0:T(8,128)S(1)}, f32[288,512]{1,0:T(8,128)S(1)}, u32[]{:S(2)}, u32[]{:S(2)}) collective-permute-start(f32[288,512]{1,0:T(8,128)S(1)} %get-tuple-element.75), channel_id=1, source_target_pairs={{8,16},{16,8},{9,17},{17,9},{10,18},{18,10},{11,19},{19,11},{12,20... | collective-permute-start | bytes 1769480 | tf_op jit(solution)/shard_map/ppermute | solution.py:650
  47.4 34.9 %collective-permute-start.12 = (f32[5,128,512]{2,1,0:T(8,128)S(1)}, f32[5,128,512]{2,1,0:T(8,128)S(1)}, u32[]{:S(2)}, u32[]{:S(2)}) collective-permute-start(f32[5,128,512]{2,1,0:T(8,128)S(1)} %get-tuple-element.90.begin_here), channel_id=1, source_target_pairs={{0,4},{4,0},{1,5},{5,1},{2,6},{6,2},{3,7},{7,3},{8,12},{12,8},{9,1... | collective-permute-start | bytes 3932168 | tf_op jit(solution)/shard_map/ppermute | solution.py:657
  58.6 11.4 %collective-permute-start.7 = (f32[256,512]{1,0:T(8,128)S(1)}, f32[256,512]{1,0:T(8,128)S(1)}, u32[]{:S(2)}, u32[]{:S(2)}) collective-permute-start(f32[256,512]{1,0:T(8,128)S(1)} %get-tuple-element.82), channel_id=1, source_target_pairs={{0,8},{8,0},{16,24},{24,16},{1,9},{9,1},{17,25},{25,17},{2,10},{10... | collective-permute-start | bytes 1572872 | tf_op jit(solution)/shard_map/ppermute | solution.py:648
  61.7 8.9 %collective-permute-start.9 = (f32[256,512]{1,0:T(8,128)S(1)}, f32[256,512]{1,0:T(8,128)S(1)}, u32[]{:S(2)}, u32[]{:S(2)}) collective-permute-start(f32[256,512]{1,0:T(8,128)S(1)} %get-tuple-element.86), channel_id=1, source_target_pairs={{8,16},{16,8},{9,17},{17,9},{10,18},{18,10},{11,19},{19,11},{12,20... | collective-permute-start | bytes 1572872 | tf_op jit(solution)/shard_map/ppermute | solution.py:650
  63.8 1.2 %collective-permute-start.10 = (f32[8,128]{1,0:T(8,128)S(1)}, f32[8,128]{1,0:T(8,128)S(1)}, u32[]{:S(2)}, u32[]{:S(2)}) collective-permute-start(f32[8,128]{1,0:T(8,128)S(1)} %shard_map.173.refs_5_), channel_id=1, source_target_pairs={{0,1},{1,0},{2,3},{3,2},{4,5},{5,4},{6,7},{7,6},{8,9},{9,8},{10,11... | collective-permute-start | bytes 12296 | tf_op jit(solution)/shard_map/ppermute | solution.py:455
  71.3 11.0 %collective-permute-start.11 = (f32[256,512]{1,0:T(8,128)S(1)}, f32[256,512]{1,0:T(8,128)S(1)}, u32[]{:S(2)}, u32[]{:S(2)}) collective-permute-start(f32[256,512]{1,0:T(8,128)S(1)} %get-tuple-element.88), channel_id=1, source_target_pairs={{0,8},{8,0},{16,24},{24,16},{1,9},{9,1},{17,25},{25,17},{2,10},{10... | collective-permute-start | bytes 1572872 | tf_op jit(solution)/shard_map/ppermute | solution.py:648
  74.3 8.6 %collective-permute-start.8 = (f32[256,512]{1,0:T(8,128)S(1)}, f32[256,512]{1,0:T(8,128)S(1)}, u32[]{:S(2)}, u32[]{:S(2)}) collective-permute-start(f32[256,512]{1,0:T(8,128)S(1)} %get-tuple-element.85), channel_id=1, source_target_pairs={{8,16},{16,8},{9,17},{17,9},{10,18},{18,10},{11,19},{19,11},{12,20... | collective-permute-start | bytes 1572872 | tf_op jit(solution)/shard_map/ppermute | solution.py:650
  75.0 3.7 %collective-permute-start.13 = (f32[8,128]{1,0:T(8,128)S(1)}, f32[8,128]{1,0:T(8,128)S(1)}, u32[]{:S(2)}, u32[]{:S(2)}) collective-permute-start(f32[8,128]{1,0:T(8,128)S(1)} %add.42.refs_5_), channel_id=1, source_target_pairs={{0,2},{1,3},{2,0},{3,1},{4,6},{5,7},{6,4},{7,5},{8,10},{9,11},{10,... | collective-permute-start | bytes 12296 | tf_op jit(solution)/shard_map/ppermute | solution.py:455
  78.7 3.6 %collective-permute-start.14 = (f32[8,128]{1,0:T(8,128)S(1)}, f32[8,128]{1,0:T(8,128)S(1)}, u32[]{:S(2)}, u32[]{:S(2)}) collective-permute-start(f32[8,128]{1,0:T(8,128)S(1)} %add.43.refs_6_), channel_id=1, source_target_pairs={{0,4},{4,0},{1,5},{5,1},{2,6},{6,2},{3,7},{7,3},{8,12},{12,8},{9,1... | collective-permute-start | bytes 12296 | tf_op jit(solution)/shard_map/ppermute | solution.py:455
  82.9 3.2 %copy-start = (f32[16]{0:T(128)S(1)}, f32[16]{0:T(128)}, u32[]{:S(2)}) copy-start(f32[16]{0:T(128)} %gains.3) | copy-start | bytes 196
  83.6 14.7 %collective-permute-start.15 = (f32[256,512]{1,0:T(8,128)S(1)}, f32[256,512]{1,0:T(8,128)S(1)}, u32[]{:S(2)}, u32[]{:S(2)}) collective-permute-start(f32[256,512]{1,0:T(8,128)S(1)} %get-tuple-element.94), channel_id=1, source_target_pairs={{0,8},{8,0},{16,24},{24,16},{1,9},{9,1},{17,25},{25,17},{2,10},{10... | collective-permute-start | bytes 1572872 | tf_op jit(solution)/shard_map/ppermute | solution.py:648
  90.5 4.4 %collective-permute-start.16 = (f32[8,128]{1,0:T(8,128)S(1)}, f32[8,128]{1,0:T(8,128)S(1)}, u32[]{:S(2)}, u32[]{:S(2)}) collective-permute-start(f32[8,128]{1,0:T(8,128)S(1)} %get-tuple-element.97.refs_2_), channel_id=1, source_target_pairs={{0,8},{8,0},{16,24},{24,16},{1,9},{9,1},{17,25},{25,17},{2,10},{10... | collective-permute-start | bytes 12296 | tf_op jit(solution)/shard_map/ppermute | solution.py:730
  90.5 4.5 %collective-permute-start.17 = (f32[8,128]{1,0:T(8,128)S(1)}, f32[8,128]{1,0:T(8,128)S(1)}, u32[]{:S(2)}, u32[]{:S(2)}) collective-permute-start(f32[8,128]{1,0:T(8,128)S(1)} %get-tuple-element.97.refs_2_), channel_id=1, source_target_pairs={{0,16},{8,24},{16,0},{24,8},{1,17},{9,25},{17,1},{25,9},{2,18},{10... | collective-permute-start | bytes 12296 | tf_op jit(solution)/shard_map/ppermute | solution.py:730
  92.8 5.4 %collective-permute-start.18 = (f32[8,128]{1,0:T(8,128)S(1)}, f32[8,128]{1,0:T(8,128)S(1)}, u32[]{:S(2)}, u32[]{:S(2)}) collective-permute-start(f32[8,128]{1,0:T(8,128)S(1)} %get-tuple-element.97.refs_2_), channel_id=1, source_target_pairs={{0,24},{8,16},{16,8},{24,0},{1,25},{9,17},{17,9},{25,1},{2,26},{10... | collective-permute-start | bytes 12296 | tf_op jit(solution)/shard_map/ppermute | solution.py:730

commit v7 on v6

--- a/solution.py
+++ b/solution.py
@@ -673,7 +673,7 @@
             break
         if slot >= count - 1:
             if slot > count - 1:
-                waits_down.append(begin_there)
+                waits_up.append(begin_there)
                 for step in sums[:1]:
                     total = step(total)
                 sums = sums[1:]

time: 101 us -> 100 us (0.990)
  waiting for transfers between devices: 39.5 us -> 38 us
    ppermute x3, waiting for transfers between devices: 3.37 us -> 1.91 us  [per_device(): exchanged = [exchange(total) for exchange in exchanges]]
  transfers between devices with their start and end apart: 19 -> 19, of which waited for: 10 -> 10; matrix products, arithmetic and copies ran while one was open for 0% -> 0% of each run, Pallas kernels for 20% -> 21%
where the time goes in v7:
time: 100 us; the launch traced here: 99.4 us
  waiting for transfers between devices  38 us (38%)
  starting transfers between devices  33 us (33%)
  Pallas kernels  26 us (26%)
  between operations  2.2 us (2%)
    ppermute x6, waiting for transfers between devices, per_device(): got_x = lax.ppermute(send_x, 'ctx', even_links)  30 us
    pallas_call x17, Pallas kernels, call(): pl.pallas_call(body, out_shape=[jax.ShapeDtypeStruct(shape, kind) if plac...  26 us
    ppermute x6, starting transfers between devices, per_device(): got_x = lax.ppermute(send_x, 'ctx', even_links)  17.4 us
    ppermute x3, waiting for transfers between devices, sum_steps(): steps.append(lambda value, group=group: value + group[0](value))  5.36 us
    ppermute x3, starting transfers between devices, per_device(): exchanged = [exchange(total) for exchange in exchanges]  4.39 us
    ppermute x5, starting transfers between devices, per_device(): got_y = lax.ppermute(send_y, 'ctx', odd_links)  3.42 us
    ppermute x3, starting transfers between devices, sum_steps(): steps.append(lambda value, group=group: value + group[0](value))  3.11 us
    ppermute x1, starting transfers between devices, per_device(): pieces = [lax.ppermute(own_state, 'ctx', swap), own_state]  3.09 us
  transfers between devices with their start and end apart: 19, of which 10 were waited for; matrix products, arithmetic and copies ran while one was open for 0% of the time, Pallas kernels for 21%

profile of v7, /device:TPU:0, one launch (start us, length us, event | category | flops | bytes accessed | tf_op | source)
XLA Modules:
  0.0 99.4 jit_solution(9478281799309521648)
XLA Ops:
  0.6 3.1 %collective-permute-start = (f32[4,128,128]{2,1,0:T(8,128)}, f32[4,128,128]{2,1,0:T(8,128)S(1)}, u32[]{:S(2)}, u32[]{:S(2)}) collective-permute-start(f32[4,128,128]{2,1,0:T(8,128)} %bitcast.31), channel_id=1, source_target_pairs={{0,8},{8,0},{16,24},{24,16},{1,9},{9,1},{17,25},{25,17},{2,10},{10... | collective-permute-start | bytes 786440 | tf_op jit(solution)/shard_map/ppermute | solution.py:530
  5.2 4.3 %shard_map.163 = (f32[288,512]{1,0:T(8,128)S(1)}, f32[288,512]{1,0:T(8,128)S(1)}, f32[2,4,8,512]{3,2,1,0:T(8,128)S(1)}, f32[4,128,128]{2,1,0:T(8,128)S(1)}, bf16...) custom-call(s32[65]{0:T(128)S(1)} %concatenate.3.meta.refs_0_, ...), custom_call_target="tpu_custom_call" | custom-call | tf_op jit(solution)/shard_map/pallas_call | solution.py:409
  11.1 1.9 %collective-permute-start.2 = (f32[288,512]{1,0:T(8,128)S(1)}, f32[288,512]{1,0:T(8,128)S(1)}, u32[]{:S(2)}, u32[]{:S(2)}) collective-permute-start(f32[288,512]{1,0:T(8,128)S(1)} %get-tuple-element.69), channel_id=1, source_target_pairs={{0,8},{8,0},{16,24},{24,16},{1,9},{9,1},{17,25},{25,17},{2,10},{10... | collective-permute-start | bytes 1769480 | tf_op jit(solution)/shard_map/ppermute | solution.py:648
  13.7 5.4 %shard_map.164 = (f32[2,4,2,128,512]{4,3,2,1,0:T(8,128)S(1)}, f32[128,2048]{1,0:T(8,128)S(1)}, f32[128,2048]{1,0:T(8,128)S(1)}, f32[128,128]{1,0:T(8,128)S(1)}, ...) custom-call(s32[65]{0:T(128)S(1)} %concatenate.3.meta.refs_0_, bf16[128,2048]{1,0:T(8,128)(2,1)S(1)} %get-tuple-element.55.hid, ...), custom_call_target="tpu_custom_call" | custom-call | tf_op jit(solution)/shard_map/pallas_call | solution.py:409
  19.8 5.9 %collective-permute-done.2.refs_1_ = f32[288,512]{1,0:T(8,128)S(1)} collective-permute-done((f32[288,512]{1,0:T(8,128)S(1)}, f32[288,512]{1,0:T(8,128)S(1)}, u32[]{:S(2)}, u32[]{:S(2)}) %collective-permute-start.2) | collective-permute-done | bytes 589856 | tf_op jit(solution)/shard_map/ppermute | solution.py:648
  27.0 3.8 %collective-permute-start.3 = (f32[288,512]{1,0:T(8,128)S(1)}, f32[288,512]{1,0:T(8,128)S(1)}, u32[]{:S(2)}, u32[]{:S(2)}) collective-permute-start(f32[288,512]{1,0:T(8,128)S(1)} %get-tuple-element.72), channel_id=1, source_target_pairs={{0,8},{8,0},{16,24},{24,16},{1,9},{9,1},{17,25},{25,17},{2,10},{10... | collective-permute-start | bytes 1769480 | tf_op jit(solution)/shard_map/ppermute | solution.py:648
  31.5 10.8 %collective-permute-done.3.refs_1_ = f32[288,512]{1,0:T(8,128)S(1)} collective-permute-done((f32[288,512]{1,0:T(8,128)S(1)}, f32[288,512]{1,0:T(8,128)S(1)}, u32[]{:S(2)}, u32[]{:S(2)}) %collective-permute-start.3) | collective-permute-done | bytes 589856 | tf_op jit(solution)/shard_map/ppermute | solution.py:648
  43.7 3.0 %collective-permute-start.6 = (f32[288,512]{1,0:T(8,128)S(1)}, f32[288,512]{1,0:T(8,128)S(1)}, u32[]{:S(2)}, u32[]{:S(2)}) collective-permute-start(f32[288,512]{1,0:T(8,128)S(1)} %get-tuple-element.79), channel_id=1, source_target_pairs={{0,8},{8,0},{16,24},{24,16},{1,9},{9,1},{17,25},{25,17},{2,10},{10... | collective-permute-start | bytes 1769480 | tf_op jit(solution)/shard_map/ppermute | solution.py:648
  47.4 1.6 %collective-permute-start.13 = (f32[5,128,512]{2,1,0:T(8,128)S(1)}, f32[5,128,512]{2,1,0:T(8,128)S(1)}, u32[]{:S(2)}, u32[]{:S(2)}) collective-permute-start(f32[5,128,512]{2,1,0:T(8,128)S(1)} %get-tuple-element.90.begin_here), channel_id=1, source_target_pairs={{0,4},{4,0},{1,5},{5,1},{2,6},{6,2},{3,7},{7,3},{8,12},{12,8},{9,1... | collective-permute-start | bytes 3932168 | tf_op jit(solution)/shard_map/ppermute | solution.py:657
  49.0 8.3 %collective-permute-done.6.refs_1_.from_x = f32[288,512]{1,0:T(8,128)S(1)} collective-permute-done((f32[288,512]{1,0:T(8,128)S(1)}, f32[288,512]{1,0:T(8,128)S(1)}, u32[]{:S(2)}, u32[]{:S(2)}) %collective-permute-start.6) | collective-permute-done | bytes 589856 | tf_op jit(solution)/shard_map/ppermute | solution.py:648
  58.6 3.1 %collective-permute-start.7 = (f32[256,512]{1,0:T(8,128)S(1)}, f32[256,512]{1,0:T(8,128)S(1)}, u32[]{:S(2)}, u32[]{:S(2)}) collective-permute-start(f32[256,512]{1,0:T(8,128)S(1)} %get-tuple-element.82), channel_id=1, source_target_pairs={{0,8},{8,0},{16,24},{24,16},{1,9},{9,1},{17,25},{25,17},{2,10},{10... | collective-permute-start | bytes 1572872 | tf_op jit(solution)/shard_map/ppermute | solution.py:648
  62.4 1.5 %shard_map.173.refs_5_ = f32[8,128]{1,0:T(8,128)S(1)} custom-call(s32[65]{0:T(128)S(1)} %concatenate.3.meta.refs_0_, f32[288,512]{1,0:T(8,128)S(1)} %collective-permute-done.6.refs_1_.from_x, f32[288,512]{1,0:T(8,128)S(1)} %collective-permute-done.4.refs_1_.from_y, f32[2,4,8,512]{3,2,1,0:T(8,128)S(1)} %get-tuple-element.68.refs_3_.small, ...), custom_call_target="tpu_custom_call" | custom-call | tf_op jit(solution)/shard_map/pallas_call | solution.py:409
  63.9 1.2 %collective-permute-done.10 = f32[8,128]{1,0:T(8,128)S(1)} collective-permute-done((f32[8,128]{1,0:T(8,128)S(1)}, f32[8,128]{1,0:T(8,128)S(1)}, u32[]{:S(2)}, u32[]{:S(2)}) %collective-permute-start.10) | collective-permute-done | bytes 4128 | tf_op jit(solution)/shard_map/ppermute | solution.py:455
  65.0 4.9 %collective-permute-done.7.refs_1_ = f32[256,512]{1,0:T(8,128)S(1)} collective-permute-done((f32[256,512]{1,0:T(8,128)S(1)}, f32[256,512]{1,0:T(8,128)S(1)}, u32[]{:S(2)}, u32[]{:S(2)}) %collective-permute-start.7) | collective-permute-done | bytes 524320 | tf_op jit(solution)/shard_map/ppermute | solution.py:648
  71.3 3.1 %collective-permute-start.11 = (f32[256,512]{1,0:T(8,128)S(1)}, f32[256,512]{1,0:T(8,128)S(1)}, u32[]{:S(2)}, u32[]{:S(2)}) collective-permute-start(f32[256,512]{1,0:T(8,128)S(1)} %get-tuple-element.88), channel_id=1, source_target_pairs={{0,8},{8,0},{16,24},{24,16},{1,9},{9,1},{17,25},{25,17},{2,10},{10... | collective-permute-start | bytes 1572872 | tf_op jit(solution)/shard_map/ppermute | solution.py:648
  75.0 1.6 %collective-permute-start.12 = (f32[8,128]{1,0:T(8,128)S(1)}, f32[8,128]{1,0:T(8,128)S(1)}, u32[]{:S(2)}, u32[]{:S(2)}) collective-permute-start(f32[8,128]{1,0:T(8,128)S(1)} %add.42.refs_5_), channel_id=1, source_target_pairs={{0,2},{1,3},{2,0},{3,1},{4,6},{5,7},{6,4},{7,5},{8,10},{9,11},{10,... | collective-permute-start | bytes 12296 | tf_op jit(solution)/shard_map/ppermute | solution.py:455
  76.6 2.1 %collective-permute-done.12 = f32[8,128]{1,0:T(8,128)S(1)} collective-permute-done((f32[8,128]{1,0:T(8,128)S(1)}, f32[8,128]{1,0:T(8,128)S(1)}, u32[]{:S(2)}, u32[]{:S(2)}) %collective-permute-start.12) | collective-permute-done | bytes 4128 | tf_op jit(solution)/shard_map/ppermute | solution.py:455
  78.7 1.5 %collective-permute-start.14 = (f32[8,128]{1,0:T(8,128)S(1)}, f32[8,128]{1,0:T(8,128)S(1)}, u32[]{:S(2)}, u32[]{:S(2)}) collective-permute-start(f32[8,128]{1,0:T(8,128)S(1)} %add.43.refs_5_), channel_id=1, source_target_pairs={{0,4},{4,0},{1,5},{5,1},{2,6},{6,2},{3,7},{7,3},{8,12},{12,8},{9,1... | collective-permute-start | bytes 12296 | tf_op jit(solution)/shard_map/ppermute | solution.py:455
  80.2 2.1 %collective-permute-done.14 = f32[8,128]{1,0:T(8,128)S(1)} collective-permute-done((f32[8,128]{1,0:T(8,128)S(1)}, f32[8,128]{1,0:T(8,128)S(1)}, u32[]{:S(2)}, u32[]{:S(2)}) %collective-permute-start.14) | collective-permute-done | bytes 4128 | tf_op jit(solution)/shard_map/ppermute | solution.py:455
  83.6 2.6 %collective-permute-start.15 = (f32[256,512]{1,0:T(8,128)S(1)}, f32[256,512]{1,0:T(8,128)S(1)}, u32[]{:S(2)}, u32[]{:S(2)}) collective-permute-start(f32[256,512]{1,0:T(8,128)S(1)} %get-tuple-element.94), channel_id=1, source_target_pairs={{0,8},{8,0},{16,24},{24,16},{1,9},{9,1},{17,25},{25,17},{2,10},{10... | collective-permute-start | bytes 1572872 | tf_op jit(solution)/shard_map/ppermute | solution.py:648
  86.1 4.3 %shard_map.178 = (bf16[128,2048]{1,0:T(8,128)(2,1)}, bf16[128,2048]{1,0:T(8,128)(2,1)}, f32[128,128]{1,0:T(8,128)S(1)}, f32[128,128]{1,0:T(8,128)S(1)}, f32[8,128]{1,0:T(8,128)S(1)}) custom-call(s32[65]{0:T(128)S(1)} %concatenate.3.meta.refs_0_, f32[16]{0:T(128)S(1)} %copy-done, ...), custom_call_target="tpu_custom_call", output_to_operand_aliasing={{4}: (17, {})} | custom-call | tf_op jit(solution)/shard_map/pallas_call | solution.py:409
  90.5 1.8 %collective-permute-start.18 = (f32[8,128]{1,0:T(8,128)S(1)}, f32[8,128]{1,0:T(8,128)S(1)}, u32[]{:S(2)}, u32[]{:S(2)}) collective-permute-start(f32[8,128]{1,0:T(8,128)S(1)} %get-tuple-element.97.refs_2_), channel_id=1, source_target_pairs={{0,24},{8,16},{16,8},{24,0},{1,25},{9,17},{17,9},{25,1},{2,26},{10... | collective-permute-start | bytes 12296 | tf_op jit(solution)/shard_map/ppermute | solution.py:730
  92.3 2.6 %collective-permute-start.16 = (f32[8,128]{1,0:T(8,128)S(1)}, f32[8,128]{1,0:T(8,128)S(1)}, u32[]{:S(2)}, u32[]{:S(2)}) collective-permute-start(f32[8,128]{1,0:T(8,128)S(1)} %get-tuple-element.97.refs_2_), channel_id=1, source_target_pairs={{0,8},{8,0},{16,24},{24,16},{1,9},{9,1},{17,25},{25,17},{2,10},{10... | collective-permute-start | bytes 12296 | tf_op jit(solution)/shard_map/ppermute | solution.py:730
  96.8 2.7 %shard_map.179 = (bf16[128,2048]{1,0:T(8,128)(2,1)}, bf16[128,2048]{1,0:T(8,128)(2,1)}, bf16[128,128]{1,0:T(8,128)(2,1)}, bf16[128,128]{1,0:T(8,128)(2,1)}, f32[4,128]{1,0:T(4,128)}, /*index=5*/f32[1,16]{1,0:T(1,128)}) custom-call(s32[65]{0:T(128)S(1)} %concatenate.3.meta.refs_0_, f32[16]{0:T(128)S(1)} %copy-done, ...), custom_call_target="tpu_custom_call", output_to_operand_aliasing={{0}: (18, {}), {1}: (19, {})} | custom-call | tf_op jit(solution)/shard_map/pallas_call | solution.py:409
  (42 shorter events, 14.2 us)
Async XLA Ops:
  0.6 9.6 %collective-permute-start = (f32[4,128,128]{2,1,0:T(8,128)}, f32[4,128,128]{2,1,0:T(8,128)S(1)}, u32[]{:S(2)}, u32[]{:S(2)}) collective-permute-start(f32[4,128,128]{2,1,0:T(8,128)} %bitcast.31), channel_id=1, source_target_pairs={{0,8},{8,0},{16,24},{24,16},{1,9},{9,1},{17,25},{25,17},{2,10},{10... | collective-permute-start | bytes 786440 | tf_op jit(solution)/shard_map/ppermute | solution.py:530
  11.1 14.6 %collective-permute-start.2 = (f32[288,512]{1,0:T(8,128)S(1)}, f32[288,512]{1,0:T(8,128)S(1)}, u32[]{:S(2)}, u32[]{:S(2)}) collective-permute-start(f32[288,512]{1,0:T(8,128)S(1)} %get-tuple-element.69), channel_id=1, source_target_pairs={{0,8},{8,0},{16,24},{24,16},{1,9},{9,1},{17,25},{25,17},{2,10},{10... | collective-permute-start | bytes 1769480 | tf_op jit(solution)/shard_map/ppermute | solution.py:648
  13.0 13.4 %collective-permute-start.1 = (f32[288,512]{1,0:T(8,128)S(1)}, f32[288,512]{1,0:T(8,128)S(1)}, u32[]{:S(2)}, u32[]{:S(2)}) collective-permute-start(f32[288,512]{1,0:T(8,128)S(1)} %get-tuple-element.66), channel_id=1, source_target_pairs={{8,16},{16,8},{9,17},{17,9},{10,18},{18,10},{11,19},{19,11},{12,20... | collective-permute-start | bytes 1769480 | tf_op jit(solution)/shard_map/ppermute | solution.py:650
  27.0 15.4 %collective-permute-start.3 = (f32[288,512]{1,0:T(8,128)S(1)}, f32[288,512]{1,0:T(8,128)S(1)}, u32[]{:S(2)}, u32[]{:S(2)}) collective-permute-start(f32[288,512]{1,0:T(8,128)S(1)} %get-tuple-element.72), channel_id=1, source_target_pairs={{0,8},{8,0},{16,24},{24,16},{1,9},{9,1},{17,25},{25,17},{2,10},{10... | collective-permute-start | bytes 1769480 | tf_op jit(solution)/shard_map/ppermute | solution.py:648
  30.8 12.2 %collective-permute-start.5 = (f32[288,512]{1,0:T(8,128)S(1)}, f32[288,512]{1,0:T(8,128)S(1)}, u32[]{:S(2)}, u32[]{:S(2)}) collective-permute-start(f32[288,512]{1,0:T(8,128)S(1)} %get-tuple-element.76), channel_id=1, source_target_pairs={{8,16},{16,8},{9,17},{17,9},{10,18},{18,10},{11,19},{19,11},{12,20... | collective-permute-start | bytes 1769480 | tf_op jit(solution)/shard_map/ppermute | solution.py:650
  43.7 13.7 %collective-permute-start.6 = (f32[288,512]{1,0:T(8,128)S(1)}, f32[288,512]{1,0:T(8,128)S(1)}, u32[]{:S(2)}, u32[]{:S(2)}) collective-permute-start(f32[288,512]{1,0:T(8,128)S(1)} %get-tuple-element.79), channel_id=1, source_target_pairs={{0,8},{8,0},{16,24},{24,16},{1,9},{9,1},{17,25},{25,17},{2,10},{10... | collective-permute-start | bytes 1769480 | tf_op jit(solution)/shard_map/ppermute | solution.py:648
  46.7 11.3 %collective-permute-start.4 = (f32[288,512]{1,0:T(8,128)S(1)}, f32[288,512]{1,0:T(8,128)S(1)}, u32[]{:S(2)}, u32[]{:S(2)}) collective-permute-start(f32[288,512]{1,0:T(8,128)S(1)} %get-tuple-element.75), channel_id=1, source_target_pairs={{8,16},{16,8},{9,17},{17,9},{10,18},{18,10},{11,19},{19,11},{12,20... | collective-permute-start | bytes 1769480 | tf_op jit(solution)/shard_map/ppermute | solution.py:650
  47.4 35.5 %collective-permute-start.13 = (f32[5,128,512]{2,1,0:T(8,128)S(1)}, f32[5,128,512]{2,1,0:T(8,128)S(1)}, u32[]{:S(2)}, u32[]{:S(2)}) collective-permute-start(f32[5,128,512]{2,1,0:T(8,128)S(1)} %get-tuple-element.90.begin_here), channel_id=1, source_target_pairs={{0,4},{4,0},{1,5},{5,1},{2,6},{6,2},{3,7},{7,3},{8,12},{12,8},{9,1... | collective-permute-start | bytes 3932168 | tf_op jit(solution)/shard_map/ppermute | solution.py:657
  58.6 11.4 %collective-permute-start.7 = (f32[256,512]{1,0:T(8,128)S(1)}, f32[256,512]{1,0:T(8,128)S(1)}, u32[]{:S(2)}, u32[]{:S(2)}) collective-permute-start(f32[256,512]{1,0:T(8,128)S(1)} %get-tuple-element.82), channel_id=1, source_target_pairs={{0,8},{8,0},{16,24},{24,16},{1,9},{9,1},{17,25},{25,17},{2,10},{10... | collective-permute-start | bytes 1572872 | tf_op jit(solution)/shard_map/ppermute | solution.py:648
  61.7 8.9 %collective-permute-start.9 = (f32[256,512]{1,0:T(8,128)S(1)}, f32[256,512]{1,0:T(8,128)S(1)}, u32[]{:S(2)}, u32[]{:S(2)}) collective-permute-start(f32[256,512]{1,0:T(8,128)S(1)} %get-tuple-element.86), channel_id=1, source_target_pairs={{8,16},{16,8},{9,17},{17,9},{10,18},{18,10},{11,19},{19,11},{12,20... | collective-permute-start | bytes 1572872 | tf_op jit(solution)/shard_map/ppermute | solution.py:650
  63.8 1.2 %collective-permute-start.10 = (f32[8,128]{1,0:T(8,128)S(1)}, f32[8,128]{1,0:T(8,128)S(1)}, u32[]{:S(2)}, u32[]{:S(2)}) collective-permute-start(f32[8,128]{1,0:T(8,128)S(1)} %shard_map.173.refs_5_), channel_id=1, source_target_pairs={{0,1},{1,0},{2,3},{3,2},{4,5},{5,4},{6,7},{7,6},{8,9},{9,8},{10,11... | collective-permute-start | bytes 12296 | tf_op jit(solution)/shard_map/ppermute | solution.py:455
  71.3 11.0 %collective-permute-start.11 = (f32[256,512]{1,0:T(8,128)S(1)}, f32[256,512]{1,0:T(8,128)S(1)}, u32[]{:S(2)}, u32[]{:S(2)}) collective-permute-start(f32[256,512]{1,0:T(8,128)S(1)} %get-tuple-element.88), channel_id=1, source_target_pairs={{0,8},{8,0},{16,24},{24,16},{1,9},{9,1},{17,25},{25,17},{2,10},{10... | collective-permute-start | bytes 1572872 | tf_op jit(solution)/shard_map/ppermute | solution.py:648
  74.3 8.6 %collective-permute-start.8 = (f32[256,512]{1,0:T(8,128)S(1)}, f32[256,512]{1,0:T(8,128)S(1)}, u32[]{:S(2)}, u32[]{:S(2)}) collective-permute-start(f32[256,512]{1,0:T(8,128)S(1)} %get-tuple-element.85), channel_id=1, source_target_pairs={{8,16},{16,8},{9,17},{17,9},{10,18},{18,10},{11,19},{19,11},{12,20... | collective-permute-start | bytes 1572872 | tf_op jit(solution)/shard_map/ppermute | solution.py:650
  75.0 3.7 %collective-permute-start.12 = (f32[8,128]{1,0:T(8,128)S(1)}, f32[8,128]{1,0:T(8,128)S(1)}, u32[]{:S(2)}, u32[]{:S(2)}) collective-permute-start(f32[8,128]{1,0:T(8,128)S(1)} %add.42.refs_5_), channel_id=1, source_target_pairs={{0,2},{1,3},{2,0},{3,1},{4,6},{5,7},{6,4},{7,5},{8,10},{9,11},{10,... | collective-permute-start | bytes 12296 | tf_op jit(solution)/shard_map/ppermute | solution.py:455
  78.7 3.6 %collective-permute-start.14 = (f32[8,128]{1,0:T(8,128)S(1)}, f32[8,128]{1,0:T(8,128)S(1)}, u32[]{:S(2)}, u32[]{:S(2)}) collective-permute-start(f32[8,128]{1,0:T(8,128)S(1)} %add.43.refs_5_), channel_id=1, source_target_pairs={{0,4},{4,0},{1,5},{5,1},{2,6},{6,2},{3,7},{7,3},{8,12},{12,8},{9,1... | collective-permute-start | bytes 12296 | tf_op jit(solution)/shard_map/ppermute | solution.py:455
  82.9 3.2 %copy-start = (f32[16]{0:T(128)S(1)}, f32[16]{0:T(128)}, u32[]{:S(2)}) copy-start(f32[16]{0:T(128)} %gains.3) | copy-start | bytes 196
  83.6 13.2 %collective-permute-start.15 = (f32[256,512]{1,0:T(8,128)S(1)}, f32[256,512]{1,0:T(8,128)S(1)}, u32[]{:S(2)}, u32[]{:S(2)}) collective-permute-start(f32[256,512]{1,0:T(8,128)S(1)} %get-tuple-element.94), channel_id=1, source_target_pairs={{0,8},{8,0},{16,24},{24,16},{1,9},{9,1},{17,25},{25,17},{2,10},{10... | collective-permute-start | bytes 1572872 | tf_op jit(solution)/shard_map/ppermute | solution.py:648
  90.5 5.4 %collective-permute-start.18 = (f32[8,128]{1,0:T(8,128)S(1)}, f32[8,128]{1,0:T(8,128)S(1)}, u32[]{:S(2)}, u32[]{:S(2)}) collective-permute-start(f32[8,128]{1,0:T(8,128)S(1)} %get-tuple-element.97.refs_2_), channel_id=1, source_target_pairs={{0,24},{8,16},{16,8},{24,0},{1,25},{9,17},{17,9},{25,1},{2,26},{10... | collective-permute-start | bytes 12296 | tf_op jit(solution)/shard_map/ppermute | solution.py:730
  92.3 4.5 %collective-permute-start.17 = (f32[8,128]{1,0:T(8,128)S(1)}, f32[8,128]{1,0:T(8,128)S(1)}, u32[]{:S(2)}, u32[]{:S(2)}) collective-permute-start(f32[8,128]{1,0:T(8,128)S(1)} %get-tuple-element.97.refs_2_), channel_id=1, source_target_pairs={{0,16},{8,24},{16,0},{24,8},{1,17},{9,25},{17,1},{25,9},{2,18},{10... | collective-permute-start | bytes 12296 | tf_op jit(solution)/shard_map/ppermute | solution.py:730
  92.3 4.5 %collective-permute-start.16 = (f32[8,128]{1,0:T(8,128)S(1)}, f32[8,128]{1,0:T(8,128)S(1)}, u32[]{:S(2)}, u32[]{:S(2)}) collective-permute-start(f32[8,128]{1,0:T(8,128)S(1)} %get-tuple-element.97.refs_2_), channel_id=1, source_target_pairs={{0,8},{8,0},{16,24},{24,16},{1,9},{9,1},{17,25},{25,17},{2,10},{10... | collective-permute-start | bytes 12296 | tf_op jit(solution)/shard_map/ppermute | solution.py:730
